TPU v7x, 32 devices: a whole 2x2x4 slice. The times are simulated.
32 devices in a mesh: lev: 4 (over y, x), lat: 8 (over z, core).
Axes of the slice: x: 2, y: 2, z: 4, core: 2. Of those that a mesh axis runs over, the one named last changes fastest.
Arguments:
- zonal_velocity: bfloat16 [8, 1280, 2560], P(None, 'lat', 'lev'), may hold values from -6 to 6
- meridional_velocity: bfloat16 [8, 1280, 2560], P(None, 'lat', 'lev'), may hold values from -6 to 6
- air_warmth: bfloat16 [8, 1280, 2560], P(None, 'lat', 'lev'), may hold values from -6 to 6
- pressure_integration_operator: bfloat16 [8, 8], replicated, may hold values from -2 to 2
- quadrature_factors_north: float32 [640], replicated, may hold values from 0.3 to 1.7
- associated_polynomial_table: bfloat16 [320, 641, 640], P('lat'), may hold values from -0.15625 to 0.15625
- position_wavenumber_couples: int32 [320], replicated, may hold values from 0 to 319, each once
- layer_projection_operator: bfloat16 [8, 8], replicated, may hold values from -2 to 2
- eigen_reconstruction_operator: bfloat16 [8, 8], replicated, may hold values from -2 to 2
- eigen_backward_factors: float32 [8], replicated, may hold values from 0.1 to 10
Outputs:
- tendency_fourier: float32 [2, 8, 320, 2, 2, 1280], P(None, 'lev', 'lat')
Inputs may be any that keep to these rules, and one draw needn't show every extreme that they name: `position_wavenumber_couples`: every slot number from 0 to 319 names a different pair.
All inputs are finite; a program needn't handle non-finite values.
Results may differ from a plain program's by a relative error of at most 0.0072.
Values may be sent and summed in bfloat16 or wider, within the bound.
No kernel may reach another device: no remote copies, remote signals or barrier semaphores. Data moves between devices by JAX's collectives and lax.ppermute only.
A program may use at most 128 MiB of HBM per device.

v0:
```python
import math

import jax
import jax.numpy as jnp
from jax import lax
from jax.sharding import PartitionSpec as P


def fourier_table(position_wavenumber_couples, lon_count, wave_count):
    repeated = jnp.repeat(position_wavenumber_couples, 4)
    column = jnp.arange(repeated.shape[0], dtype=jnp.int32)
    wavenumber = jnp.where(column // 2 % 2 == 0, repeated, wave_count - 1 - repeated)
    longitude = jnp.arange(lon_count, dtype=jnp.int32)
    phase_index = longitude[:, None] * wavenumber[None, :] % lon_count
    radians = phase_index.astype(jnp.float32) * (2.0 * math.pi / lon_count)
    values = jnp.where(column % 2 == 0, jnp.cos(radians), -jnp.sin(radians)) / math.sqrt(lon_count)
    return values.astype(jnp.bfloat16)


def row_layout(low_waves, wave_count, row_index):
    row_grid = row_index[None, :]
    low_grid = low_waves[:, None]
    boundary = wave_count - low_grid
    second_part = row_grid >= boundary
    parity = jnp.where(second_part, row_grid - boundary, row_grid) % 2
    degree = jnp.where(second_part, row_grid - 1, low_grid + row_grid)
    return (second_part, parity, degree)


def row_selector(second_part, parity):
    choices_two = jnp.arange(2, dtype=jnp.int32)
    parity_hit = parity[..., None] == choices_two
    part_hit = second_part.astype(jnp.int32)[..., None] == choices_two
    return parity_hit[..., :, None] & part_hit[..., None, :]


def damping(degree, eigen_backward_factors, wave_count):
    total = degree.astype(jnp.float32)
    factor = total * (total + 1.0) / float(wave_count * wave_count)
    return 1.0 / (1.0 + factor[:, :, None] * eigen_backward_factors[None, None, :])


def forward_legendre(
    by_wave, associated_polynomial_table, quadrature_factors_north, own_pairs, wave_count
):
    field_count, layer_tally, lat_count, column_count = by_wave.shape
    half_rows = lat_count // 2
    slot_count = column_count // 4
    northern = by_wave[:, :, :half_rows].astype(jnp.float32)
    southern = by_wave[:, :, half_rows:][:, :, ::-1].astype(jnp.float32)
    folded = (
        jnp.stack([northern + southern, northern - southern]) * quadrature_factors_north[:, None]
    )
    folded = folded.astype(jnp.bfloat16).reshape(
        2, field_count, layer_tally, half_rows, slot_count, 2, 2
    )
    folded = jnp.transpose(folded, (4, 3, 0, 5, 6, 1, 2)).reshape(slot_count, half_rows, -1)
    product = jnp.einsum(
        "srl,slc->src", associated_polynomial_table, folded, preferred_element_type=jnp.float32
    )
    product = product.reshape(slot_count, wave_count + 1, 2, 2, 2, field_count, layer_tally)
    layout = row_layout(own_pairs, wave_count, jnp.arange(wave_count + 1, dtype=jnp.int32))
    chosen = row_selector(layout[0], layout[1])
    return jnp.sum(jnp.where(chosen[..., None, None, None], product, 0.0), axis=(2, 3)).astype(
        jnp.bfloat16
    )


def inverse_legendre(implicit, associated_polynomial_table, own_pairs, wave_count):
    slot_count = implicit.shape[0]
    row_total = implicit.shape[1]
    field_count = implicit.shape[3]
    layer_tally = implicit.shape[4]
    layout = row_layout(own_pairs, wave_count, jnp.arange(row_total, dtype=jnp.int32))
    chosen = row_selector(layout[0], layout[1])
    spread = jnp.where(
        chosen[..., None, None, None], implicit[:, :, None, None], jnp.zeros((), implicit.dtype)
    )
    spread = spread.reshape(slot_count, row_total, -1)
    summed = jnp.einsum(
        "srl,src->slc", associated_polynomial_table, spread, preferred_element_type=jnp.float32
    )
    summed = summed.reshape(
        slot_count, associated_polynomial_table.shape[2], 2, 2, 2, field_count, layer_tally
    )
    northern = summed[:, :, 0] + summed[:, :, 1]
    southern = (summed[:, :, 0] - summed[:, :, 1])[:, ::-1]
    latitudes = jnp.concatenate([northern, southern], axis=1)
    return jnp.transpose(latitudes, (4, 5, 0, 2, 3, 1))


def local(
    zonal_velocity,
    meridional_velocity,
    air_warmth,
    pressure_integration_operator,
    quadrature_factors_north,
    associated_polynomial_table,
    position_wavenumber_couples,
    layer_projection_operator,
    eigen_reconstruction_operator,
    eigen_backward_factors,
):
    layer_tally = air_warmth.shape[0]
    gravity_potential_surface = jnp.dot(
        pressure_integration_operator,
        air_warmth.reshape(layer_tally, -1),
        preferred_element_type=jnp.float32,
    )
    gravity_potential_surface = gravity_potential_surface.reshape(air_warmth.shape)
    eastward = zonal_velocity.astype(jnp.float32)
    northward = meridional_velocity.astype(jnp.float32)
    warmth_spectrum_field = air_warmth.astype(jnp.float32)
    products = jnp.stack(
        [
            eastward * northward + gravity_potential_surface,
            (eastward + northward) * warmth_spectrum_field,
        ]
    ).astype(jnp.bfloat16)
    by_level = lax.all_to_all(products, "lev", split_axis=1, concat_axis=3, tiled=True)
    field_count = by_level.shape[0]
    own_levels = by_level.shape[1]
    band_rows = by_level.shape[2]
    lon_count = by_level.shape[3]
    slot_count = associated_polynomial_table.shape[0]
    wave_count = associated_polynomial_table.shape[1] - 1
    row_total = wave_count + 1
    transform = fourier_table(position_wavenumber_couples, lon_count, wave_count)
    harmonic_coefficients_field = jnp.dot(
        by_level.reshape(-1, lon_count), transform, preferred_element_type=jnp.float32
    )
    harmonic_coefficients_field = harmonic_coefficients_field.astype(jnp.bfloat16).reshape(
        field_count, own_levels, band_rows, -1
    )
    by_wave = lax.all_to_all(
        harmonic_coefficients_field, "lat", split_axis=3, concat_axis=2, tiled=True
    )
    own_pairs = lax.dynamic_slice_in_dim(
        position_wavenumber_couples, lax.axis_index("lat") * slot_count, slot_count
    )
    spectral = forward_legendre(
        by_wave, associated_polynomial_table, quadrature_factors_north, own_pairs, wave_count
    )
    group_size = lax.axis_size("lev")
    padded_rows = -(-row_total // group_size) * group_size
    block_rows = padded_rows // group_size
    padded = jnp.pad(spectral, ((0, 0), (0, padded_rows - row_total), (0, 0), (0, 0), (0, 0)))
    received = lax.all_to_all(padded, "lev", split_axis=1, concat_axis=4, tiled=True)
    row_index = lax.axis_index("lev") * block_rows + jnp.arange(block_rows, dtype=jnp.int32)
    degree = row_layout(own_pairs, wave_count, row_index)[2]
    level_total = received.shape[4]
    flat_rows = received.reshape(-1, level_total)
    mode_values = jnp.dot(
        flat_rows, layer_projection_operator.T, preferred_element_type=jnp.float32
    ).reshape(received.shape)
    damped = (
        mode_values * damping(degree, eigen_backward_factors, wave_count)[:, :, None, None, :]
    ).astype(jnp.bfloat16)
    result = jnp.dot(
        damped.reshape(-1, level_total),
        eigen_reconstruction_operator.T,
        preferred_element_type=jnp.float32,
    )
    result = result.reshape(received.shape).astype(jnp.bfloat16)
    implicit = lax.all_to_all(result, "lev", split_axis=4, concat_axis=1, tiled=True)[:, :row_total]
    return inverse_legendre(implicit, associated_polynomial_table, own_pairs, wave_count)


def solution(mesh):
    placed = (
        P(None, "lat", "lev"),
        P(None, "lat", "lev"),
        P(None, "lat", "lev"),
        P(),
        P(),
        P("lat", None, None),
        P(),
        P(),
        P(),
        P(),
    )
    return jax.shard_map(
        local,
        mesh=mesh,
        in_specs=placed,
        out_specs=P(None, "lev", "lat", None, None, None),
        check_vma=False,
    )
```

profile of v0, /device:TPU:0, one launch (start us, length us, event | category | flops | bytes accessed | tf_op | source)
XLA Modules:
  0.0 354.7 jit_solution(3300230274046121506)
XLA Ops:
  0.0 4.0 %fusion.28 = bf16[1,8,160,640]{3,1,2,0:T(8,128)(2,1)S(1)} fusion(bf16[8,160,640]{2,1,0:T(8,128)(2,1)} %param.12, bf16[8,160,640]{2,1,0:T(8,128)(2,1)} %param.11, bf16[8,160,640]{2,1,0:T(8,128)(2,1)} %param.10), kind=kLoop, calls=%fused_computation.37 | loop fusion | flops 4915200 | bytes 6553600 | tf_op jit(solution)/shard_map/stack | solution.py:114
  8.0 5.3 %all-to-all-start = ((bf16[2,8,160,640]{3,2,0,1:T(8,128)(2,1)}), bf16[2,8,160,640]{3,2,0,1:T(8,128)(2,1)S(1)}, u32[]{:S(2)}, u32[]{:S(2)}) async-start(bf16[2,8,160,640]{3,2,0,1:T(8,128)(2,1)} %copy.46), calls=%async_computation | async-start | bytes 6553600 | tf_op jit(solution)/shard_map/all_to_all | solution.py:120
  13.6 37.2 %all-to-all-done = bf16[2,8,160,640]{3,2,0,1:T(8,128)(2,1)S(1)} async-done(((bf16[2,8,160,640]{3,2,0,1:T(8,128)(2,1)}), bf16[2,8,160,640]{3,2,0,1:T(8,128)(2,1)S(1)}, u32[]{:S(2)}, u32[]{:S(2)}) %all-to-all-start) | async-done | bytes 3276832 | tf_op jit(solution)/shard_map/all_to_all | solution.py:120
  53.9 58.6 %fusion.21 = bf16[640,1280]{1,0:T(8,128)(2,1)S(1)} fusion(bf16[640,2560]{1,0:T(8,128)(2,1)S(1)} %bitcast.92, s32[1280]{0:T(1024)S(1)} %subtract_select_fusion, pred[1280]{0:T(1024)(128)(4,1)S(1)} %fusion.38), kind=kOutput, calls=%fused_computation.31 | convolution fusion | flops 4237721600 | bytes 4921600 | tf_op jit(solution)/shard_map/dot_general | solution.py:129
  112.6 4.8 %copy.48 = bf16[2,2,160,1280]{2,1,0,3:T(2,128)(2,1)} copy(bf16[2,2,160,1280]{3,2,1,0:T(8,128)(2,1)S(1)} %bitcast.98) | data formatting | bytes 3276800 | tf_op jit(solution)/shard_map/reshape | solution.py:132
  117.3 5.7 %all-to-all-start.1 = ((bf16[2,2,160,1280]{2,1,0,3:T(2,128)(2,1)}), bf16[2,2,160,1280]{2,1,0,3:T(2,128)(2,1)S(1)}, u32[]{:S(2)}, u32[]{:S(2)}) async-start(bf16[2,2,160,1280]{2,1,0,3:T(2,128)(2,1)} %copy.48), calls=%async_computation.1 | async-start | bytes 5242880 | tf_op jit(solution)/shard_map/all_to_all | solution.py:135
  124.0 59.3 %all-to-all-done.1 = bf16[2,2,160,1280]{2,1,0,3:T(2,128)(2,1)S(1)} async-done(((bf16[2,2,160,1280]{2,1,0,3:T(2,128)(2,1)}), bf16[2,2,160,1280]{2,1,0,3:T(2,128)(2,1)S(1)}, u32[]{:S(2)}, u32[]{:S(2)}) %all-to-all-start.1) | async-done | bytes 1638432 | tf_op jit(solution)/shard_map/all_to_all | solution.py:135
  183.3 3.0 copy.99
  186.2 4.3 %all_to_all.54 = bf16[2,2,1280,160]{2,3,1,0:T(8,128)(2,1)S(1)} reshape(bf16[2,2,8,160,160]{3,2,4,1,0:T(8,128)(2,1)} %bitcast.89) | data formatting | bytes 3276800 | tf_op jit(solution)/shard_map/all_to_all | solution.py:135
  190.6 14.0 %rev.6 = bf16[2,2,640,160]{2,3,1,0:T(8,128)(2,1)} reverse(bf16[2,2,640,160]{2,3,1,0:T(8,128)(2,1)S(1)} %slice.23), dimensions={2} | reverse | bytes 1638400 | tf_op jit(solution)/shard_map/rev | solution.py:50
  211.6 3.4 fusion.29
  217.3 31.8 %fusion.22 = f32[40,641,32]{1,2,0:T(8,128)} fusion(bf16[40,640,32]{1,2,0:T(8,128)(2,1)S(1)} %reshape.251, bf16[40,641,640]{2,0,1:T(8,128)(2,1)} %param.15), kind=kOutput, calls=%fused_computation.33 | convolution fusion | flops 1050214400 | bytes 37739520 | tf_op jit(solution)/shard_map/srl,slc->src/dot_general | solution.py:58
  249.1 5.8 %reshape.252 = f32[40,641,2,2,2,2,2]{1,6,5,4,3,2,0:T(2,128)} reshape(f32[40,641,32]{1,2,0:T(8,128)} %fusion.22) | data formatting | bytes 6563840 | tf_op jit(solution)/shard_map/reshape | solution.py:61
  254.9 7.0 %select_reduce_fusion = bf16[40,641,2,2,2]{1,4,3,2,0:T(2,128)(2,1)S(1)} fusion(f32[40,641,2,2,2,2,2]{1,6,5,4,3,2,0:T(2,128)} %reshape.252, pred[40,641,2,2]{1,3,2,0:T(4,128)(4,1)S(1)} %broadcast_and_fusion), kind=kLoop, calls=%fused_computation.21 | loop fusion | flops 1435840 | bytes 3794720 | tf_op jit(solution)/shard_map/reduce_sum | solution.py:64
  265.0 2.6 reshape.257
  267.7 3.5 all-to-all-start.2
  271.4 6.6 %all-to-all-done.2 = bf16[4,2,25760]{2,1,0:T(2,128)(2,1)S(1)} async-done(((bf16[4,2,25760]{2,1,0:T(2,128)(2,1)}), bf16[4,2,25760]{2,1,0:T(2,128)(2,1)S(1)}, u32[]{:S(2)}, u32[]{:S(2)}) %all-to-all-start.2) | async-done | bytes 412192 | tf_op jit(solution)/shard_map/all_to_all | solution.py:148
  279.4 2.7 copy.67
  283.2 11.9 %all_to_all.66 = bf16[40,161,2,2,8]{1,3,2,0,4:T(2,128)(2,1)S(1)} all-to-all(bf16[40,161,2,2,8]{1,3,2,0,4:T(2,128)(2,1)S(1)} %copy.57), channel_id=1, replica_groups=mesh['lev'=4,'lat'=8] {'lev'}, dimensions={4} | all-to-all | bytes 824320 | tf_op jit(solution)/shard_map/all_to_all | solution.py:165
  300.8 30.9 %fusion.25 = f32[40,640,32]{1,2,0:T(8,128)S(1)} fusion(bf16[40,641,32]{1,2,0:T(8,128)(2,1)} %select_n.97, bf16[40,641,640]{2,0,1:T(8,128)(2,1)} %param.15), kind=kOutput, calls=%fused_computation.36 | convolution fusion | flops 1050214400 | bytes 37736960 | tf_op jit(solution)/shard_map/srl,src->slc/dot_general | solution.py:80
  331.7 3.3 reshape.253
  335.0 3.1 fusion.54
  339.8 10.1 %rev.7 = f32[40,640,2,2,2,2]{1,3,2,0,5,4:T(2,128)} reverse(f32[40,640,2,2,2,2]{1,3,2,0,5,4:T(2,128)S(1)} %get-tuple-element.8), dimensions={1} | reverse | bytes 3276800 | tf_op jit(solution)/shard_map/rev | solution.py:87
  349.9 4.6 %maximum_bitcast_fusion = f32[2,2,40,2,2,1280]{5,4,3,2,1,0:T(2,128)} fusion(f32[40,640,2,2,2,2]{1,3,2,0,5,4:T(2,128)} %rev.7, f32[40,640,2,2,2,2]{1,3,2,0,5,4:T(2,128)S(1)} %get-tuple-element.7), kind=kLoop, calls=%fused_computation.30 | loop fusion | flops 819200 | bytes 6553600 | tf_op jit(solution)/shard_map/transpose | solution.py:89
  (55 shorter events, 30.7 us)
Async XLA Ops:
  0.0 4.0 %copy-start = (bf16[8,8]{1,0:T(8,128)(2,1)S(1)}, bf16[8,8]{1,0:T(8,128)(2,1)}, u32[]{:S(2)}) copy-start(bf16[8,8]{1,0:T(8,128)(2,1)} %param.13) | copy-start | bytes 388
  0.0 4.0 %copy-start.4 = (bf16[8,160,640]{2,1,0:T(8,128)(2,1)S(1)}, bf16[8,160,640]{2,1,0:T(8,128)(2,1)}, u32[]{:S(2)}) copy-start(bf16[8,160,640]{2,1,0:T(8,128)(2,1)} %param.10) | copy-start | bytes 4915204
  0.0 4.0 %copy-start.3 = (bf16[8,160,640]{2,1,0:T(8,128)(2,1)S(1)}, bf16[8,160,640]{2,1,0:T(8,128)(2,1)}, u32[]{:S(2)}) copy-start(bf16[8,160,640]{2,1,0:T(8,128)(2,1)} %param.11) | copy-start | bytes 4915204
  0.0 4.0 %copy-start.2 = (bf16[8,160,640]{2,1,0:T(8,128)(2,1)S(1)}, bf16[8,160,640]{2,1,0:T(8,128)(2,1)}, u32[]{:S(2)}) copy-start(bf16[8,160,640]{2,1,0:T(8,128)(2,1)} %param.12) | copy-start | bytes 4915204
  8.0 5.3 %copy-start.6 = (s32[320]{0:T(512)S(1)}, s32[320]{0:T(512)}, u32[]{:S(2)}) copy-start(s32[320]{0:T(512)} %param.16) | copy-start | bytes 3844
  8.0 42.8 %all-to-all-start = ((bf16[2,8,160,640]{3,2,0,1:T(8,128)(2,1)}), bf16[2,8,160,640]{3,2,0,1:T(8,128)(2,1)S(1)}, u32[]{:S(2)}, u32[]{:S(2)}) async-start(bf16[2,8,160,640]{3,2,0,1:T(8,128)(2,1)} %copy.46), calls=%async_computation | async-start | bytes 6553600 | tf_op jit(solution)/shard_map/all_to_all | solution.py:120
  117.3 65.9 %all-to-all-start.1 = ((bf16[2,2,160,1280]{2,1,0,3:T(2,128)(2,1)}), bf16[2,2,160,1280]{2,1,0,3:T(2,128)(2,1)S(1)}, u32[]{:S(2)}, u32[]{:S(2)}) async-start(bf16[2,2,160,1280]{2,1,0,3:T(2,128)(2,1)} %copy.48), calls=%async_computation.1 | async-start | bytes 5242880 | tf_op jit(solution)/shard_map/all_to_all | solution.py:135
  209.4 2.2 copy-start.5
  263.6 7.6 %copy-start.9 = (f32[8]{0:T(128)S(1)}, f32[8]{0:T(128)}, u32[]{:S(2)}) copy-start(f32[8]{0:T(128)} %param.19) | copy-start | bytes 100
  267.7 10.3 %all-to-all-start.2 = ((bf16[4,2,25760]{2,1,0:T(2,128)(2,1)}), bf16[4,2,25760]{2,1,0:T(2,128)(2,1)S(1)}, u32[]{:S(2)}, u32[]{:S(2)}) async-start(bf16[4,2,25760]{2,1,0:T(2,128)(2,1)} %reshape.257), calls=%async_computation.2 | async-start | bytes 827392 | tf_op jit(solution)/shard_map/all_to_all | solution.py:148
  279.4 2.8 copy-start.7
  279.4 2.8 copy-start.8
  349.9 4.6 %copy-start.1 = (bf16[8,8]{1,0:T(8,128)(2,1)S(1)}, bf16[8,8]{1,0:T(8,128)(2,1)}, u32[]{:S(2)}) copy-start(bf16[8,8]{1,0:T(8,128)(2,1)} %param.13) | copy-start | bytes 388
where the time goes:
time: 361 us; the launch traced here: 355 us
  matrix products  123 us (34%)
  waiting for transfers between devices  103 us (29%)
  local copies, waits for them, and re-layouts  74.8 us (21%)
  other arithmetic  26.6 us (7%)
  starting transfers between devices  14.5 us (4%)
  blocking collectives  11.9 us (3%)
    all_to_all x1, waiting for transfers between devices, local(): lax.all_to_all(harmonic_coefficients_field, 'lat', split_axis=3, concat_a...  59.3 us
    dot_general x1, matrix products, local(): jnp.dot(by_level.reshape(-1, lon_count), transform, preferred_element_typ...  58.6 us
    all_to_all x1, waiting for transfers between devices, local(): lax.all_to_all(products, 'lev', split_axis=1, concat_axis=3, tiled=True)  37.2 us
    dot_general x1, matrix products, forward_legendre(): jnp.einsum('srl,slc->src', associated_polynomial_table, folded, preferred...  31.8 us
    dot_general x1, matrix products, inverse_legendre(): jnp.einsum('srl,src->slc', associated_polynomial_table, spread, preferred...  30.9 us
    rev x1, local copies, waits for them, and re-layouts, forward_legendre(): southern = by_wave[:, :, half_rows:][:, :, ::-1].astype(jnp.float32)  14 us
    all_to_all x1, blocking collectives, local(): lax.all_to_all(result, 'lev', split_axis=4, concat_axis=1, tiled=True)  11.9 us
    rev x1, local copies, waits for them, and re-layouts, inverse_legendre(): southern = (summed[:, :, 0] - summed[:, :, 1])[:, ::-1]  10.1 us
  transfers between devices with their start and end apart: 3, of which 3 were waited for; matrix products, arithmetic and copies ran while one was open for 0% of the time, Pallas kernels for 0%

commit v1 on v0

--- a/solution.py
+++ b/solution.py
@@ -3,7 +3,394 @@
 import jax
 import jax.numpy as jnp
 from jax import lax
+from jax.experimental import pallas as pl
+from jax.experimental.pallas import tpu as pltpu
 from jax.sharding import PartitionSpec as P
+
+BF = jnp.bfloat16
+F32 = jnp.float32
+LANE = 128
+GROUP = 8
+SUB = 32
+CHUNKS = ((0, 2), (2, 5))
+
+
+def products_call(u, v, t, operator, lev, first, count):
+    levels, band, lons = u.shape
+    own = levels // lev
+
+    def body(op, u_ref, v_ref, t_ref, out):
+        for tile in range(lons // LANE):
+            at = slice(tile * LANE, (tile + 1) * LANE)
+            warm = [t_ref[j, :, at].astype(F32) for j in range(levels)]
+            for k in range(levels):
+                height = op[k, 0] * warm[0]
+                for j in range(1, levels):
+                    height = height + op[k, j] * warm[j]
+                east = u_ref[k, :, at].astype(F32)
+                north = v_ref[k, :, at].astype(F32)
+                out[k // own, 0, k % own, :, at] = (east * north + height).astype(BF)
+                out[k // own, 0, own + k % own, :, at] = ((east + north) * warm[k]).astype(BF)
+
+    grid_in = pl.BlockSpec((levels, SUB, lons), lambda h: (0, first + h, 0))
+    return pl.pallas_call(
+        body,
+        name="products",
+        grid=(count,),
+        in_specs=[pl.BlockSpec(memory_space=pltpu.SMEM), grid_in, grid_in, grid_in],
+        out_specs=pl.BlockSpec((lev, 1, 2 * own, SUB, lons), lambda h: (0, h, 0, 0, 0)),
+        out_shape=jax.ShapeDtypeStruct((lev, count, 2 * own, SUB, lons), BF),
+    )(operator.astype(F32), u, v, t)
+
+
+def wave_rows_call(couples, lon_count, wave_count):
+    rows = 4 * couples.shape[0]
+    row = jnp.arange(rows, dtype=jnp.int32)
+    low = jnp.repeat(couples, 4)
+    wave = jnp.where(row // 2 % 2 == 0, low, wave_count - 1 - low)[:, None]
+    lane = jnp.arange(LANE, dtype=jnp.int32)[None, :]
+    unit = 2.0 * math.pi / lon_count
+    start = (wave * lane % lon_count).astype(F32) * unit
+    step = jnp.broadcast_to((wave * LANE % lon_count).astype(F32) * unit, (rows, LANE))
+    scale = 1.0 / math.sqrt(lon_count)
+    cosine, sine = jnp.cos(start) * scale, jnp.sin(start) * scale
+    is_sine = (row % 2 == 1)[:, None]
+    first = jnp.where(is_sine, -sine, cosine)
+    second = jnp.where(is_sine, cosine, sine)
+    block = GROUP * 4
+
+    def body(a_ref, b_ref, c_ref, s_ref, out):
+        a, b, c, s = a_ref[...], b_ref[...], c_ref[...], s_ref[...]
+        for tile in range(lon_count // LANE):
+            out[:, tile * LANE : (tile + 1) * LANE] = a.astype(BF)
+            a, b = a * c - b * s, b * c + a * s
+
+    spec = pl.BlockSpec((block, LANE), lambda i: (i, 0))
+    return pl.pallas_call(
+        body,
+        name="wave_rows",
+        grid=(rows // block,),
+        in_specs=[spec] * 4,
+        out_specs=pl.BlockSpec((block, lon_count), lambda i: (i, 0)),
+        out_shape=jax.ShapeDtypeStruct((rows, lon_count), BF),
+    )(first, second, jnp.cos(step), jnp.sin(step))
+
+
+def fourier_call(waves, pieces, steps=4):
+    parts, rows, lons = pieces.shape
+    columns = waves.shape[0]
+    block = columns // steps
+
+    def body(w_ref, x_ref, out):
+        total = None
+        for j in range(parts):
+            term = lax.dot_general(
+                w_ref[:, j * lons : (j + 1) * lons],
+                x_ref[j],
+                (((1,), (1,)), ((), ())),
+                preferred_element_type=F32,
+            )
+            total = term if total is None else total + term
+        out[...] = total.astype(BF)
+
+    return pl.pallas_call(
+        body,
+        name="fourier",
+        grid=(steps,),
+        in_specs=[
+            pl.BlockSpec((block, parts * lons), lambda i: (i, 0)),
+            pl.BlockSpec((parts, rows, lons), lambda i: (0, 0, 0)),
+        ],
+        out_specs=pl.BlockSpec((block, rows), lambda i: (i, 0)),
+        out_shape=jax.ShapeDtypeStruct((columns, rows), BF),
+    )(waves, pieces)
+
+
+def by_slot(index, pairs, group):
+    value = jnp.full(index.shape, pairs[group * GROUP], jnp.int32)
+    for s in range(1, GROUP):
+        value = jnp.where(index == s, pairs[group * GROUP + s], value)
+    return value
+
+
+def part_code(pairs, group, wave_count, half, par, lanes):
+    lane = lax.broadcasted_iota(jnp.int32, (1, lanes), 1)
+    slot = lane % GROUP
+    r = 2 * (lane // GROUP + half) + par
+    low = by_slot(slot, pairs, group)
+    return 2 * slot + (r >= wave_count - low).astype(jnp.int32)
+
+
+def forward_call(pairs, received, chunks, table, quadrature, lev):
+    row_total, slots, half_lat = table.shape
+    wave_count = row_total - 1
+    bands = received[0].shape[0]
+    units = chunks[-1][1]
+    groups = slots // GROUP
+    row_block = GROUP * 4
+    fields = LANE // SUB
+    rows = fields * row_block
+    per = wave_count // 2 * GROUP
+    piece = per * 2 // lev
+    where_unit = {}
+    for number, (lo, hi) in enumerate(chunks):
+        for unit in range(lo, hi):
+            where_unit[unit] = (number, unit - lo)
+
+    def body(pairs_ref, *refs):
+        recv = refs[: len(chunks)]
+        table_ref, quad_ref, out, spread = refs[len(chunks) :]
+        group = pl.program_id(0)
+        lane = lax.broadcasted_iota(jnp.int32, (row_block, LANE), 1)
+        within, place = lane % SUB, lane // SUB
+        row = lax.broadcasted_iota(jnp.int32, (row_block, LANE), 0)
+        low = by_slot(row // 4, pairs_ref, group)
+        second = row // 2 % 2
+        signs = [(1 - 2 * ((par + second * low) % 2)).astype(F32) for par in range(2)]
+
+        def tile(band, unit):
+            number, local = where_unit[unit]
+            return recv[number][band, :, local * LANE : (local + 1) * LANE].astype(F32)
+
+        for target in range(half_lat // LANE):
+            at = slice(target * LANE, (target + 1) * LANE)
+            north_tiles, south_tiles = [], []
+            for d in range(fields):
+                beta = fields * target + d
+                band, unit = beta // units, beta % units
+                north_tiles.append(tile(band, unit))
+                south_tiles.append(tile(bands - 1 - band, units - 1 - unit))
+            weight = quad_ref[0:1, at]
+            for f in range(fields):
+                north = jnp.zeros((row_block, LANE), F32)
+                south = jnp.zeros((row_block, LANE), F32)
+                for d in range(fields):
+                    moved = jnp.take_along_axis(north_tiles[d], f * SUB + within, axis=1)
+                    north = jnp.where(place == d, moved, north)
+                    moved = jnp.take_along_axis(south_tiles[d], f * SUB + SUB - 1 - within, axis=1)
+                    south = jnp.where(place == d, moved, south)
+                for par in range(2):
+                    folded = (north + signs[par] * south) * weight
+                    spread[par, f * row_block : (f + 1) * row_block, at] = folded.astype(BF)
+        to = lax.broadcasted_iota(jnp.int32, (rows, rows), 0)
+        source = lax.broadcasted_iota(jnp.int32, (rows, rows), 1)
+        wanted = to // 2 % fields * row_block + to // (2 * fields) * 2 + to % 2
+        order = (source == wanted).astype(BF)
+        whole = table_ref[0:wave_count].reshape(wave_count // 2, 2, GROUP, half_lat)
+        last = table_ref[wave_count]
+        out[...] = jnp.zeros(out.shape, BF)
+        for par in range(2):
+            field = jnp.dot(order, spread[par], preferred_element_type=F32).astype(BF)
+            matrix = whole[:, par].reshape(per, half_lat)
+            product = lax.dot_general(
+                field, matrix, (((1,), (1,)), ((), ())), preferred_element_type=F32
+            )
+            code = part_code(pairs_ref, group, wave_count, 0, par, per)
+            kept = jnp.zeros((GROUP, per), F32)
+            for b in range(2 * GROUP):
+                kept = kept + jnp.where(code == b, product[b * 8 : (b + 1) * 8], 0.0)
+            kept = kept.astype(BF)
+            for h in range(lev // 2):
+                out[par * (lev // 2) + h, 0, :, 0:piece] = kept[:, h * piece : (h + 1) * piece]
+            if par == 0:
+                ending = lax.dot_general(
+                    field, last, (((1,), (1,)), ((), ())), preferred_element_type=F32
+                )
+                lane8 = lax.broadcasted_iota(jnp.int32, (1, GROUP), 1)
+                kept = jnp.zeros((GROUP, GROUP), F32)
+                for b in range(GROUP):
+                    kept = kept + jnp.where(lane8 == b, ending[b * 16 + 8 : b * 16 + 16], 0.0)
+                out[lev // 2 - 1, 0, :, piece : piece + GROUP] = kept.astype(BF)
+
+    recv_specs = [
+        pl.BlockSpec((bands, row_block, (hi - lo) * LANE), lambda g, *_: (0, g, 0))
+        for lo, hi in chunks
+    ]
+    return pl.pallas_call(
+        body,
+        name="forward",
+        grid_spec=pltpu.PrefetchScalarGridSpec(
+            num_scalar_prefetch=1,
+            grid=(groups,),
+            in_specs=recv_specs
+            + [
+                pl.BlockSpec((row_total, GROUP, half_lat), lambda g, *_: (0, g, 0)),
+                pl.BlockSpec((1, half_lat), lambda g, *_: (0, 0)),
+            ],
+            out_specs=pl.BlockSpec((lev, 1, 8, piece + LANE), lambda g, *_: (0, g, 0, 0)),
+            scratch_shapes=[pltpu.VMEM((2, rows, half_lat), BF)],
+        ),
+        out_shape=jax.ShapeDtypeStruct((lev, groups, 8, piece + LANE), BF),
+    )(pairs, *received, table, quadrature[None, :])
+
+
+def mix_matrix(operator, own):
+    levels = operator.shape[0]
+    n = levels * 4
+    row = jnp.arange(n, dtype=jnp.int32)
+    level = row // (4 * own) * own + row // 2 % own
+    rest = row // (2 * own) % 2 * 2 + row % 2
+    hot = (level[:, None] == jnp.arange(levels)[None, :]).astype(BF)
+    spread = jnp.dot(jnp.dot(hot, operator, preferred_element_type=F32).astype(BF), hot.T,
+                     preferred_element_type=F32)
+    return jnp.where(rest[:, None] == rest[None, :], spread, 0.0).astype(BF), level
+
+
+def implicit_call(pairs, position, received, project, rebuild, factors, wave_count):
+    lev, groups, eight, lanes = received.shape
+    n = lev * eight
+    piece = lanes - LANE
+
+    def body(pairs_ref, pos_ref, x_ref, p_ref, r_ref, f_ref, out):
+        group = pl.program_id(0)
+        place = pos_ref[0]
+        par = place // (lev // 2)
+        half = place % (lev // 2) * (piece // GROUP)
+        lane = lax.broadcasted_iota(jnp.int32, (1, lanes), 1)
+        r = 2 * (lane // GROUP + half) + par
+        low = by_slot(lane % GROUP, pairs_ref, group)
+        degree = jnp.where(r >= wave_count - low, r - 1, low + r).astype(F32)
+        factor = degree * (degree + 1.0) / float(wave_count * wave_count)
+        damping = 1.0 / (1.0 + factor * f_ref[:, 0:1])
+        values = x_ref[...].reshape(n, lanes)
+        modes = jnp.dot(p_ref[...], values, preferred_element_type=F32)
+        damped = (modes * damping).astype(BF)
+        result = jnp.dot(r_ref[...], damped, preferred_element_type=F32)
+        out[...] = result.astype(BF).reshape(lev, 1, eight, lanes)
+
+    block = pl.BlockSpec((lev, 1, eight, lanes), lambda g, *_: (0, g, 0, 0))
+    small = pl.BlockSpec((n, n), lambda g, *_: (0, 0))
+    return pl.pallas_call(
+        body,
+        name="implicit",
+        grid_spec=pltpu.PrefetchScalarGridSpec(
+            num_scalar_prefetch=2,
+            grid=(groups,),
+            in_specs=[block, small, small, pl.BlockSpec((n, LANE), lambda g, *_: (0, 0))],
+            out_specs=block,
+        ),
+        out_shape=jax.ShapeDtypeStruct(received.shape, BF),
+    )(pairs, position, received, project, rebuild, factors)
+
+
+def inverse_call(pairs, implicit, table):
+    row_total, slots, half_lat = table.shape
+    wave_count = row_total - 1
+    lev, groups, eight, lanes = implicit.shape
+    piece = lanes - LANE
+    per = wave_count // 2 * GROUP
+    rows = 2 * GROUP * eight
+    own = eight // 4
+
+    def body(pairs_ref, x_ref, table_ref, out):
+        group = pl.program_id(0)
+        whole = table_ref[0:wave_count].reshape(wave_count // 2, 2, GROUP, half_lat)
+        sums = []
+        for par in range(2):
+            value = jnp.concatenate(
+                [x_ref[par * (lev // 2) + h, 0, :, 0:piece] for h in range(lev // 2)], axis=1
+            ).astype(F32)
+            code = part_code(pairs_ref, group, wave_count, 0, par, per)
+            spread = jnp.concatenate(
+                [jnp.where(code == b, value, 0.0) for b in range(2 * GROUP)], axis=0
+            ).astype(BF)
+            matrix = whole[:, par].reshape(per, half_lat)
+            sums.append(jnp.dot(spread, matrix, preferred_element_type=F32))
+        tail = x_ref[lev // 2 - 1, 0, :, piece : piece + GROUP].astype(F32)
+        lane8 = lax.broadcasted_iota(jnp.int32, (1, GROUP), 1)
+        nothing = jnp.zeros((eight, GROUP), F32)
+        spread = jnp.concatenate(
+            [
+                jnp.where(lane8 == b // 2, tail, 0.0) if b % 2 else nothing
+                for b in range(2 * GROUP)
+            ],
+            axis=0,
+        ).astype(BF)
+        sums[0] = sums[0] + jnp.dot(spread, table_ref[wave_count], preferred_element_type=F32)
+        row = lax.broadcasted_iota(jnp.int32, (rows, LANE), 0)
+        low = by_slot(row // (2 * eight), pairs_ref, group)
+        sign = (1 - 2 * (row // eight % 2 * low % 2)).astype(F32)
+        north = sums[0] + sums[1]
+        back = LANE - 1 - lax.broadcasted_iota(jnp.int32, (rows, LANE), 1)
+        tiles = half_lat // LANE
+        for target in range(tiles):
+            source = slice((tiles - 1 - target) * LANE, (tiles - target) * LANE)
+            south = sign * (sums[0][:, source] - sums[1][:, source])
+            south = jnp.take_along_axis(south, back, axis=1)
+            upper = north[:, target * LANE : (target + 1) * LANE]
+            for b in range(2 * GROUP):
+                for f in range(2 * own):
+                    at = slice(b * eight + 2 * f, b * eight + 2 * f + 2)
+                    place = (f // own, f % own, b // 2, b % 2)
+                    out[(*place, slice(None), slice(target * LANE, (target + 1) * LANE))] = upper[at]
+                    out[
+                        (
+                            *place,
+                            slice(None),
+                            slice(half_lat + target * LANE, half_lat + (target + 1) * LANE),
+                        )
+                    ] = south[at]
+
+    return pl.pallas_call(
+        body,
+        name="inverse",
+        grid_spec=pltpu.PrefetchScalarGridSpec(
+            num_scalar_prefetch=1,
+            grid=(groups,),
+            in_specs=[
+                pl.BlockSpec((lev, 1, eight, lanes), lambda g, *_: (0, g, 0, 0)),
+                pl.BlockSpec((row_total, GROUP, half_lat), lambda g, *_: (0, g, 0)),
+            ],
+            out_specs=pl.BlockSpec(
+                (2, own, GROUP, 2, 2, 2 * half_lat), lambda g, *_: (0, 0, g, 0, 0, 0)
+            ),
+        ),
+        out_shape=jax.ShapeDtypeStruct((2, own, slots, 2, 2, 2 * half_lat), F32),
+    )(pairs, implicit, table)
+
+
+def exchange(x, axis):
+    return lax.all_to_all(x, axis, 0, 0, tiled=True)
+
+
+def tiled_local(u, v, t, operator, quadrature, table, couples, project, rebuild, factors):
+    lev, lat = lax.axis_size("lev"), lax.axis_size("lat")
+    levels, band, lons = u.shape
+    own = levels // lev
+    slots, row_total, _ = table.shape
+    wave_count = row_total - 1
+    pairs = lax.dynamic_slice_in_dim(couples, lax.axis_index("lat") * slots, slots)
+    flat = jnp.transpose(table, (1, 0, 2))
+    waves = wave_rows_call(couples, lons * lev, wave_count)
+    received = []
+    for lo, hi in CHUNKS:
+        products = products_call(u, v, t, operator, lev, lo, hi - lo)
+        products = exchange(products, "lev")
+        pieces = products.reshape(lev, (hi - lo) * LANE, lons)
+        fourier = fourier_call(waves, pieces)
+        received.append(exchange(fourier.reshape(lat, slots * 4, -1), "lat"))
+    spectral = exchange(forward_call(pairs, received, CHUNKS, flat, quadrature, lev), "lev")
+    to_modes, level = mix_matrix(project, own)
+    to_levels, _ = mix_matrix(rebuild, own)
+    factor_rows = jnp.broadcast_to(factors[level][:, None], (level.shape[0], LANE))
+    position = lax.axis_index("lev").astype(jnp.int32)[None]
+    implicit = implicit_call(
+        pairs, position, spectral, to_modes, to_levels, factor_rows, wave_count
+    )
+    return inverse_call(pairs, exchange(implicit, "lev"), flat)
+
+
+def fits(lev, band, lons, levels, slots, row_total, half_lat):
+    return (
+        lev % 2 == 0
+        and levels == 2 * lev
+        and band == CHUNKS[-1][1] * SUB
+        and lons % LANE == 0
+        and slots % GROUP == 0
+        and row_total % 2 == 1
+        and (row_total - 1) * GROUP % (lev * LANE) == 0
+        and half_lat % LANE == 0
+    )
 
 
 def fourier_table(position_wavenumber_couples, lon_count, wave_count):
@@ -89,7 +476,7 @@
     return jnp.transpose(latitudes, (4, 5, 0, 2, 3, 1))
 
 
-def local(
+def plain_local(
     zonal_velocity,
     meridional_velocity,
     air_warmth,
@@ -166,6 +553,22 @@
     return inverse_legendre(implicit, associated_polynomial_table, own_pairs, wave_count)
 
 
+def local(*args):
+    table = args[5]
+    sizes = args[0].shape
+    if fits(
+        lax.axis_size("lev"),
+        sizes[1],
+        sizes[2],
+        sizes[0],
+        table.shape[0],
+        table.shape[1],
+        table.shape[2],
+    ):
+        return tiled_local(*args)
+    return plain_local(*args)
+
+
 def solution(mesh):
     placed = (
         P(None, "lat", "lev"),

time: 361 us -> 183 us (0.51)
  matrix products: 123 us -> 1.79 us
  Pallas kernels: 0 us -> 82.8 us
  local copies, waits for them, and re-layouts: 74.8 us -> 6.07 us
  waiting for transfers between devices: 103 us -> 50.4 us
  other arithmetic: 26.6 us -> 5.8 us
  starting transfers between devices: 14.5 us -> 21.5 us
    dot_general x5 -> x2, matrix products: 123 us -> 1.79 us  [mix_matrix(): jnp.dot(jnp.dot(hot, operator, preferred_element_type=F32).astype(BF), ho...]
    pallas_call x0 -> x8, Pallas kernels: none -> 82.8 us  [the longest x1 21.1 us: wave_rows_call(): pl.pallas_call(body, name='wave_rows', grid=(rows // block,), in_specs=[s...]
    all_to_all x3 -> x5, waiting for transfers between devices: 103 us -> 50.4 us  [exchange(): return lax.all_to_all(x, axis, 0, 0, tiled=True)]
    rev x2 -> x0, local copies, waits for them, and re-layouts: 24.1 us -> none  [the longest x1 14 us: forward_legendre(): southern = by_wave[:, :, half_rows:][:, :, ::-1].astype(jnp.float32)]
    reshape x5 -> x1, local copies, waits for them, and re-layouts: 14.6 us -> 0.13 us  [wave_rows_call(): low = jnp.repeat(couples, 4)]
    all_to_all x7 -> x0, local copies, waits for them, and re-layouts: 13.5 us -> none  [the longest x2 7.3 us: local(): lax.all_to_all(harmonic_coefficients_field, 'lat', split_axis=3, concat_a...]
    transpose x2 -> x0, other arithmetic: 8.07 us -> none  [the longest x1 4.62 us: inverse_legendre(): return jnp.transpose(latitudes, (4, 5, 0, 2, 3, 1))]
    reduce_sum x1 -> x0, other arithmetic: 7.02 us -> none  [forward_legendre(): jnp.sum(jnp.where(chosen[..., None, None, None], product, 0.0), axis=(2, 3))]
  transfers between devices with their start and end apart: 3 -> 5, of which waited for: 3 -> 4; matrix products, arithmetic and copies ran while one was open for 0% -> 6% of each run, Pallas kernels for 0% -> 22%
where the time goes in v1:
time: 183 us; the launch traced here: 180 us
  Pallas kernels  82.8 us (45%)
  waiting for transfers between devices  50.4 us (28%)
  starting transfers between devices  21.5 us (12%)
  blocking collectives  11.1 us (6%)
  local copies, waits for them, and re-layouts  6.07 us (3%)
  other arithmetic  5.8 us (3%)
    all_to_all x5, waiting for transfers between devices, exchange(): return lax.all_to_all(x, axis, 0, 0, tiled=True)  50.4 us
    all_to_all x5, starting transfers between devices, exchange(): return lax.all_to_all(x, axis, 0, 0, tiled=True)  21.5 us
    pallas_call x1, Pallas kernels, wave_rows_call(): pl.pallas_call(body, name='wave_rows', grid=(rows // block,), in_specs=[s...  21.1 us
    pallas_call x1, Pallas kernels, forward_call(): pl.pallas_call(body, name='forward', grid_spec=pltpu.PrefetchScalarGridSp...  19.4 us
    pallas_call x1, Pallas kernels, inverse_call(): pl.pallas_call(body, name='inverse', grid_spec=pltpu.PrefetchScalarGridSp...  15.6 us
    pallas_call x2, Pallas kernels, fourier_call(): pl.pallas_call(body, name='fourier', grid=(steps,), in_specs=[pl.BlockSpe...  13.9 us
    all_to_all x1, blocking collectives, exchange(): return lax.all_to_all(x, axis, 0, 0, tiled=True)  11.1 us
    pallas_call x2, Pallas kernels, products_call(): pl.pallas_call(body, name='products', grid=(count,), in_specs=[pl.BlockSp...  7.74 us
  transfers between devices with their start and end apart: 5, of which 4 were waited for; matrix products, arithmetic and copies ran while one was open for 6% of the time, Pallas kernels for 22%

profile of v1, /device:TPU:0, one launch (start us, length us, event | category | flops | bytes accessed | tf_op | source)
XLA Modules:
  0.0 179.6 jit_solution(11947587222023413130)
XLA Ops:
  0.0 1.3 convert_element_type.31.op
  1.3 3.2 %products.2 = bf16[4,2,4,32,640]{4,3,2,1,0:T(8,128)(2,1)} custom-call(f32[8,8]{1,0:T(8,128)} %convert_element_type.31.op, bf16[8,160,640]{2,1,0:T(8,128)(2,1)} %u_ref.3, bf16[8,160,640]{2,1,0:T(8,128)(2,1)} %v_ref.3, bf16[8,160,640]{2,1,0:T(8,128)(2,1)} %t_ref.3), custom_call_target="tpu_custom_call" | custom-call | tf_op jit(solution)/shard_map/products/pallas_call | solution.py:36
  4.5 5.2 %all-to-all-start = ((bf16[4,2,4,32,640]{4,3,2,1,0:T(8,128)(2,1)}), bf16[4,2,4,32,640]{4,3,2,1,0:T(8,128)(2,1)S(1)}, u32[]{:S(2)}, u32[]{:S(2)}) async-start(bf16[4,2,4,32,640]{4,3,2,1,0:T(8,128)(2,1)} %products.2), calls=%async_computation | async-start | bytes 2621440 | tf_op jit(solution)/shard_map/all_to_all | solution.py:353
  9.6 4.6 %products.3 = bf16[4,3,4,32,640]{4,3,2,1,0:T(8,128)(2,1)} custom-call(f32[8,8]{1,0:T(8,128)} %convert_element_type.31.op, bf16[8,160,640]{2,1,0:T(8,128)(2,1)} %u_ref.3, bf16[8,160,640]{2,1,0:T(8,128)(2,1)} %v_ref.3, bf16[8,160,640]{2,1,0:T(8,128)(2,1)} %t_ref.3), custom_call_target="tpu_custom_call" | custom-call | tf_op jit(solution)/shard_map/products/pallas_call | solution.py:36
  14.2 11.9 %all-to-all-done = bf16[4,2,4,32,640]{4,3,2,1,0:T(8,128)(2,1)S(1)} async-done(((bf16[4,2,4,32,640]{4,3,2,1,0:T(8,128)(2,1)}), bf16[4,2,4,32,640]{4,3,2,1,0:T(8,128)(2,1)S(1)}, u32[]{:S(2)}, u32[]{:S(2)}) %all-to-all-start) | async-done | bytes 1310752 | tf_op jit(solution)/shard_map/all_to_all | solution.py:353
  26.1 3.6 %all-to-all-start.2 = ((bf16[4,3,4,32,640]{4,3,2,1,0:T(8,128)(2,1)}), bf16[4,3,4,32,640]{4,3,2,1,0:T(8,128)(2,1)S(1)}, u32[]{:S(2)}, u32[]{:S(2)}) async-start(bf16[4,3,4,32,640]{4,3,2,1,0:T(8,128)(2,1)} %products.3), calls=%async_computation.2 | async-start | bytes 3932160 | tf_op jit(solution)/shard_map/all_to_all | solution.py:353
  30.1 4.3 %fusion.7 = (f32[1280,128]{1,0:T(8,128)}, f32[1280,128]{1,0:T(8,128)}) fusion(s32[1280]{0:T(1024)S(1)} %get-tuple-element.6, pred[1280]{0:T(1024)(128)(4,1)S(1)} %fusion.8), kind=kLoop, calls=%fused_computation.17 | loop fusion | flops 2293760 | bytes 1317120 | tf_op jit(solution)/shard_map/jit(_where)/select_n | solution.py:59
  34.5 1.1 broadcast_in_dim.55.c_ref
  35.5 1.1 broadcast_in_dim.56.s_ref
  36.6 21.1 %wave_rows.1.w_ref = bf16[1280,2560]{1,0:T(8,128)(2,1)} custom-call(f32[1280,128]{1,0:T(8,128)} %get-tuple-element.8.a_ref, f32[1280,128]{1,0:T(8,128)} %get-tuple-element.7.b_ref, f32[1280,128]{1,0:T(8,128)} %broadcast_in_dim.55.c_ref, f32[1280,128]{1,0:T(8,128)} %broadcast_in_dim.56.s_ref), custom_call_target="tpu_custom_call" | custom-call | tf_op jit(solution)/shard_map/wave_rows/pallas_call | solution.py:69
  57.8 6.1 %fourier.2 = bf16[1280,256]{1,0:T(8,128)(2,1)} custom-call(bf16[1280,2560]{1,0:T(8,128)(2,1)} %wave_rows.1.w_ref, bf16[4,256,640]{2,1,0:T(8,128)(2,1)} %bitcast.13), custom_call_target="tpu_custom_call" | custom-call | tf_op jit(solution)/shard_map/fourier/pallas_call | solution.py:96
  63.9 5.0 %all-to-all-start.1 = ((bf16[8,160,256]{2,1,0:T(8,128)(2,1)}), bf16[8,160,256]{2,1,0:T(8,128)(2,1)S(1)}, u32[]{:S(2)}, u32[]{:S(2)}) async-start(bf16[8,160,256]{2,1,0:T(8,128)(2,1)} %bitcast.15), calls=%async_computation.1 | async-start | bytes 1310720 | tf_op jit(solution)/shard_map/all_to_all | solution.py:353
  68.9 7.8 %fourier.3 = bf16[1280,384]{1,0:T(8,128)(2,1)} custom-call(bf16[1280,2560]{1,0:T(8,128)(2,1)} %wave_rows.1.w_ref, bf16[4,384,640]{2,1,0:T(8,128)(2,1)} %bitcast.12), custom_call_target="tpu_custom_call" | custom-call | tf_op jit(solution)/shard_map/fourier/pallas_call | solution.py:96
  76.7 10.3 %all-to-all-done.1.refs_0_ = bf16[8,160,256]{2,1,0:T(8,128)(2,1)S(1)} async-done(((bf16[8,160,256]{2,1,0:T(8,128)(2,1)}), bf16[8,160,256]{2,1,0:T(8,128)(2,1)S(1)}, u32[]{:S(2)}, u32[]{:S(2)}) %all-to-all-start.1) | async-done | bytes 655392 | tf_op jit(solution)/shard_map/all_to_all | solution.py:353
  87.0 3.6 %all-to-all-start.3 = ((bf16[8,160,384]{2,1,0:T(8,128)(2,1)}), bf16[8,160,384]{2,1,0:T(8,128)(2,1)S(1)}, u32[]{:S(2)}, u32[]{:S(2)}) async-start(bf16[8,160,384]{2,1,0:T(8,128)(2,1)} %bitcast.14), calls=%async_computation.3 | async-start | bytes 1966080 | tf_op jit(solution)/shard_map/all_to_all | solution.py:353
  92.6 23.1 %all-to-all-done.3.refs_1_ = bf16[8,160,384]{2,1,0:T(8,128)(2,1)S(1)} async-done(((bf16[8,160,384]{2,1,0:T(8,128)(2,1)}), bf16[8,160,384]{2,1,0:T(8,128)(2,1)S(1)}, u32[]{:S(2)}, u32[]{:S(2)}) %all-to-all-start.3) | async-done | bytes 983072 | tf_op jit(solution)/shard_map/all_to_all | solution.py:353
  115.7 0.9 copy-done.4
  116.6 19.4 %forward.1 = bf16[4,5,8,1408]{3,2,1,0:T(8,128)(2,1)} custom-call(s32[40]{0:T(128)} %dynamic_slice.3.pairs_ref, bf16[8,160,256]{2,1,0:T(8,128)(2,1)} %copy-done.5, bf16[8,160,384]{2,1,0:T(8,128)(2,1)} %copy-done.4, bf16[641,40,640]{2,1,0:T(8,128)(2,1)} %bitcast.10, f32[1,640]{1,0:T(1,128)} %broadcast_in_dim.57.refs_3_), custom_call_target="tpu_custom_call" | custom-call | tf_op jit(solution)/shard_map/forward/pallas_call | solution.py:209
  136.1 4.2 %all-to-all-start.4 = ((bf16[4,5,8,1408]{3,2,1,0:T(8,128)(2,1)}), bf16[4,5,8,1408]{3,2,1,0:T(8,128)(2,1)S(1)}, u32[]{:S(2)}, u32[]{:S(2)}) async-start(bf16[4,5,8,1408]{3,2,1,0:T(8,128)(2,1)} %forward.1), calls=%async_computation.4 | async-start | bytes 901120 | tf_op jit(solution)/shard_map/all_to_all | solution.py:353
  141.1 0.9 fusion.1.r_ref
  142.0 5.1 %all-to-all-done.4.x_ref = bf16[4,5,8,1408]{3,2,1,0:T(8,128)(2,1)S(1)} async-done(((bf16[4,5,8,1408]{3,2,1,0:T(8,128)(2,1)}), bf16[4,5,8,1408]{3,2,1,0:T(8,128)(2,1)S(1)}, u32[]{:S(2)}, u32[]{:S(2)}) %all-to-all-start.4) | async-done | bytes 450592 | tf_op jit(solution)/shard_map/all_to_all | solution.py:353
  147.9 5.0 %implicit.1 = bf16[4,5,8,1408]{3,2,1,0:T(8,128)(2,1)} custom-call(s32[40]{0:T(128)} %dynamic_slice.3.pairs_ref, s32[1]{0:T(128)} %bitcast.pos_ref, bf16[4,5,8,1408]{3,2,1,0:T(8,128)(2,1)} %copy-done.6, bf16[32,32]{1,0:T(8,128)(2,1)} %fusion.p_ref, bf16[32,32]{1,0:T(8,128)(2,1)} %fusion.1.r_ref, f32[32,128]{1,0:T(8,128)} %broadcast_in_dim.59.f_ref), custom_call_target="tpu_custom_call" | custom-call | tf_op jit(solution)/shard_map/implicit/pallas_call | solution.py:263
  152.8 11.1 %all_to_all.30.x_ref = bf16[4,5,8,1408]{3,2,1,0:T(8,128)(2,1)} all-to-all(bf16[4,5,8,1408]{3,2,1,0:T(8,128)(2,1)} %implicit.1), channel_id=1, replica_groups=mesh['lev'=4,'lat'=8] {'lev'}, dimensions={0} | all-to-all | bytes 901120 | tf_op jit(solution)/shard_map/all_to_all | solution.py:353
  163.9 15.6 %inverse.1 = f32[2,2,40,2,2,1280]{5,4,3,2,1,0:T(2,128)} custom-call(s32[40]{0:T(128)} %dynamic_slice.3.pairs_ref, bf16[4,5,8,1408]{3,2,1,0:T(8,128)(2,1)} %all_to_all.30.x_ref, bf16[641,40,640]{2,1,0:T(8,128)(2,1)} %bitcast.11), custom_call_target="tpu_custom_call" | custom-call | tf_op jit(solution)/shard_map/inverse/pallas_call | solution.py:334
  (33 shorter events, 4.0 us)
Async XLA Ops:
  0.0 140.2 %copy-start = (bf16[8,8]{1,0:T(8,128)(2,1)S(1)}, bf16[8,8]{1,0:T(8,128)(2,1)}, u32[]{:S(2)}) copy-start(bf16[8,8]{1,0:T(8,128)(2,1)} %param.17) | copy-start | bytes 388
  4.5 21.6 %all-to-all-start = ((bf16[4,2,4,32,640]{4,3,2,1,0:T(8,128)(2,1)}), bf16[4,2,4,32,640]{4,3,2,1,0:T(8,128)(2,1)S(1)}, u32[]{:S(2)}, u32[]{:S(2)}) async-start(bf16[4,2,4,32,640]{4,3,2,1,0:T(8,128)(2,1)} %products.2), calls=%async_computation | async-start | bytes 2621440 | tf_op jit(solution)/shard_map/all_to_all | solution.py:353
  14.2 15.5 %copy-start.8 = (s32[320]{0:T(512)S(1)}, s32[320]{0:T(512)}, u32[]{:S(2)}) copy-start(s32[320]{0:T(512)} %param.16) | copy-start | bytes 3844
  26.1 3.7 %copy-start.3 = (bf16[4,2,4,32,640]{4,3,2,1,0:T(8,128)(2,1)}, bf16[4,2,4,32,640]{4,3,2,1,0:T(8,128)(2,1)S(1)}, u32[]{:S(2)}) copy-start(bf16[4,2,4,32,640]{4,3,2,1,0:T(8,128)(2,1)S(1)} %all-to-all-done) | copy-start | bytes 3932164
  26.1 37.8 %all-to-all-start.2 = ((bf16[4,3,4,32,640]{4,3,2,1,0:T(8,128)(2,1)}), bf16[4,3,4,32,640]{4,3,2,1,0:T(8,128)(2,1)S(1)}, u32[]{:S(2)}, u32[]{:S(2)}) async-start(bf16[4,3,4,32,640]{4,3,2,1,0:T(8,128)(2,1)} %products.3), calls=%async_computation.2 | async-start | bytes 3932160 | tf_op jit(solution)/shard_map/all_to_all | solution.py:353
  63.9 5.0 %copy-start.2 = (bf16[4,3,4,32,640]{4,3,2,1,0:T(8,128)(2,1)}, bf16[4,3,4,32,640]{4,3,2,1,0:T(8,128)(2,1)S(1)}, u32[]{:S(2)}) copy-start(bf16[4,3,4,32,640]{4,3,2,1,0:T(8,128)(2,1)S(1)} %all-to-all-done.2) | copy-start | bytes 5898244
  63.9 23.1 %all-to-all-start.1 = ((bf16[8,160,256]{2,1,0:T(8,128)(2,1)}), bf16[8,160,256]{2,1,0:T(8,128)(2,1)S(1)}, u32[]{:S(2)}, u32[]{:S(2)}) async-start(bf16[8,160,256]{2,1,0:T(8,128)(2,1)} %bitcast.15), calls=%async_computation.1 | async-start | bytes 1310720 | tf_op jit(solution)/shard_map/all_to_all | solution.py:353
  76.7 14.6 %copy-start.7 = (f32[640]{0:T(1024)S(1)}, f32[640]{0:T(1024)}, u32[]{:S(2)}) copy-start(f32[640]{0:T(1024)} %param.14) | copy-start | bytes 7684
  76.7 15.2 %copy-start.1 = (f32[8]{0:T(128)S(1)}, f32[8]{0:T(128)}, u32[]{:S(2)}) copy-start(f32[8]{0:T(128)} %param.19) | copy-start | bytes 100
  87.0 28.7 %copy-start.5 = (bf16[8,160,256]{2,1,0:T(8,128)(2,1)}, bf16[8,160,256]{2,1,0:T(8,128)(2,1)S(1)}, u32[]{:S(2)}) copy-start(bf16[8,160,256]{2,1,0:T(8,128)(2,1)S(1)} %all-to-all-done.1.refs_0_) | copy-start | bytes 1966084
  87.0 28.6 %all-to-all-start.3 = ((bf16[8,160,384]{2,1,0:T(8,128)(2,1)}), bf16[8,160,384]{2,1,0:T(8,128)(2,1)S(1)}, u32[]{:S(2)}, u32[]{:S(2)}) async-start(bf16[8,160,384]{2,1,0:T(8,128)(2,1)} %bitcast.14), calls=%async_computation.3 | async-start | bytes 1966080 | tf_op jit(solution)/shard_map/all_to_all | solution.py:353
  115.7 0.9 copy-start.4
  116.6 24.5 %copy-start.9 = (bf16[8,8]{1,0:T(8,128)(2,1)S(1)}, bf16[8,8]{1,0:T(8,128)(2,1)}, u32[]{:S(2)}) copy-start(bf16[8,8]{1,0:T(8,128)(2,1)} %param.18) | copy-start | bytes 388
  136.1 11.0 %all-to-all-start.4 = ((bf16[4,5,8,1408]{3,2,1,0:T(8,128)(2,1)}), bf16[4,5,8,1408]{3,2,1,0:T(8,128)(2,1)S(1)}, u32[]{:S(2)}, u32[]{:S(2)}) async-start(bf16[4,5,8,1408]{3,2,1,0:T(8,128)(2,1)} %forward.1), calls=%async_computation.4 | async-start | bytes 901120 | tf_op jit(solution)/shard_map/all_to_all | solution.py:353
  147.1 0.8 copy-start.6

commit v2 on v1

--- a/solution.py
+++ b/solution.py
@@ -7,103 +7,168 @@
 from jax.experimental.pallas import tpu as pltpu
 from jax.sharding import PartitionSpec as P
 
+
 BF = jnp.bfloat16
 F32 = jnp.float32
 LANE = 128
 GROUP = 8
 SUB = 32
 CHUNKS = ((0, 2), (2, 5))
-
-
-def products_call(u, v, t, operator, lev, first, count):
-    levels, band, lons = u.shape
+CUT = (1, 2)
+
+
+def products_call(place, u, v, t, operator, lev, first, count):
+    levels, _, lons = u.shape
     own = levels // lev
-
-    def body(op, u_ref, v_ref, t_ref, out):
+    split = SUB // 8
+
+    def body(place_ref, op_ref, u_ref, v_ref, t_ref, *rest):
+        outs, factors = rest[:lev], rest[lev]
+
+        @pl.when(pl.program_id(0) == 0)
+        def _():
+            values = op_ref[...].astype(F32)
+            for k in range(levels):
+                for j in range(levels):
+                    factors[k, j] = jnp.broadcast_to(values[k : k + 1, j : j + 1], (8, LANE))
+
         for tile in range(lons // LANE):
             at = slice(tile * LANE, (tile + 1) * LANE)
-            warm = [t_ref[j, :, at].astype(F32) for j in range(levels)]
-            for k in range(levels):
-                height = op[k, 0] * warm[0]
-                for j in range(1, levels):
-                    height = height + op[k, j] * warm[j]
-                east = u_ref[k, :, at].astype(F32)
-                north = v_ref[k, :, at].astype(F32)
-                out[k // own, 0, k % own, :, at] = (east * north + height).astype(BF)
-                out[k // own, 0, own + k % own, :, at] = ((east + north) * warm[k]).astype(BF)
-
-    grid_in = pl.BlockSpec((levels, SUB, lons), lambda h: (0, first + h, 0))
+            warm = [t_ref[j, :, at].astype(F32).reshape(split, 8, LANE) for j in range(levels)]
+            for d in range(lev):
+                for own_level in range(own):
+                    k = jnp.bitwise_xor(place_ref[0], d) * own + own_level
+                    height = factors[k, 0] * warm[0]
+                    for j in range(1, levels):
+                        height = height + factors[k, j] * warm[j]
+                    height = height.reshape(SUB, LANE)
+                    east = u_ref[k, :, at].astype(F32)
+                    north = v_ref[k, :, at].astype(F32)
+                    here = t_ref[k, :, at].astype(F32)
+                    outs[d][0, own_level, :, at] = (east * north + height).astype(BF)
+                    outs[d][0, own + own_level, :, at] = ((east + north) * here).astype(BF)
+
+    grid_in = pl.BlockSpec((levels, SUB, lons), lambda h, *_: (0, first + h, 0))
     return pl.pallas_call(
         body,
         name="products",
-        grid=(count,),
-        in_specs=[pl.BlockSpec(memory_space=pltpu.SMEM), grid_in, grid_in, grid_in],
-        out_specs=pl.BlockSpec((lev, 1, 2 * own, SUB, lons), lambda h: (0, h, 0, 0, 0)),
-        out_shape=jax.ShapeDtypeStruct((lev, count, 2 * own, SUB, lons), BF),
-    )(operator.astype(F32), u, v, t)
+        grid_spec=pltpu.PrefetchScalarGridSpec(
+            num_scalar_prefetch=1,
+            grid=(count,),
+            in_specs=[
+                pl.BlockSpec((levels, levels), lambda h, *_: (0, 0)),
+                grid_in,
+                grid_in,
+                grid_in,
+            ],
+            out_specs=[pl.BlockSpec((1, 2 * own, SUB, lons), lambda h, *_: (h, 0, 0, 0))] * lev,
+            scratch_shapes=[pltpu.VMEM((levels, levels, 8, LANE), F32)],
+        ),
+        out_shape=[jax.ShapeDtypeStruct((count, 2 * own, SUB, lons), BF)] * lev,
+    )(place, operator, u, v, t)
+
+
+def sine_cosine(index, period):
+    quarter = period // 4
+    turn = (index + period // 8) // quarter
+    angle = (index - turn * quarter).astype(F32) * (2.0 * math.pi / period)
+    square = angle * angle
+    sine = 1.0 / 362880
+    for c in (-1.0 / 5040, 1.0 / 120, -1.0 / 6, 1.0):
+        sine = sine * square + c
+    sine = sine * angle
+    cosine = -1.0 / 3628800
+    for c in (1.0 / 40320, -1.0 / 720, 1.0 / 24, -0.5, 1.0):
+        cosine = cosine * square + c
+    odd = turn % 2 == 1
+    first = jnp.where(odd, cosine, sine)
+    second = jnp.where(odd, sine, cosine)
+    turn = turn % 4
+    return jnp.where(turn >= 2, -first, first), jnp.where((turn == 1) | (turn == 2), -second, second)
 
 
 def wave_rows_call(couples, lon_count, wave_count):
     rows = 4 * couples.shape[0]
-    row = jnp.arange(rows, dtype=jnp.int32)
-    low = jnp.repeat(couples, 4)
-    wave = jnp.where(row // 2 % 2 == 0, low, wave_count - 1 - low)[:, None]
-    lane = jnp.arange(LANE, dtype=jnp.int32)[None, :]
-    unit = 2.0 * math.pi / lon_count
-    start = (wave * lane % lon_count).astype(F32) * unit
-    step = jnp.broadcast_to((wave * LANE % lon_count).astype(F32) * unit, (rows, LANE))
+    block = rows // 4
+    chunk = 16
     scale = 1.0 / math.sqrt(lon_count)
-    cosine, sine = jnp.cos(start) * scale, jnp.sin(start) * scale
-    is_sine = (row % 2 == 1)[:, None]
-    first = jnp.where(is_sine, -sine, cosine)
-    second = jnp.where(is_sine, cosine, sine)
-    block = GROUP * 4
-
-    def body(a_ref, b_ref, c_ref, s_ref, out):
-        a, b, c, s = a_ref[...], b_ref[...], c_ref[...], s_ref[...]
-        for tile in range(lon_count // LANE):
-            out[:, tile * LANE : (tile + 1) * LANE] = a.astype(BF)
-            a, b = a * c - b * s, b * c + a * s
-
-    spec = pl.BlockSpec((block, LANE), lambda i: (i, 0))
+
+    def body(couples_ref, out):
+        base = pl.program_id(0) * (block // 4)
+        row = lax.broadcasted_iota(jnp.int32, (chunk, LANE), 0)
+        lane = lax.broadcasted_iota(jnp.int32, (chunk, LANE), 1)
+
+        def some_rows(index, carry):
+            low = jnp.full((chunk, LANE), couples_ref[base + index * (chunk // 4)], jnp.int32)
+            for n in range(1, chunk // 4):
+                low = jnp.where(row // 4 == n, couples_ref[base + index * (chunk // 4) + n], low)
+            wave = jnp.where(row // 2 % 2 == 0, low, wave_count - 1 - low)
+            sine, cosine = sine_cosine(wave * lane % lon_count, lon_count)
+            s, c = sine_cosine(wave * LANE % lon_count, lon_count)
+            is_sine = row % 2 == 1
+            a = jnp.where(is_sine, -sine, cosine) * scale
+            b = jnp.where(is_sine, cosine, sine) * scale
+            at = pl.ds(pl.multiple_of(index * chunk, chunk), chunk)
+            for tile in range(lon_count // LANE):
+                out[at, tile * LANE : (tile + 1) * LANE] = a.astype(BF)
+                a, b = a * c - b * s, b * c + a * s
+            return carry
+
+        lax.fori_loop(0, block // chunk, some_rows, 0, unroll=2)
+
     return pl.pallas_call(
         body,
         name="wave_rows",
-        grid=(rows // block,),
-        in_specs=[spec] * 4,
-        out_specs=pl.BlockSpec((block, lon_count), lambda i: (i, 0)),
+        grid_spec=pltpu.PrefetchScalarGridSpec(
+            num_scalar_prefetch=1,
+            grid=(rows // block,),
+            in_specs=[],
+            out_specs=pl.BlockSpec((block, lon_count), lambda i, *_: (i, 0)),
+        ),
         out_shape=jax.ShapeDtypeStruct((rows, lon_count), BF),
-    )(first, second, jnp.cos(step), jnp.sin(step))
-
-
-def fourier_call(waves, pieces, steps=4):
-    parts, rows, lons = pieces.shape
+    )(couples)
+
+
+def fourier_call(place, here, waves, pieces, peers):
+    parts = len(pieces)
+    rows, lons = pieces[0].shape
     columns = waves.shape[0]
-    block = columns // steps
-
-    def body(w_ref, x_ref, out):
-        total = None
-        for j in range(parts):
-            term = lax.dot_general(
-                w_ref[:, j * lons : (j + 1) * lons],
-                x_ref[j],
-                (((1,), (1,)), ((), ())),
-                preferred_element_type=F32,
-            )
-            total = term if total is None else total + term
-        out[...] = total.astype(BF)
+    block = columns // peers
+
+    def body(place_ref, here_ref, w_ref, *refs):
+        outs, total = refs[parts : parts + peers], refs[parts + peers]
+        for d in range(parts):
+
+            @pl.when(pl.program_id(0) == d)
+            def _():
+                term = lax.dot_general(
+                    w_ref[...], refs[d][...], (((1,), (1,)), ((), ())), preferred_element_type=F32
+                )
+                if d > 0:
+                    term = total[...] + term
+                total[...] = term
+
+        @pl.when(pl.program_id(0) == parts - 1)
+        def _():
+            for e in range(peers):
+                start = pl.multiple_of(jnp.bitwise_xor(here_ref[0], e) * block, 16)
+                outs[e][...] = total[pl.ds(start, block)].astype(BF)
 
     return pl.pallas_call(
         body,
         name="fourier",
-        grid=(steps,),
-        in_specs=[
-            pl.BlockSpec((block, parts * lons), lambda i: (i, 0)),
-            pl.BlockSpec((parts, rows, lons), lambda i: (0, 0, 0)),
-        ],
-        out_specs=pl.BlockSpec((block, rows), lambda i: (i, 0)),
-        out_shape=jax.ShapeDtypeStruct((columns, rows), BF),
-    )(waves, pieces)
+        grid_spec=pltpu.PrefetchScalarGridSpec(
+            num_scalar_prefetch=2,
+            grid=(parts,),
+            in_specs=[
+                pl.BlockSpec((columns, lons), lambda i, p, h: (0, jnp.bitwise_xor(p[0], i)))
+            ]
+            + [pl.BlockSpec((rows, lons), lambda i, *_: (0, 0))] * parts,
+            out_specs=[pl.BlockSpec((block, rows), lambda i, *_: (0, 0))] * peers,
+            scratch_shapes=[pltpu.VMEM((columns, rows), F32)],
+        ),
+        out_shape=[jax.ShapeDtypeStruct((block, rows), BF)] * peers,
+    )(place, here, waves, *pieces)
 
 
 def by_slot(index, pairs, group):
@@ -121,26 +186,31 @@
     return 2 * slot + (r >= wave_count - low).astype(jnp.int32)
 
 
-def forward_call(pairs, received, chunks, table, quadrature, lev):
-    row_total, slots, half_lat = table.shape
+def forward_call(pairs, here, received, chunks, table, quadrature, first, groups):
+    row_total, _, half_lat = table.shape
     wave_count = row_total - 1
-    bands = received[0].shape[0]
+    bands = len(received[0])
+    shares = [block for blocks in received for block in blocks]
     units = chunks[-1][1]
-    groups = slots // GROUP
     row_block = GROUP * 4
     fields = LANE // SUB
     rows = fields * row_block
     per = wave_count // 2 * GROUP
-    piece = per * 2 // lev
     where_unit = {}
     for number, (lo, hi) in enumerate(chunks):
         for unit in range(lo, hi):
             where_unit[unit] = (number, unit - lo)
 
-    def body(pairs_ref, *refs):
-        recv = refs[: len(chunks)]
-        table_ref, quad_ref, out, spread = refs[len(chunks) :]
-        group = pl.program_id(0)
+    def body(pairs_ref, here_ref, *refs):
+        shared = refs[: len(shares)]
+        table_ref, quad_ref, out, spread = refs[len(shares) : len(shares) + 4]
+        recv = refs[len(shares) + 4 :]
+        group = pl.program_id(0) + first
+        mine = pl.ds(pl.multiple_of(group * row_block, row_block), row_block)
+        for number in range(len(chunks)):
+            for e in range(bands):
+                band = jnp.bitwise_xor(here_ref[0], e)
+                recv[number][band] = shared[number * bands + e][mine].astype(F32)
         lane = lax.broadcasted_iota(jnp.int32, (row_block, LANE), 1)
         within, place = lane % SUB, lane // SUB
         row = lax.broadcasted_iota(jnp.int32, (row_block, LANE), 0)
@@ -150,7 +220,7 @@
 
         def tile(band, unit):
             number, local = where_unit[unit]
-            return recv[number][band, :, local * LANE : (local + 1) * LANE].astype(F32)
+            return recv[number][band, :, local * LANE : (local + 1) * LANE]
 
         for target in range(half_lat // LANE):
             at = slice(target * LANE, (target + 1) * LANE)
@@ -178,7 +248,7 @@
         order = (source == wanted).astype(BF)
         whole = table_ref[0:wave_count].reshape(wave_count // 2, 2, GROUP, half_lat)
         last = table_ref[wave_count]
-        out[...] = jnp.zeros(out.shape, BF)
+        out[0, :, 2 * per :] = jnp.zeros((8, LANE), BF)
         for par in range(2):
             field = jnp.dot(order, spread[par], preferred_element_type=F32).astype(BF)
             matrix = whole[:, par].reshape(per, half_lat)
@@ -189,9 +259,7 @@
             kept = jnp.zeros((GROUP, per), F32)
             for b in range(2 * GROUP):
                 kept = kept + jnp.where(code == b, product[b * 8 : (b + 1) * 8], 0.0)
-            kept = kept.astype(BF)
-            for h in range(lev // 2):
-                out[par * (lev // 2) + h, 0, :, 0:piece] = kept[:, h * piece : (h + 1) * piece]
+            out[0, :, par * per : (par + 1) * per] = kept.astype(BF)
             if par == 0:
                 ending = lax.dot_general(
                     field, last, (((1,), (1,)), ((), ())), preferred_element_type=F32
@@ -200,28 +268,25 @@
                 kept = jnp.zeros((GROUP, GROUP), F32)
                 for b in range(GROUP):
                     kept = kept + jnp.where(lane8 == b, ending[b * 16 + 8 : b * 16 + 16], 0.0)
-                out[lev // 2 - 1, 0, :, piece : piece + GROUP] = kept.astype(BF)
-
-    recv_specs = [
-        pl.BlockSpec((bands, row_block, (hi - lo) * LANE), lambda g, *_: (0, g, 0))
-        for lo, hi in chunks
-    ]
+                out[0, :, 2 * per : 2 * per + GROUP] = kept.astype(BF)
+
     return pl.pallas_call(
         body,
         name="forward",
         grid_spec=pltpu.PrefetchScalarGridSpec(
-            num_scalar_prefetch=1,
+            num_scalar_prefetch=2,
             grid=(groups,),
-            in_specs=recv_specs
+            in_specs=[pl.BlockSpec(block.shape, lambda g, *_: (0, 0)) for block in shares]
             + [
-                pl.BlockSpec((row_total, GROUP, half_lat), lambda g, *_: (0, g, 0)),
+                pl.BlockSpec((row_total, GROUP, half_lat), lambda g, *_: (0, first + g, 0)),
                 pl.BlockSpec((1, half_lat), lambda g, *_: (0, 0)),
             ],
-            out_specs=pl.BlockSpec((lev, 1, 8, piece + LANE), lambda g, *_: (0, g, 0, 0)),
-            scratch_shapes=[pltpu.VMEM((2, rows, half_lat), BF)],
+            out_specs=pl.BlockSpec((1, 8, 2 * per + LANE), lambda g, *_: (g, 0, 0)),
+            scratch_shapes=[pltpu.VMEM((2, rows, half_lat), BF)]
+            + [pltpu.VMEM((bands, row_block, (hi - lo) * LANE), F32) for lo, hi in chunks],
         ),
-        out_shape=jax.ShapeDtypeStruct((lev, groups, 8, piece + LANE), BF),
-    )(pairs, *received, table, quadrature[None, :])
+        out_shape=jax.ShapeDtypeStruct((groups, 8, 2 * per + LANE), BF),
+    )(pairs, here, *shares, table, quadrature[None, :])
 
 
 def mix_matrix(operator, own):
@@ -236,67 +301,48 @@
     return jnp.where(rest[:, None] == rest[None, :], spread, 0.0).astype(BF), level
 
 
-def implicit_call(pairs, position, received, project, rebuild, factors, wave_count):
-    lev, groups, eight, lanes = received.shape
+def inverse_call(pairs, place, gathered, project, rebuild, factors, table, first, before):
+    row_total, slots, half_lat = table.shape
+    wave_count = row_total - 1
+    lev = len(gathered)
+    groups, eight, lanes = gathered[0].shape
     n = lev * eight
-    piece = lanes - LANE
-
-    def body(pairs_ref, pos_ref, x_ref, p_ref, r_ref, f_ref, out):
-        group = pl.program_id(0)
-        place = pos_ref[0]
-        par = place // (lev // 2)
-        half = place % (lev // 2) * (piece // GROUP)
+    per = wave_count // 2 * GROUP
+    rows = 2 * GROUP * eight
+    own = eight // 4
+
+    def body(pairs_ref, place_ref, *refs):
+        got = refs[:lev]
+        p_ref, r_ref, f_ref, table_ref = refs[lev : lev + 4]
+        out, stack, x_ref = refs[-3:]
+        group = pl.program_id(0) + first
+        for d in range(lev):
+            stack[jnp.bitwise_xor(place_ref[0], d)] = got[d][0].astype(F32)
         lane = lax.broadcasted_iota(jnp.int32, (1, lanes), 1)
-        r = 2 * (lane // GROUP + half) + par
+        place = lane // GROUP
+        half = wave_count // 2
+        r = jnp.where(
+            place < half, 2 * place, jnp.where(place < 2 * half, 2 * (place - half) + 1, wave_count)
+        )
         low = by_slot(lane % GROUP, pairs_ref, group)
         degree = jnp.where(r >= wave_count - low, r - 1, low + r).astype(F32)
         factor = degree * (degree + 1.0) / float(wave_count * wave_count)
         damping = 1.0 / (1.0 + factor * f_ref[:, 0:1])
-        values = x_ref[...].reshape(n, lanes)
+        values = stack[...].reshape(n, lanes).astype(BF)
         modes = jnp.dot(p_ref[...], values, preferred_element_type=F32)
         damped = (modes * damping).astype(BF)
-        result = jnp.dot(r_ref[...], damped, preferred_element_type=F32)
-        out[...] = result.astype(BF).reshape(lev, 1, eight, lanes)
-
-    block = pl.BlockSpec((lev, 1, eight, lanes), lambda g, *_: (0, g, 0, 0))
-    small = pl.BlockSpec((n, n), lambda g, *_: (0, 0))
-    return pl.pallas_call(
-        body,
-        name="implicit",
-        grid_spec=pltpu.PrefetchScalarGridSpec(
-            num_scalar_prefetch=2,
-            grid=(groups,),
-            in_specs=[block, small, small, pl.BlockSpec((n, LANE), lambda g, *_: (0, 0))],
-            out_specs=block,
-        ),
-        out_shape=jax.ShapeDtypeStruct(received.shape, BF),
-    )(pairs, position, received, project, rebuild, factors)
-
-
-def inverse_call(pairs, implicit, table):
-    row_total, slots, half_lat = table.shape
-    wave_count = row_total - 1
-    lev, groups, eight, lanes = implicit.shape
-    piece = lanes - LANE
-    per = wave_count // 2 * GROUP
-    rows = 2 * GROUP * eight
-    own = eight // 4
-
-    def body(pairs_ref, x_ref, table_ref, out):
-        group = pl.program_id(0)
+        x_ref[...] = jnp.dot(r_ref[...], damped, preferred_element_type=F32).astype(BF)
         whole = table_ref[0:wave_count].reshape(wave_count // 2, 2, GROUP, half_lat)
         sums = []
         for par in range(2):
-            value = jnp.concatenate(
-                [x_ref[par * (lev // 2) + h, 0, :, 0:piece] for h in range(lev // 2)], axis=1
-            ).astype(F32)
+            value = x_ref[:, par * per : (par + 1) * per].astype(F32)
             code = part_code(pairs_ref, group, wave_count, 0, par, per)
             spread = jnp.concatenate(
                 [jnp.where(code == b, value, 0.0) for b in range(2 * GROUP)], axis=0
             ).astype(BF)
             matrix = whole[:, par].reshape(per, half_lat)
             sums.append(jnp.dot(spread, matrix, preferred_element_type=F32))
-        tail = x_ref[lev // 2 - 1, 0, :, piece : piece + GROUP].astype(F32)
+        tail = x_ref[:, 2 * per : 2 * per + GROUP].astype(F32)
         lane8 = lax.broadcasted_iota(jnp.int32, (1, GROUP), 1)
         nothing = jnp.zeros((eight, GROUP), F32)
         spread = jnp.concatenate(
@@ -331,64 +377,95 @@
                         )
                     ] = south[at]
 
+    more = () if before is None else (before,)
     return pl.pallas_call(
         body,
         name="inverse",
         grid_spec=pltpu.PrefetchScalarGridSpec(
-            num_scalar_prefetch=1,
+            num_scalar_prefetch=2,
             grid=(groups,),
-            in_specs=[
-                pl.BlockSpec((lev, 1, eight, lanes), lambda g, *_: (0, g, 0, 0)),
-                pl.BlockSpec((row_total, GROUP, half_lat), lambda g, *_: (0, g, 0)),
+            in_specs=[pl.BlockSpec((1, eight, lanes), lambda g, *_: (g, 0, 0))] * lev
+            + [
+                pl.BlockSpec((n, n), lambda g, *_: (0, 0)),
+                pl.BlockSpec((eight, n), lambda g, p, q: (q[0], 0)),
+                pl.BlockSpec((n, LANE), lambda g, *_: (0, 0)),
+                pl.BlockSpec((row_total, GROUP, half_lat), lambda g, *_: (0, first + g, 0)),
+            ]
+            + [pl.BlockSpec(memory_space=pl.ANY)] * len(more),
+            out_specs=pl.BlockSpec(
+                (2, own, GROUP, 2, 2, 2 * half_lat), lambda g, *_: (0, 0, first + g, 0, 0, 0)
+            ),
+            scratch_shapes=[
+                pltpu.VMEM((lev, eight, lanes), F32),
+                pltpu.VMEM((eight, lanes), BF),
             ],
-            out_specs=pl.BlockSpec(
-                (2, own, GROUP, 2, 2, 2 * half_lat), lambda g, *_: (0, 0, g, 0, 0, 0)
-            ),
         ),
         out_shape=jax.ShapeDtypeStruct((2, own, slots, 2, 2, 2 * half_lat), F32),
-    )(pairs, implicit, table)
-
-
-def exchange(x, axis):
-    return lax.all_to_all(x, axis, 0, 0, tiled=True)
+        input_output_aliases={lev + 6: 0} if more else {},
+    )(pairs, place, *gathered, project, rebuild, factors, table, *more)
+
+
+def swap(blocks, axis):
+    count = len(blocks)
+    return [blocks[0]] + [
+        lax.ppermute(blocks[d], axis, [(i, i ^ d) for i in range(count)]) for d in range(1, count)
+    ]
 
 
 def tiled_local(u, v, t, operator, quadrature, table, couples, project, rebuild, factors):
     lev, lat = lax.axis_size("lev"), lax.axis_size("lat")
-    levels, band, lons = u.shape
+    levels, _, lons = u.shape
     own = levels // lev
     slots, row_total, _ = table.shape
     wave_count = row_total - 1
+    place = lax.axis_index("lev").astype(jnp.int32)[None]
+    here = lax.axis_index("lat").astype(jnp.int32)[None]
     pairs = lax.dynamic_slice_in_dim(couples, lax.axis_index("lat") * slots, slots)
     flat = jnp.transpose(table, (1, 0, 2))
-    waves = wave_rows_call(couples, lons * lev, wave_count)
     received = []
+    after = (u, v, t)
+    waves = None
     for lo, hi in CHUNKS:
-        products = products_call(u, v, t, operator, lev, lo, hi - lo)
-        products = exchange(products, "lev")
-        pieces = products.reshape(lev, (hi - lo) * LANE, lons)
-        fourier = fourier_call(waves, pieces)
-        received.append(exchange(fourier.reshape(lat, slots * 4, -1), "lat"))
-    spectral = exchange(forward_call(pairs, received, CHUNKS, flat, quadrature, lev), "lev")
+        blocks = products_call(place, *after, operator, lev, lo, hi - lo)
+        if waves is None:
+            couples, blocks = lax.optimization_barrier((couples, blocks))
+            waves = wave_rows_call(couples, lons * lev, wave_count)
+            after = lax.optimization_barrier((u, v, t, waves))
+            after, waves = after[:3], after[3]
+        blocks = swap(blocks, "lev")
+        pieces = [x.reshape((hi - lo) * LANE, lons) for x in blocks]
+        blocks = fourier_call(place, here, waves, pieces, lat)
+        received.append(swap(blocks, "lat"))
     to_modes, level = mix_matrix(project, own)
     to_levels, _ = mix_matrix(rebuild, own)
     factor_rows = jnp.broadcast_to(factors[level][:, None], (level.shape[0], LANE))
-    position = lax.axis_index("lev").astype(jnp.int32)[None]
-    implicit = implicit_call(
-        pairs, position, spectral, to_modes, to_levels, factor_rows, wave_count
-    )
-    return inverse_call(pairs, exchange(implicit, "lev"), flat)
-
-
-def fits(lev, band, lons, levels, slots, row_total, half_lat):
+    groups = slots // GROUP
+    cut = -(-groups * CUT[0] // CUT[1])
+    parts = ((0, cut), (cut, groups - cut))
+    gathered = []
+    for first, count in parts:
+        block = forward_call(pairs, here, received, CHUNKS, flat, quadrature, first, count)
+        gathered.append(swap([block] * lev, "lev"))
+    result = None
+    for (first, _), blocks in zip(parts, gathered):
+        result = inverse_call(
+            pairs, place, blocks, to_modes, to_levels, factor_rows, flat, first, result
+        )
+    return result
+
+
+def fits(lev, lat, band, lons, levels, slots, row_total, half_lat):
     return (
         lev % 2 == 0
+        and lev & (lev - 1) == 0
+        and lat & (lat - 1) == 0
+        and lons * lev % 8 == 0
         and levels == 2 * lev
         and band == CHUNKS[-1][1] * SUB
         and lons % LANE == 0
         and slots % GROUP == 0
         and row_total % 2 == 1
-        and (row_total - 1) * GROUP % (lev * LANE) == 0
+        and (row_total - 1) * GROUP % (2 * LANE) == 0
         and half_lat % LANE == 0
     )
 
@@ -558,6 +635,7 @@
     sizes = args[0].shape
     if fits(
         lax.axis_size("lev"),
+        lax.axis_size("lat"),
         sizes[1],
         sizes[2],
         sizes[0],

time: 183 us -> 175 us (0.956)
  blocking collectives: 11.1 us -> 0 us
  starting transfers between devices: 21.5 us -> 31.8 us
  other arithmetic: 5.8 us -> 0.03 us
    all_to_all x5 -> x0, waiting for transfers between devices: 50.4 us -> none  [exchange(): return lax.all_to_all(x, axis, 0, 0, tiled=True)]
    ppermute x0 -> x26, waiting for transfers between devices: none -> 49.8 us  [swap(): lax.ppermute(blocks[d], axis, [(i, i ^ d) for i in range(count)])]
    ppermute x0 -> x26, starting transfers between devices: none -> 31.8 us  [swap(): lax.ppermute(blocks[d], axis, [(i, i ^ d) for i in range(count)])]
    all_to_all x5 -> x0, starting transfers between devices: 21.5 us -> none  [exchange(): return lax.all_to_all(x, axis, 0, 0, tiled=True)]
    pallas_call x6 -> x5, Pallas kernels: 47.8 us -> 32.3 us  [the longest x2 14.6 us: fourier_call(): pl.pallas_call(body, name='fourier', grid_spec=pltpu.PrefetchScalarGridSp...]
    all_to_all x1 -> x0, blocking collectives: 11.1 us -> none  [exchange(): return lax.all_to_all(x, axis, 0, 0, tiled=True)]
    pallas_call x1 -> x2, Pallas kernels: 19.4 us -> 28.9 us  [forward_call(): pl.pallas_call(body, name='forward', grid_spec=pltpu.PrefetchScalarGridSp...]
    pallas_call x1 -> x2, Pallas kernels: 15.6 us -> 20.1 us  [inverse_call(): pl.pallas_call(body, name='inverse', grid_spec=pltpu.PrefetchScalarGridSp...]
  transfers between devices with their start and end apart: 5 -> 26, of which waited for: 4 -> 4; matrix products, arithmetic and copies ran while one was open for 6% -> 3% of each run, Pallas kernels for 22% -> 31%
where the time goes in v2:
time: 175 us; the launch traced here: 172 us
  Pallas kernels  81.3 us (46%)
  waiting for transfers between devices  49.8 us (28%)
  starting transfers between devices  31.8 us (18%)
  local copies, waits for them, and re-layouts  7.1 us (4%)
  matrix products  1.8 us (1%)
    ppermute x26, waiting for transfers between devices, swap(): lax.ppermute(blocks[d], axis, [(i, i ^ d) for i in range(count)])  49.8 us
    ppermute x26, starting transfers between devices, swap(): lax.ppermute(blocks[d], axis, [(i, i ^ d) for i in range(count)])  31.8 us
    pallas_call x2, Pallas kernels, forward_call(): pl.pallas_call(body, name='forward', grid_spec=pltpu.PrefetchScalarGridSp...  28.9 us
    pallas_call x2, Pallas kernels, inverse_call(): pl.pallas_call(body, name='inverse', grid_spec=pltpu.PrefetchScalarGridSp...  20.1 us
    pallas_call x2, Pallas kernels, fourier_call(): pl.pallas_call(body, name='fourier', grid_spec=pltpu.PrefetchScalarGridSp...  14.6 us
    pallas_call x1, Pallas kernels, wave_rows_call(): pl.pallas_call(body, name='wave_rows', grid_spec=pltpu.PrefetchScalarGrid...  9.75 us
    pallas_call x2, Pallas kernels, products_call(): pl.pallas_call(body, name='products', grid_spec=pltpu.PrefetchScalarGridS...  7.93 us
    unnamed x70, local copies, waits for them, and re-layouts  3.71 us
  transfers between devices with their start and end apart: 26, of which 4 were waited for; matrix products, arithmetic and copies ran while one was open for 3% of the time, Pallas kernels for 31%

profile of v2, /device:TPU:0, one launch (start us, length us, event | category | flops | bytes accessed | tf_op | source)
XLA Modules:
  0.0 172.0 jit_solution(12653581885790780844)
XLA Ops:
  0.0 3.3 %products.2 = (bf16[2,4,32,640]{3,2,1,0:T(8,128)(2,1)}, bf16[2,4,32,640]{3,2,1,0:T(8,128)(2,1)}, bf16[2,4,32,640]{3,2,1,0:T(8,128)(2,1)}, bf16[2,4,32,640]{3,2,1,0:T(8,128)(2,1)}) custom-call(s32[1]{0:T(128)} %bitcast.place_ref, bf16[8,8]{1,0:T(8,128)(2,1)} %op_ref.3, bf16[8,160,640]{2,1,0:T(8,128)(2,1)} %u_ref.2, bf16[8,160,640]{2,1,0:T(8,128)(2,1)} %v_ref.2, ...), custom_call_target="tpu_custom_call" | custom-call | tf_op jit(solution)/shard_map/products/pallas_call | solution.py:52
  3.3 3.0 %collective-permute-start = (bf16[2,4,32,640]{3,2,1,0:T(8,128)(2,1)}, bf16[2,4,32,640]{3,2,1,0:T(8,128)(2,1)S(1)}, u32[]{:S(2)}, u32[]{:S(2)}) collective-permute-start(bf16[2,4,32,640]{3,2,1,0:T(8,128)(2,1)} %get-tuple-element.45), channel_id=1, source_target_pairs={{0,8},{8,0},{16,24},{24,16},{1,9},{9,1},{17,25},{25,17},{2,10},{10... | collective-permute-start | bytes 983048 | tf_op jit(solution)/shard_map/ppermute | solution.py:411
  6.3 9.7 %wave_rows.1.w_ref = bf16[1280,2560]{1,0:T(8,128)(2,1)} custom-call(s32[320]{0:T(512)} %couples_ref), custom_call_target="tpu_custom_call" | custom-call | tf_op jit(solution)/shard_map/wave_rows/pallas_call | solution.py:119
  16.0 4.6 %products.3 = (bf16[3,4,32,640]{3,2,1,0:T(8,128)(2,1)}, bf16[3,4,32,640]{3,2,1,0:T(8,128)(2,1)}, bf16[3,4,32,640]{3,2,1,0:T(8,128)(2,1)}, bf16[3,4,32,640]{3,2,1,0:T(8,128)(2,1)}) custom-call(s32[1]{0:T(128)} %bitcast.place_ref, bf16[8,8]{1,0:T(8,128)(2,1)} %op_ref.3, bf16[8,160,640]{2,1,0:T(8,128)(2,1)} %u_ref.2, bf16[8,160,640]{2,1,0:T(8,128)(2,1)} %v_ref.2, ...), custom_call_target="tpu_custom_call" | custom-call | tf_op jit(solution)/shard_map/products/pallas_call | solution.py:52
  20.7 2.0 %collective-permute-start.11 = (bf16[3,4,32,640]{3,2,1,0:T(8,128)(2,1)}, bf16[3,4,32,640]{3,2,1,0:T(8,128)(2,1)S(1)}, u32[]{:S(2)}, u32[]{:S(2)}) collective-permute-start(bf16[3,4,32,640]{3,2,1,0:T(8,128)(2,1)} %get-tuple-element.61), channel_id=1, source_target_pairs={{0,16},{8,24},{16,0},{24,8},{1,17},{9,25},{17,1},{25,9},{2,18},{10... | collective-permute-start | bytes 1474568 | tf_op jit(solution)/shard_map/ppermute | solution.py:411
  24.1 1.5 collective-permute-start.1
  25.8 32.4 %collective-permute-done.1 = bf16[2,4,32,640]{3,2,1,0:T(8,128)(2,1)S(1)} collective-permute-done((bf16[2,4,32,640]{3,2,1,0:T(8,128)(2,1)S(1)}, bf16[2,4,32,640]{3,2,1,0:T(8,128)(2,1)S(1)}, u32[]{:S(2)}, u32[]{:S(2)}) %collective-permute-start.1) | collective-permute-done | bytes 327712 | tf_op jit(solution)/shard_map/ppermute | solution.py:411
  59.0 6.5 %fourier.2 = (bf16[160,256]{1,0:T(8,128)(2,1)}, bf16[160,256]{1,0:T(8,128)(2,1)}, bf16[160,256]{1,0:T(8,128)(2,1)}, bf16[160,256]{1,0:T(8,128)(2,1)}, bf16[160,2...) custom-call(s32[1]{0:T(128)} %bitcast.place_ref, ...), custom_call_target="tpu_custom_call" | custom-call | tf_op jit(solution)/shard_map/fourier/pallas_call | solution.py:157
  65.6 1.8 %collective-permute-start.4 = (bf16[160,256]{1,0:T(8,128)(2,1)}, bf16[160,256]{1,0:T(8,128)(2,1)S(1)}, u32[]{:S(2)}, u32[]{:S(2)}) collective-permute-start(bf16[160,256]{1,0:T(8,128)(2,1)} %get-tuple-element.50), channel_id=1, source_target_pairs={{0,2},{1,3},{2,0},{3,1},{4,6},{5,7},{6,4},{7,5},{8,10},{9,11},{10,... | collective-permute-start | bytes 245768 | tf_op jit(solution)/shard_map/ppermute | solution.py:411
  67.5 2.7 %collective-permute-start.6 = (bf16[160,256]{1,0:T(8,128)(2,1)}, bf16[160,256]{1,0:T(8,128)(2,1)S(1)}, u32[]{:S(2)}, u32[]{:S(2)}) collective-permute-start(bf16[160,256]{1,0:T(8,128)(2,1)} %get-tuple-element.52), channel_id=1, source_target_pairs={{0,4},{1,5},{2,6},{3,7},{4,0},{5,1},{6,2},{7,3},{8,12},{9,13},{10,... | collective-permute-start | bytes 245768 | tf_op jit(solution)/shard_map/ppermute | solution.py:411
  71.0 8.1 %fourier.3 = (bf16[160,384]{1,0:T(8,128)(2,1)}, bf16[160,384]{1,0:T(8,128)(2,1)}, bf16[160,384]{1,0:T(8,128)(2,1)}, bf16[160,384]{1,0:T(8,128)(2,1)}, bf16[160,3...) custom-call(s32[1]{0:T(128)} %bitcast.place_ref, ...), custom_call_target="tpu_custom_call" | custom-call | tf_op jit(solution)/shard_map/fourier/pallas_call | solution.py:157
  79.2 1.6 collective-permute-start.14
  80.9 2.5 %collective-permute-start.8 = (bf16[160,256]{1,0:T(8,128)(2,1)S(1)}, bf16[160,256]{1,0:T(8,128)(2,1)S(1)}, u32[]{:S(2)}, u32[]{:S(2)}) collective-permute-start(bf16[160,256]{1,0:T(8,128)(2,1)S(1)} %copy-done.32), channel_id=1, source_target_pairs={{0,6},{1,7},{2,4},{3,5},{4,2},{5,3},{6,0},{7,1},{8,14},{9,15},{10,... | collective-permute-start | bytes 245768 | tf_op jit(solution)/shard_map/ppermute | solution.py:411
  84.7 6.8 %collective-permute-done.7.refs_5_ = bf16[160,256]{1,0:T(8,128)(2,1)S(1)} collective-permute-done((bf16[160,256]{1,0:T(8,128)(2,1)S(1)}, bf16[160,256]{1,0:T(8,128)(2,1)S(1)}, u32[]{:S(2)}, u32[]{:S(2)}) %collective-permute-start.7) | collective-permute-done | bytes 81952 | tf_op jit(solution)/shard_map/ppermute | solution.py:411
  91.5 2.5 %collective-permute-start.16 = (bf16[160,384]{1,0:T(8,128)(2,1)}, bf16[160,384]{1,0:T(8,128)(2,1)S(1)}, u32[]{:S(2)}, u32[]{:S(2)}) collective-permute-start(bf16[160,384]{1,0:T(8,128)(2,1)} %get-tuple-element.67), channel_id=1, source_target_pairs={{0,4},{1,5},{2,6},{3,7},{4,0},{5,1},{6,2},{7,3},{8,12},{9,13},{10,... | collective-permute-start | bytes 368648 | tf_op jit(solution)/shard_map/ppermute | solution.py:411
  95.0 2.8 %collective-permute-start.18 = (bf16[160,384]{1,0:T(8,128)(2,1)}, bf16[160,384]{1,0:T(8,128)(2,1)S(1)}, u32[]{:S(2)}, u32[]{:S(2)}) collective-permute-start(bf16[160,384]{1,0:T(8,128)(2,1)} %get-tuple-element.69), channel_id=1, source_target_pairs={{0,6},{1,7},{2,4},{3,5},{4,2},{5,3},{6,0},{7,1},{8,14},{9,15},{10,... | collective-permute-start | bytes 368648 | tf_op jit(solution)/shard_map/ppermute | solution.py:411
  100.0 9.5 %collective-permute-done.16.refs_12_ = bf16[160,384]{1,0:T(8,128)(2,1)S(1)} collective-permute-done((bf16[160,384]{1,0:T(8,128)(2,1)}, bf16[160,384]{1,0:T(8,128)(2,1)S(1)}, u32[]{:S(2)}, u32[]{:S(2)}) %collective-permute-start.16) | collective-permute-done | bytes 122912 | tf_op jit(solution)/shard_map/ppermute | solution.py:411
  111.2 16.5 %forward.3.refs_0_ = bf16[3,8,5248]{2,1,0:T(8,128)(2,1)} custom-call(s32[40]{0:T(128)} %dynamic_slice.3.pairs_ref, s32[1]{0:T(128)} %bitcast.1.here_ref, bf16[160,256]{1,0:T(8,128)(2,1)} %get-tuple-element.48.refs_0_, bf16[160,256]{1,0:T(8,128)(2,1)} %copy-done.12, bf16[160,256]{1,0:T(8,128)(2,1)} %copy-done.13, bf16[160,256]{1,0:T(8,128)(2,1)} %copy-done.14, ...), custom_call_target="tpu_custom_call" | custom-call | tf_op jit(solution)/shard_map/forward/pallas_call | solution.py:273
  127.7 1.5 collective-permute-start.23
  130.1 1.6 collective-permute-start.24
  132.9 12.4 %forward.2.refs_0_ = bf16[2,8,5248]{2,1,0:T(8,128)(2,1)} custom-call(s32[40]{0:T(128)} %dynamic_slice.3.pairs_ref, s32[1]{0:T(128)} %bitcast.1.here_ref, bf16[160,256]{1,0:T(8,128)(2,1)} %get-tuple-element.48.refs_0_, bf16[160,256]{1,0:T(8,128)(2,1)} %copy-done.12, bf16[160,256]{1,0:T(8,128)(2,1)} %copy-done.13, bf16[160,256]{1,0:T(8,128)(2,1)} %copy-done.14, ...), custom_call_target="tpu_custom_call" | custom-call | tf_op jit(solution)/shard_map/forward/pallas_call | solution.py:273
  146.8 1.5 collective-permute-start.21
  150.5 11.7 %inverse.2.refs_8_ = f32[2,2,40,2,2,1280]{5,4,3,2,1,0:T(2,128)} custom-call(s32[40]{0:T(128)} %dynamic_slice.3.pairs_ref, s32[1]{0:T(128)} %bitcast.place_ref, bf16[3,8,5248]{2,1,0:T(8,128)(2,1)} %forward.3.refs_0_, bf16[3,8,5248]{2,1,0:T(8,128)(2,1)} %copy-done.22, bf16[3,8,5248]{2,1,0:T(8,128)(2,1)} %copy-done.23, bf16[3,8,5248]{2,1,0:T(8,128)(2,1)} %copy-done.24, ...), custom_call_target="tpu_custom_call" | custom-call | tf_op jit(solution)/shard_map/inverse/pallas_call | solution.py:381
  163.6 8.4 %inverse.3 = f32[2,2,40,2,2,1280]{5,4,3,2,1,0:T(2,128)} custom-call(s32[40]{0:T(128)} %dynamic_slice.3.pairs_ref, s32[1]{0:T(128)} %bitcast.place_ref, bf16[2,8,5248]{2,1,0:T(8,128)(2,1)} %forward.2.refs_0_, bf16[2,8,5248]{2,1,0:T(8,128)(2,1)} %copy-done.25, bf16[2,8,5248]{2,1,0:T(8,128)(2,1)} %copy-done.26, ...), custom_call_target="tpu_custom_call", output_to_operand_aliasing={{}: (10, {})} | custom-call | tf_op jit(solution)/shard_map/inverse/pallas_call | solution.py:381
  (116 shorter events, 16.6 us)
Async XLA Ops:
  3.3 22.4 %collective-permute-start = (bf16[2,4,32,640]{3,2,1,0:T(8,128)(2,1)}, bf16[2,4,32,640]{3,2,1,0:T(8,128)(2,1)S(1)}, u32[]{:S(2)}, u32[]{:S(2)}) collective-permute-start(bf16[2,4,32,640]{3,2,1,0:T(8,128)(2,1)} %get-tuple-element.45), channel_id=1, source_target_pairs={{0,8},{8,0},{16,24},{24,16},{1,9},{9,1},{17,25},{25,17},{2,10},{10... | collective-permute-start | bytes 983048 | tf_op jit(solution)/shard_map/ppermute | solution.py:411
  20.7 46.7 %collective-permute-start.10 = (bf16[3,4,32,640]{3,2,1,0:T(8,128)(2,1)}, bf16[3,4,32,640]{3,2,1,0:T(8,128)(2,1)S(1)}, u32[]{:S(2)}, u32[]{:S(2)}) collective-permute-start(bf16[3,4,32,640]{3,2,1,0:T(8,128)(2,1)} %get-tuple-element.60), channel_id=1, source_target_pairs={{0,8},{8,0},{16,24},{24,16},{1,9},{9,1},{17,25},{25,17},{2,10},{10... | collective-permute-start | bytes 1474568 | tf_op jit(solution)/shard_map/ppermute | solution.py:411
  20.7 46.8 %collective-permute-start.11 = (bf16[3,4,32,640]{3,2,1,0:T(8,128)(2,1)}, bf16[3,4,32,640]{3,2,1,0:T(8,128)(2,1)S(1)}, u32[]{:S(2)}, u32[]{:S(2)}) collective-permute-start(bf16[3,4,32,640]{3,2,1,0:T(8,128)(2,1)} %get-tuple-element.61), channel_id=1, source_target_pairs={{0,16},{8,24},{16,0},{24,8},{1,17},{9,25},{17,1},{25,9},{2,18},{10... | collective-permute-start | bytes 1474568 | tf_op jit(solution)/shard_map/ppermute | solution.py:411
  22.7 47.5 %collective-permute-start.12 = (bf16[3,4,32,640]{3,2,1,0:T(8,128)(2,1)}, bf16[3,4,32,640]{3,2,1,0:T(8,128)(2,1)S(1)}, u32[]{:S(2)}, u32[]{:S(2)}) collective-permute-start(bf16[3,4,32,640]{3,2,1,0:T(8,128)(2,1)} %get-tuple-element.62), channel_id=1, source_target_pairs={{0,24},{8,16},{16,8},{24,0},{1,25},{9,17},{17,9},{25,1},{2,26},{10... | collective-permute-start | bytes 1474568 | tf_op jit(solution)/shard_map/ppermute | solution.py:411
  24.1 34.0 %collective-permute-start.1 = (bf16[2,4,32,640]{3,2,1,0:T(8,128)(2,1)S(1)}, bf16[2,4,32,640]{3,2,1,0:T(8,128)(2,1)S(1)}, u32[]{:S(2)}, u32[]{:S(2)}) collective-permute-start(bf16[2,4,32,640]{3,2,1,0:T(8,128)(2,1)S(1)} %copy-done.30), channel_id=1, source_target_pairs={{0,16},{8,24},{16,0},{24,8},{1,17},{9,25},{17,1},{25,9},{2,18},{10... | collective-permute-start | bytes 983048 | tf_op jit(solution)/shard_map/ppermute | solution.py:411
  25.7 32.5 %collective-permute-start.2 = (bf16[2,4,32,640]{3,2,1,0:T(8,128)(2,1)S(1)}, bf16[2,4,32,640]{3,2,1,0:T(8,128)(2,1)S(1)}, u32[]{:S(2)}, u32[]{:S(2)}) collective-permute-start(bf16[2,4,32,640]{3,2,1,0:T(8,128)(2,1)S(1)} %copy-done.29), channel_id=1, source_target_pairs={{0,24},{8,16},{16,8},{24,0},{1,25},{9,17},{17,9},{25,1},{2,26},{10... | collective-permute-start | bytes 983048 | tf_op jit(solution)/shard_map/ppermute | solution.py:411
  65.6 13.6 %collective-permute-start.3 = (bf16[160,256]{1,0:T(8,128)(2,1)}, bf16[160,256]{1,0:T(8,128)(2,1)S(1)}, u32[]{:S(2)}, u32[]{:S(2)}) collective-permute-start(bf16[160,256]{1,0:T(8,128)(2,1)} %get-tuple-element.49), channel_id=1, source_target_pairs={{0,1},{1,0},{2,3},{3,2},{4,5},{5,4},{6,7},{7,6},{8,9},{9,8},{10,11... | collective-permute-start | bytes 245768 | tf_op jit(solution)/shard_map/ppermute | solution.py:411
  65.6 15.2 %collective-permute-start.4 = (bf16[160,256]{1,0:T(8,128)(2,1)}, bf16[160,256]{1,0:T(8,128)(2,1)S(1)}, u32[]{:S(2)}, u32[]{:S(2)}) collective-permute-start(bf16[160,256]{1,0:T(8,128)(2,1)} %get-tuple-element.50), channel_id=1, source_target_pairs={{0,2},{1,3},{2,0},{3,1},{4,6},{5,7},{6,4},{7,5},{8,10},{9,11},{10,... | collective-permute-start | bytes 245768 | tf_op jit(solution)/shard_map/ppermute | solution.py:411
  67.4 13.5 %collective-permute-start.5 = (bf16[160,256]{1,0:T(8,128)(2,1)}, bf16[160,256]{1,0:T(8,128)(2,1)S(1)}, u32[]{:S(2)}, u32[]{:S(2)}) collective-permute-start(bf16[160,256]{1,0:T(8,128)(2,1)} %get-tuple-element.51), channel_id=1, source_target_pairs={{0,3},{1,2},{2,1},{3,0},{4,7},{5,6},{6,5},{7,4},{8,11},{9,10},{10,... | collective-permute-start | bytes 245768 | tf_op jit(solution)/shard_map/ppermute | solution.py:411
  67.5 15.9 %collective-permute-start.6 = (bf16[160,256]{1,0:T(8,128)(2,1)}, bf16[160,256]{1,0:T(8,128)(2,1)S(1)}, u32[]{:S(2)}, u32[]{:S(2)}) collective-permute-start(bf16[160,256]{1,0:T(8,128)(2,1)} %get-tuple-element.52), channel_id=1, source_target_pairs={{0,4},{1,5},{2,6},{3,7},{4,0},{5,1},{6,2},{7,3},{8,12},{9,13},{10,... | collective-permute-start | bytes 245768 | tf_op jit(solution)/shard_map/ppermute | solution.py:411
  79.1 15.9 %collective-permute-start.13 = (bf16[160,384]{1,0:T(8,128)(2,1)}, bf16[160,384]{1,0:T(8,128)(2,1)S(1)}, u32[]{:S(2)}, u32[]{:S(2)}) collective-permute-start(bf16[160,384]{1,0:T(8,128)(2,1)} %get-tuple-element.64), channel_id=1, source_target_pairs={{0,1},{1,0},{2,3},{3,2},{4,5},{5,4},{6,7},{7,6},{8,9},{9,8},{10,11... | collective-permute-start | bytes 368648 | tf_op jit(solution)/shard_map/ppermute | solution.py:411
  79.2 18.7 %collective-permute-start.14 = (bf16[160,384]{1,0:T(8,128)(2,1)}, bf16[160,384]{1,0:T(8,128)(2,1)S(1)}, u32[]{:S(2)}, u32[]{:S(2)}) collective-permute-start(bf16[160,384]{1,0:T(8,128)(2,1)} %get-tuple-element.65), channel_id=1, source_target_pairs={{0,2},{1,3},{2,0},{3,1},{4,6},{5,7},{6,4},{7,5},{8,10},{9,11},{10,... | collective-permute-start | bytes 368648 | tf_op jit(solution)/shard_map/ppermute | solution.py:411
  80.7 10.8 %collective-permute-start.7 = (bf16[160,256]{1,0:T(8,128)(2,1)S(1)}, bf16[160,256]{1,0:T(8,128)(2,1)S(1)}, u32[]{:S(2)}, u32[]{:S(2)}) collective-permute-start(bf16[160,256]{1,0:T(8,128)(2,1)S(1)} %copy-done.33), channel_id=1, source_target_pairs={{0,5},{1,4},{2,7},{3,6},{4,1},{5,0},{6,3},{7,2},{8,13},{9,12},{10,... | collective-permute-start | bytes 245768 | tf_op jit(solution)/shard_map/ppermute | solution.py:411
  83.4 10.6 %collective-permute-start.9 = (bf16[160,256]{1,0:T(8,128)(2,1)S(1)}, bf16[160,256]{1,0:T(8,128)(2,1)S(1)}, u32[]{:S(2)}, u32[]{:S(2)}) collective-permute-start(bf16[160,256]{1,0:T(8,128)(2,1)S(1)} %copy-done.31), channel_id=1, source_target_pairs={{0,7},{1,6},{2,5},{3,4},{4,3},{5,2},{6,1},{7,0},{8,15},{9,14},{10,... | collective-permute-start | bytes 245768 | tf_op jit(solution)/shard_map/ppermute | solution.py:411
  91.5 17.9 %collective-permute-start.16 = (bf16[160,384]{1,0:T(8,128)(2,1)}, bf16[160,384]{1,0:T(8,128)(2,1)S(1)}, u32[]{:S(2)}, u32[]{:S(2)}) collective-permute-start(bf16[160,384]{1,0:T(8,128)(2,1)} %get-tuple-element.67), channel_id=1, source_target_pairs={{0,4},{1,5},{2,6},{3,7},{4,0},{5,1},{6,2},{7,3},{8,12},{9,13},{10,... | collective-permute-start | bytes 368648 | tf_op jit(solution)/shard_map/ppermute | solution.py:411
  94.1 16.4 %collective-permute-start.17 = (bf16[160,384]{1,0:T(8,128)(2,1)}, bf16[160,384]{1,0:T(8,128)(2,1)S(1)}, u32[]{:S(2)}, u32[]{:S(2)}) collective-permute-start(bf16[160,384]{1,0:T(8,128)(2,1)} %get-tuple-element.68), channel_id=1, source_target_pairs={{0,5},{1,4},{2,7},{3,6},{4,1},{5,0},{6,3},{7,2},{8,13},{9,12},{10,... | collective-permute-start | bytes 368648 | tf_op jit(solution)/shard_map/ppermute | solution.py:411
  95.0 15.4 %collective-permute-start.18 = (bf16[160,384]{1,0:T(8,128)(2,1)}, bf16[160,384]{1,0:T(8,128)(2,1)S(1)}, u32[]{:S(2)}, u32[]{:S(2)}) collective-permute-start(bf16[160,384]{1,0:T(8,128)(2,1)} %get-tuple-element.69), channel_id=1, source_target_pairs={{0,6},{1,7},{2,4},{3,5},{4,2},{5,3},{6,0},{7,1},{8,14},{9,15},{10,... | collective-permute-start | bytes 368648 | tf_op jit(solution)/shard_map/ppermute | solution.py:411
  97.8 12.6 %collective-permute-start.19 = (bf16[160,384]{1,0:T(8,128)(2,1)}, bf16[160,384]{1,0:T(8,128)(2,1)S(1)}, u32[]{:S(2)}, u32[]{:S(2)}) collective-permute-start(bf16[160,384]{1,0:T(8,128)(2,1)} %get-tuple-element.70), channel_id=1, source_target_pairs={{0,7},{1,6},{2,5},{3,4},{4,3},{5,2},{6,1},{7,0},{8,15},{9,14},{10,... | collective-permute-start | bytes 368648 | tf_op jit(solution)/shard_map/ppermute | solution.py:411
  127.7 20.6 %collective-permute-start.23 = (bf16[3,8,5248]{2,1,0:T(8,128)(2,1)}, bf16[3,8,5248]{2,1,0:T(8,128)(2,1)S(1)}, u32[]{:S(2)}, u32[]{:S(2)}) collective-permute-start(bf16[3,8,5248]{2,1,0:T(8,128)(2,1)} %forward.3.refs_0_), channel_id=1, source_target_pairs={{0,8},{8,0},{16,24},{24,16},{1,9},{9,1},{17,25},{25,17},{2,10},{10... | collective-permute-start | bytes 755720 | tf_op jit(solution)/shard_map/ppermute | solution.py:411
  130.1 19.6 %collective-permute-start.24 = (bf16[3,8,5248]{2,1,0:T(8,128)(2,1)}, bf16[3,8,5248]{2,1,0:T(8,128)(2,1)S(1)}, u32[]{:S(2)}, u32[]{:S(2)}) collective-permute-start(bf16[3,8,5248]{2,1,0:T(8,128)(2,1)} %forward.3.refs_0_), channel_id=1, source_target_pairs={{0,16},{8,24},{16,0},{24,8},{1,17},{9,25},{17,1},{25,9},{2,18},{10... | collective-permute-start | bytes 755720 | tf_op jit(solution)/shard_map/ppermute | solution.py:411
  131.7 18.0 %collective-permute-start.25 = (bf16[3,8,5248]{2,1,0:T(8,128)(2,1)}, bf16[3,8,5248]{2,1,0:T(8,128)(2,1)S(1)}, u32[]{:S(2)}, u32[]{:S(2)}) collective-permute-start(bf16[3,8,5248]{2,1,0:T(8,128)(2,1)} %forward.3.refs_0_), channel_id=1, source_target_pairs={{0,24},{8,16},{16,8},{24,0},{1,25},{9,17},{17,9},{25,1},{2,26},{10... | collective-permute-start | bytes 755720 | tf_op jit(solution)/shard_map/ppermute | solution.py:411
  145.3 16.9 %collective-permute-start.20 = (bf16[2,8,5248]{2,1,0:T(8,128)(2,1)}, bf16[2,8,5248]{2,1,0:T(8,128)(2,1)S(1)}, u32[]{:S(2)}, u32[]{:S(2)}) collective-permute-start(bf16[2,8,5248]{2,1,0:T(8,128)(2,1)} %forward.2.refs_0_), channel_id=1, source_target_pairs={{0,8},{8,0},{16,24},{24,16},{1,9},{9,1},{17,25},{25,17},{2,10},{10... | collective-permute-start | bytes 503816 | tf_op jit(solution)/shard_map/ppermute | solution.py:411
  146.8 15.4 %collective-permute-start.21 = (bf16[2,8,5248]{2,1,0:T(8,128)(2,1)}, bf16[2,8,5248]{2,1,0:T(8,128)(2,1)S(1)}, u32[]{:S(2)}, u32[]{:S(2)}) collective-permute-start(bf16[2,8,5248]{2,1,0:T(8,128)(2,1)} %forward.2.refs_0_), channel_id=1, source_target_pairs={{0,16},{8,24},{16,0},{24,8},{1,17},{9,25},{17,1},{25,9},{2,18},{10... | collective-permute-start | bytes 503816 | tf_op jit(solution)/shard_map/ppermute | solution.py:411
  148.3 13.9 %collective-permute-start.22 = (bf16[2,8,5248]{2,1,0:T(8,128)(2,1)}, bf16[2,8,5248]{2,1,0:T(8,128)(2,1)S(1)}, u32[]{:S(2)}, u32[]{:S(2)}) collective-permute-start(bf16[2,8,5248]{2,1,0:T(8,128)(2,1)} %forward.2.refs_0_), channel_id=1, source_target_pairs={{0,24},{8,16},{16,8},{24,0},{1,25},{9,17},{17,9},{25,1},{2,26},{10... | collective-permute-start | bytes 503816 | tf_op jit(solution)/shard_map/ppermute | solution.py:411
  (37 other events, 523.9 us)

commit v3 on v2

--- a/solution.py
+++ b/solution.py
@@ -68,9 +68,14 @@
     )(place, operator, u, v, t)
 
 
+def whole_part(index, period):
+    return ((index.astype(F32) + 0.5) * (1.0 / period)).astype(jnp.int32)
+
+
 def sine_cosine(index, period):
     quarter = period // 4
-    turn = (index + period // 8) // quarter
+    index = index - whole_part(index, period) * period
+    turn = whole_part(index + period // 8, quarter)
     angle = (index - turn * quarter).astype(F32) * (2.0 * math.pi / period)
     square = angle * angle
     sine = 1.0 / 362880
@@ -80,17 +85,17 @@
     cosine = -1.0 / 3628800
     for c in (1.0 / 40320, -1.0 / 720, 1.0 / 24, -0.5, 1.0):
         cosine = cosine * square + c
-    odd = turn % 2 == 1
+    odd = (turn == 1) | (turn == 3)
     first = jnp.where(odd, cosine, sine)
     second = jnp.where(odd, sine, cosine)
-    turn = turn % 4
-    return jnp.where(turn >= 2, -first, first), jnp.where((turn == 1) | (turn == 2), -second, second)
+    minus = (turn == 2) | (turn == 3)
+    return jnp.where(minus, -first, first), jnp.where((turn == 1) | (turn == 2), -second, second)
 
 
 def wave_rows_call(couples, lon_count, wave_count):
     rows = 4 * couples.shape[0]
     block = rows // 4
-    chunk = 16
+    chunk = 32
     scale = 1.0 / math.sqrt(lon_count)
 
     def body(couples_ref, out):
@@ -103,8 +108,8 @@
             for n in range(1, chunk // 4):
                 low = jnp.where(row // 4 == n, couples_ref[base + index * (chunk // 4) + n], low)
             wave = jnp.where(row // 2 % 2 == 0, low, wave_count - 1 - low)
-            sine, cosine = sine_cosine(wave * lane % lon_count, lon_count)
-            s, c = sine_cosine(wave * LANE % lon_count, lon_count)
+            sine, cosine = sine_cosine(wave * lane, lon_count)
+            s, c = sine_cosine(wave * LANE, lon_count)
             is_sine = row % 2 == 1
             a = jnp.where(is_sine, -sine, cosine) * scale
             b = jnp.where(is_sine, cosine, sine) * scale
@@ -178,6 +183,22 @@
     return value
 
 
+def across(tiles, place):
+    tiles = list(tiles)
+    count = len(tiles)
+    step = count // 2
+    while step:
+        shift = step * (LANE // count)
+        upper = place // step % 2 == 1
+        for d in range(count):
+            if d // step % 2 == 0:
+                low, high = tiles[d], tiles[d + step]
+                tiles[d] = jnp.where(upper, pltpu.roll(high, shift, 1), low)
+                tiles[d + step] = jnp.where(upper, high, pltpu.roll(low, LANE - shift, 1))
+        step //= 2
+    return tiles
+
+
 def part_code(pairs, group, wave_count, half, par, lanes):
     lane = lax.broadcasted_iota(jnp.int32, (1, lanes), 1)
     slot = lane % GROUP
@@ -210,9 +231,10 @@
         for number in range(len(chunks)):
             for e in range(bands):
                 band = jnp.bitwise_xor(here_ref[0], e)
-                recv[number][band] = shared[number * bands + e][mine].astype(F32)
+                recv[number][band] = shared[number * bands + e][mine]
         lane = lax.broadcasted_iota(jnp.int32, (row_block, LANE), 1)
-        within, place = lane % SUB, lane // SUB
+        place = lane // SUB
+        turned = place * SUB + SUB - 1 - lane % SUB
         row = lax.broadcasted_iota(jnp.int32, (row_block, LANE), 0)
         low = by_slot(row // 4, pairs_ref, group)
         second = row // 2 % 2
@@ -230,15 +252,11 @@
                 band, unit = beta // units, beta % units
                 north_tiles.append(tile(band, unit))
                 south_tiles.append(tile(bands - 1 - band, units - 1 - unit))
+            north_tiles, south_tiles = across(north_tiles, place), across(south_tiles, place)
             weight = quad_ref[0:1, at]
             for f in range(fields):
-                north = jnp.zeros((row_block, LANE), F32)
-                south = jnp.zeros((row_block, LANE), F32)
-                for d in range(fields):
-                    moved = jnp.take_along_axis(north_tiles[d], f * SUB + within, axis=1)
-                    north = jnp.where(place == d, moved, north)
-                    moved = jnp.take_along_axis(south_tiles[d], f * SUB + SUB - 1 - within, axis=1)
-                    south = jnp.where(place == d, moved, south)
+                north = north_tiles[f].astype(F32)
+                south = jnp.take_along_axis(south_tiles[f].astype(F32), turned, axis=1)
                 for par in range(2):
                     folded = (north + signs[par] * south) * weight
                     spread[par, f * row_block : (f + 1) * row_block, at] = folded.astype(BF)
@@ -283,7 +301,7 @@
             ],
             out_specs=pl.BlockSpec((1, 8, 2 * per + LANE), lambda g, *_: (g, 0, 0)),
             scratch_shapes=[pltpu.VMEM((2, rows, half_lat), BF)]
-            + [pltpu.VMEM((bands, row_block, (hi - lo) * LANE), F32) for lo, hi in chunks],
+            + [pltpu.VMEM((bands, row_block, (hi - lo) * LANE), BF) for lo, hi in chunks],
         ),
         out_shape=jax.ShapeDtypeStruct((groups, 8, 2 * per + LANE), BF),
     )(pairs, here, *shares, table, quadrature[None, :])
@@ -420,25 +438,30 @@
     wave_count = row_total - 1
     place = lax.axis_index("lev").astype(jnp.int32)[None]
     here = lax.axis_index("lat").astype(jnp.int32)[None]
-    pairs = lax.dynamic_slice_in_dim(couples, lax.axis_index("lat") * slots, slots)
     flat = jnp.transpose(table, (1, 0, 2))
     received = []
-    after = (u, v, t)
-    waves = None
+    products = []
     for lo, hi in CHUNKS:
-        blocks = products_call(place, *after, operator, lev, lo, hi - lo)
-        if waves is None:
-            couples, blocks = lax.optimization_barrier((couples, blocks))
-            waves = wave_rows_call(couples, lons * lev, wave_count)
-            after = lax.optimization_barrier((u, v, t, waves))
-            after, waves = after[:3], after[3]
+        products.append(products_call(place, u, v, t, operator, lev, lo, hi - lo))
+    couples, products[-1] = lax.optimization_barrier((couples, products[-1]))
+    waves = wave_rows_call(couples, lons * lev, wave_count)
+    for (lo, hi), blocks in zip(CHUNKS, products):
         blocks = swap(blocks, "lev")
         pieces = [x.reshape((hi - lo) * LANE, lons) for x in blocks]
         blocks = fourier_call(place, here, waves, pieces, lat)
+        if hi == CHUNKS[-1][1]:
+            blocks, late = lax.optimization_barrier(
+                (blocks, (couples, quadrature, project, rebuild, factors))
+            )
         received.append(swap(blocks, "lat"))
+    couples, quadrature, project, rebuild, factors = late
+    pairs = lax.dynamic_slice_in_dim(couples, lax.axis_index("lat") * slots, slots)
     to_modes, level = mix_matrix(project, own)
     to_levels, _ = mix_matrix(rebuild, own)
     factor_rows = jnp.broadcast_to(factors[level][:, None], (level.shape[0], LANE))
+    received, to_modes, to_levels, factor_rows = lax.optimization_barrier(
+        (received, to_modes, to_levels, factor_rows)
+    )
     groups = slots // GROUP
     cut = -(-groups * CUT[0] // CUT[1])
     parts = ((0, cut), (cut, groups - cut))
@@ -460,6 +483,7 @@
         and lev & (lev - 1) == 0
         and lat & (lat - 1) == 0
         and lons * lev % 8 == 0
+        and 2 * (row_total - 1) * LANE < 2**8 * lons * lev
         and levels == 2 * lev
         and band == CHUNKS[-1][1] * SUB
         and lons % LANE == 0

time: 175 us -> 156 us (0.89)
  the two profiles are of different devices: /device:TPU:0 before, /device:TPU:18 now
where the time goes in v3:
time: 156 us; the launch traced here: 155 us
  Pallas kernels  73.1 us (47%)
  waiting for transfers between devices  44.3 us (28%)
  starting transfers between devices  28.8 us (18%)
  local copies, waits for them, and re-layouts  6.93 us (4%)
  matrix products  1.79 us (1%)
    ppermute x26, waiting for transfers between devices, swap(): lax.ppermute(blocks[d], axis, [(i, i ^ d) for i in range(count)])  44.3 us
    ppermute x26, starting transfers between devices, swap(): lax.ppermute(blocks[d], axis, [(i, i ^ d) for i in range(count)])  28.8 us
    pallas_call x2, Pallas kernels, forward_call(): pl.pallas_call(body, name='forward', grid_spec=pltpu.PrefetchScalarGridSp...  23 us
    pallas_call x2, Pallas kernels, inverse_call(): pl.pallas_call(body, name='inverse', grid_spec=pltpu.PrefetchScalarGridSp...  20.1 us
    pallas_call x2, Pallas kernels, fourier_call(): pl.pallas_call(body, name='fourier', grid_spec=pltpu.PrefetchScalarGridSp...  14.6 us
    pallas_call x2, Pallas kernels, products_call(): pl.pallas_call(body, name='products', grid_spec=pltpu.PrefetchScalarGridS...  7.85 us
    pallas_call x1, Pallas kernels, wave_rows_call(): pl.pallas_call(body, name='wave_rows', grid_spec=pltpu.PrefetchScalarGrid...  7.59 us
    unnamed x68, local copies, waits for them, and re-layouts  3.73 us
  transfers between devices with their start and end apart: 26, of which 7 were waited for; matrix products, arithmetic and copies ran while one was open for 3% of the time, Pallas kernels for 31%

profile of v3, /device:TPU:18, one launch (start us, length us, event | category | flops | bytes accessed | tf_op | source)
XLA Modules:
  0.0 155.2 jit_solution(233524876432547816)
XLA Ops:
  0.0 3.3 %products.3 = (bf16[2,4,32,640]{3,2,1,0:T(8,128)(2,1)}, bf16[2,4,32,640]{3,2,1,0:T(8,128)(2,1)}, bf16[2,4,32,640]{3,2,1,0:T(8,128)(2,1)}, bf16[2,4,32,640]{3,2,1,0:T(8,128)(2,1)}) custom-call(s32[1]{0:T(128)} %bitcast.place_ref, bf16[8,8]{1,0:T(8,128)(2,1)} %op_ref.3, bf16[8,160,640]{2,1,0:T(8,128)(2,1)} %u_ref.3, bf16[8,160,640]{2,1,0:T(8,128)(2,1)} %v_ref.3, ...), custom_call_target="tpu_custom_call" | custom-call | tf_op jit(solution)/shard_map/products/pallas_call | solution.py:52
  3.9 4.6 %products.2 = (bf16[3,4,32,640]{3,2,1,0:T(8,128)(2,1)}, bf16[3,4,32,640]{3,2,1,0:T(8,128)(2,1)}, bf16[3,4,32,640]{3,2,1,0:T(8,128)(2,1)}, bf16[3,4,32,640]{3,2,1,0:T(8,128)(2,1)}) custom-call(s32[1]{0:T(128)} %bitcast.place_ref, bf16[8,8]{1,0:T(8,128)(2,1)} %op_ref.3, bf16[8,160,640]{2,1,0:T(8,128)(2,1)} %u_ref.3, bf16[8,160,640]{2,1,0:T(8,128)(2,1)} %v_ref.3, ...), custom_call_target="tpu_custom_call" | custom-call | tf_op jit(solution)/shard_map/products/pallas_call | solution.py:52
  8.5 1.5 collective-permute-start
  10.0 1.5 collective-permute-start.1
  12.0 1.5 collective-permute-start.4
  14.2 1.5 collective-permute-start.5
  15.7 7.6 %wave_rows.1.w_ref = bf16[1280,2560]{1,0:T(8,128)(2,1)} custom-call(s32[320]{0:T(512)} %couples_ref), custom_call_target="tpu_custom_call" | custom-call | tf_op jit(solution)/shard_map/wave_rows/pallas_call | solution.py:124
  23.3 23.9 %collective-permute-done.4 = bf16[2,4,32,640]{3,2,1,0:T(8,128)(2,1)S(1)} collective-permute-done((bf16[2,4,32,640]{3,2,1,0:T(8,128)(2,1)S(1)}, bf16[2,4,32,640]{3,2,1,0:T(8,128)(2,1)S(1)}, u32[]{:S(2)}, u32[]{:S(2)}) %collective-permute-start.4) | collective-permute-done | bytes 327712 | tf_op jit(solution)/shard_map/ppermute | solution.py:429
  48.0 6.5 %fourier.3 = (bf16[160,256]{1,0:T(8,128)(2,1)}, bf16[160,256]{1,0:T(8,128)(2,1)}, bf16[160,256]{1,0:T(8,128)(2,1)}, bf16[160,256]{1,0:T(8,128)(2,1)}, bf16[160,2...) custom-call(s32[1]{0:T(128)} %bitcast.place_ref, ...), custom_call_target="tpu_custom_call" | custom-call | tf_op jit(solution)/shard_map/fourier/pallas_call | solution.py:162
  54.5 1.6 %collective-permute-start.7 = (bf16[160,256]{1,0:T(8,128)(2,1)}, bf16[160,256]{1,0:T(8,128)(2,1)S(1)}, u32[]{:S(2)}, u32[]{:S(2)}) collective-permute-start(bf16[160,256]{1,0:T(8,128)(2,1)} %get-tuple-element.90), channel_id=1, source_target_pairs={{0,2},{1,3},{2,0},{3,1},{4,6},{5,7},{6,4},{7,5},{8,10},{9,11},{10,... | collective-permute-start | bytes 245768 | tf_op jit(solution)/shard_map/ppermute | solution.py:429
  56.8 2.3 %collective-permute-start.10 = (bf16[160,256]{1,0:T(8,128)(2,1)}, bf16[160,256]{1,0:T(8,128)(2,1)S(1)}, u32[]{:S(2)}, u32[]{:S(2)}) collective-permute-start(bf16[160,256]{1,0:T(8,128)(2,1)} %get-tuple-element.93), channel_id=1, source_target_pairs={{0,5},{1,4},{2,7},{3,6},{4,1},{5,0},{6,3},{7,2},{8,13},{9,12},{10,... | collective-permute-start | bytes 245768 | tf_op jit(solution)/shard_map/ppermute | solution.py:429
  59.1 8.1 %fourier.2 = (bf16[160,384]{1,0:T(8,128)(2,1)}, bf16[160,384]{1,0:T(8,128)(2,1)}, bf16[160,384]{1,0:T(8,128)(2,1)}, bf16[160,384]{1,0:T(8,128)(2,1)}, bf16[160,3...) custom-call(s32[1]{0:T(128)} %bitcast.place_ref, ...), custom_call_target="tpu_custom_call" | custom-call | tf_op jit(solution)/shard_map/fourier/pallas_call | solution.py:162
  69.5 3.4 %collective-permute-start.14 = (bf16[160,384]{1,0:T(8,128)(2,1)}, bf16[160,384]{1,0:T(8,128)(2,1)S(1)}, u32[]{:S(2)}, u32[]{:S(2)}) collective-permute-start(bf16[160,384]{1,0:T(8,128)(2,1)} %get-tuple-element.98), channel_id=1, source_target_pairs={{0,2},{1,3},{2,0},{3,1},{4,6},{5,7},{6,4},{7,5},{8,10},{9,11},{10,... | collective-permute-start | bytes 368648 | tf_op jit(solution)/shard_map/ppermute | solution.py:429
  77.3 1.5 collective-permute-start.17
  82.2 2.2 %collective-permute-done.16.refs_12_ = bf16[160,384]{1,0:T(8,128)(2,1)S(1)} collective-permute-done((bf16[160,384]{1,0:T(8,128)(2,1)}, bf16[160,384]{1,0:T(8,128)(2,1)S(1)}, u32[]{:S(2)}, u32[]{:S(2)}) %collective-permute-start.16) | collective-permute-done | bytes 122912 | tf_op jit(solution)/shard_map/ppermute | solution.py:429
  84.4 10.1 %collective-permute-done.17.refs_13_ = bf16[160,384]{1,0:T(8,128)(2,1)S(1)} collective-permute-done((bf16[160,384]{1,0:T(8,128)(2,1)}, bf16[160,384]{1,0:T(8,128)(2,1)S(1)}, u32[]{:S(2)}, u32[]{:S(2)}) %collective-permute-start.17) | collective-permute-done | bytes 122912 | tf_op jit(solution)/shard_map/ppermute | solution.py:429
  94.6 5.0 %collective-permute-done.18.refs_14_ = bf16[160,384]{1,0:T(8,128)(2,1)S(1)} collective-permute-done((bf16[160,384]{1,0:T(8,128)(2,1)}, bf16[160,384]{1,0:T(8,128)(2,1)S(1)}, u32[]{:S(2)}, u32[]{:S(2)}) %collective-permute-start.18) | collective-permute-done | bytes 122912 | tf_op jit(solution)/shard_map/ppermute | solution.py:429
  99.6 1.9 %collective-permute-done.19.refs_15_ = bf16[160,384]{1,0:T(8,128)(2,1)S(1)} collective-permute-done((bf16[160,384]{1,0:T(8,128)(2,1)}, bf16[160,384]{1,0:T(8,128)(2,1)S(1)}, u32[]{:S(2)}, u32[]{:S(2)}) %collective-permute-start.19) | collective-permute-done | bytes 122912 | tf_op jit(solution)/shard_map/ppermute | solution.py:429
  102.3 13.1 %forward.3.refs_0_ = bf16[3,8,5248]{2,1,0:T(8,128)(2,1)} custom-call(s32[40]{0:T(128)} %dynamic_slice.3.pairs_ref, s32[1]{0:T(128)} %bitcast.1.here_ref, bf16[160,256]{1,0:T(8,128)(2,1)} %get-tuple-element.107.refs_0_, bf16[160,256]{1,0:T(8,128)(2,1)} %copy-done.12, bf16[160,256]{1,0:T(8,128)(2,1)} %copy-done.13, bf16[160,256]{1,0:T(8,128)(2,1)} %copy-done.14, ...), custom_call_target="tpu_custom_call" | custom-call | tf_op jit(solution)/shard_map/forward/pallas_call | solution.py:291
  115.9 1.5 collective-permute-start.24
  118.9 9.9 %forward.2.refs_0_ = bf16[2,8,5248]{2,1,0:T(8,128)(2,1)} custom-call(s32[40]{0:T(128)} %dynamic_slice.3.pairs_ref, s32[1]{0:T(128)} %bitcast.1.here_ref, bf16[160,256]{1,0:T(8,128)(2,1)} %get-tuple-element.107.refs_0_, bf16[160,256]{1,0:T(8,128)(2,1)} %copy-done.12, bf16[160,256]{1,0:T(8,128)(2,1)} %copy-done.13, bf16[160,256]{1,0:T(8,128)(2,1)} %copy-done.14, ...), custom_call_target="tpu_custom_call" | custom-call | tf_op jit(solution)/shard_map/forward/pallas_call | solution.py:291
  129.3 1.5 collective-permute-start.21
  133.7 11.7 %inverse.2.refs_8_ = f32[2,2,40,2,2,1280]{5,4,3,2,1,0:T(2,128)} custom-call(s32[40]{0:T(128)} %dynamic_slice.3.pairs_ref, s32[1]{0:T(128)} %bitcast.place_ref, bf16[3,8,5248]{2,1,0:T(8,128)(2,1)} %forward.3.refs_0_, bf16[3,8,5248]{2,1,0:T(8,128)(2,1)} %copy-done.22, bf16[3,8,5248]{2,1,0:T(8,128)(2,1)} %copy-done.23, bf16[3,8,5248]{2,1,0:T(8,128)(2,1)} %copy-done.24, ...), custom_call_target="tpu_custom_call" | custom-call | tf_op jit(solution)/shard_map/inverse/pallas_call | solution.py:399
  146.8 8.4 %inverse.3 = f32[2,2,40,2,2,1280]{5,4,3,2,1,0:T(2,128)} custom-call(s32[40]{0:T(128)} %dynamic_slice.3.pairs_ref, s32[1]{0:T(128)} %bitcast.place_ref, bf16[2,8,5248]{2,1,0:T(8,128)(2,1)} %forward.2.refs_0_, bf16[2,8,5248]{2,1,0:T(8,128)(2,1)} %copy-done.25, bf16[2,8,5248]{2,1,0:T(8,128)(2,1)} %copy-done.26, ...), custom_call_target="tpu_custom_call", output_to_operand_aliasing={{}: (10, {})} | custom-call | tf_op jit(solution)/shard_map/inverse/pallas_call | solution.py:399
  (114 shorter events, 20.7 us)
Async XLA Ops:
  3.3 10.9 %collective-permute-start.3 = (bf16[2,4,32,640]{3,2,1,0:T(8,128)(2,1)}, bf16[2,4,32,640]{3,2,1,0:T(8,128)(2,1)S(1)}, u32[]{:S(2)}, u32[]{:S(2)}) collective-permute-start(bf16[2,4,32,640]{3,2,1,0:T(8,128)(2,1)} %get-tuple-element.85), channel_id=1, source_target_pairs={{0,8},{8,0},{16,24},{24,16},{1,9},{9,1},{17,25},{25,17},{2,10},{10... | collective-permute-start | bytes 983048 | tf_op jit(solution)/shard_map/ppermute | solution.py:429
  8.5 47.7 %collective-permute-start = (bf16[3,4,32,640]{3,2,1,0:T(8,128)(2,1)}, bf16[3,4,32,640]{3,2,1,0:T(8,128)(2,1)S(1)}, u32[]{:S(2)}, u32[]{:S(2)}) collective-permute-start(bf16[3,4,32,640]{3,2,1,0:T(8,128)(2,1)} %get-tuple-element.72), channel_id=1, source_target_pairs={{0,8},{8,0},{16,24},{24,16},{1,9},{9,1},{17,25},{25,17},{2,10},{10... | collective-permute-start | bytes 1474568 | tf_op jit(solution)/shard_map/ppermute | solution.py:429
  10.0 46.5 %collective-permute-start.1 = (bf16[3,4,32,640]{3,2,1,0:T(8,128)(2,1)}, bf16[3,4,32,640]{3,2,1,0:T(8,128)(2,1)S(1)}, u32[]{:S(2)}, u32[]{:S(2)}) collective-permute-start(bf16[3,4,32,640]{3,2,1,0:T(8,128)(2,1)} %get-tuple-element.73), channel_id=1, source_target_pairs={{0,16},{8,24},{16,0},{24,8},{1,17},{9,25},{17,1},{25,9},{2,18},{10... | collective-permute-start | bytes 1474568 | tf_op jit(solution)/shard_map/ppermute | solution.py:429
  11.5 45.3 %collective-permute-start.2 = (bf16[3,4,32,640]{3,2,1,0:T(8,128)(2,1)}, bf16[3,4,32,640]{3,2,1,0:T(8,128)(2,1)S(1)}, u32[]{:S(2)}, u32[]{:S(2)}) collective-permute-start(bf16[3,4,32,640]{3,2,1,0:T(8,128)(2,1)} %get-tuple-element.74), channel_id=1, source_target_pairs={{0,24},{8,16},{16,8},{24,0},{1,25},{9,17},{17,9},{25,1},{2,26},{10... | collective-permute-start | bytes 1474568 | tf_op jit(solution)/shard_map/ppermute | solution.py:429
  12.0 35.2 %collective-permute-start.4 = (bf16[2,4,32,640]{3,2,1,0:T(8,128)(2,1)S(1)}, bf16[2,4,32,640]{3,2,1,0:T(8,128)(2,1)S(1)}, u32[]{:S(2)}, u32[]{:S(2)}) collective-permute-start(bf16[2,4,32,640]{3,2,1,0:T(8,128)(2,1)S(1)} %copy-done.30), channel_id=1, source_target_pairs={{0,16},{8,24},{16,0},{24,8},{1,17},{9,25},{17,1},{25,9},{2,18},{10... | collective-permute-start | bytes 983048 | tf_op jit(solution)/shard_map/ppermute | solution.py:429
  14.2 33.0 %collective-permute-start.5 = (bf16[2,4,32,640]{3,2,1,0:T(8,128)(2,1)S(1)}, bf16[2,4,32,640]{3,2,1,0:T(8,128)(2,1)S(1)}, u32[]{:S(2)}, u32[]{:S(2)}) collective-permute-start(bf16[2,4,32,640]{3,2,1,0:T(8,128)(2,1)S(1)} %copy-done.29), channel_id=1, source_target_pairs={{0,24},{8,16},{16,8},{24,0},{1,25},{9,17},{17,9},{25,1},{2,26},{10... | collective-permute-start | bytes 983048 | tf_op jit(solution)/shard_map/ppermute | solution.py:429
  54.5 12.7 %collective-permute-start.6 = (bf16[160,256]{1,0:T(8,128)(2,1)}, bf16[160,256]{1,0:T(8,128)(2,1)S(1)}, u32[]{:S(2)}, u32[]{:S(2)}) collective-permute-start(bf16[160,256]{1,0:T(8,128)(2,1)} %get-tuple-element.89), channel_id=1, source_target_pairs={{0,1},{1,0},{2,3},{3,2},{4,5},{5,4},{6,7},{7,6},{8,9},{9,8},{10,11... | collective-permute-start | bytes 245768 | tf_op jit(solution)/shard_map/ppermute | solution.py:429
  54.5 13.9 %collective-permute-start.7 = (bf16[160,256]{1,0:T(8,128)(2,1)}, bf16[160,256]{1,0:T(8,128)(2,1)S(1)}, u32[]{:S(2)}, u32[]{:S(2)}) collective-permute-start(bf16[160,256]{1,0:T(8,128)(2,1)} %get-tuple-element.90), channel_id=1, source_target_pairs={{0,2},{1,3},{2,0},{3,1},{4,6},{5,7},{6,4},{7,5},{8,10},{9,11},{10,... | collective-permute-start | bytes 245768 | tf_op jit(solution)/shard_map/ppermute | solution.py:429
  56.2 13.0 %collective-permute-start.8 = (bf16[160,256]{1,0:T(8,128)(2,1)}, bf16[160,256]{1,0:T(8,128)(2,1)S(1)}, u32[]{:S(2)}, u32[]{:S(2)}) collective-permute-start(bf16[160,256]{1,0:T(8,128)(2,1)} %get-tuple-element.91), channel_id=1, source_target_pairs={{0,3},{1,2},{2,1},{3,0},{4,7},{5,6},{6,5},{7,4},{8,11},{9,10},{10,... | collective-permute-start | bytes 245768 | tf_op jit(solution)/shard_map/ppermute | solution.py:429
  56.4 13.1 %collective-permute-start.9 = (bf16[160,256]{1,0:T(8,128)(2,1)}, bf16[160,256]{1,0:T(8,128)(2,1)S(1)}, u32[]{:S(2)}, u32[]{:S(2)}) collective-permute-start(bf16[160,256]{1,0:T(8,128)(2,1)} %get-tuple-element.92), channel_id=1, source_target_pairs={{0,4},{1,5},{2,6},{3,7},{4,0},{5,1},{6,2},{7,3},{8,12},{9,13},{10,... | collective-permute-start | bytes 245768 | tf_op jit(solution)/shard_map/ppermute | solution.py:429
  56.8 19.6 %collective-permute-start.10 = (bf16[160,256]{1,0:T(8,128)(2,1)}, bf16[160,256]{1,0:T(8,128)(2,1)S(1)}, u32[]{:S(2)}, u32[]{:S(2)}) collective-permute-start(bf16[160,256]{1,0:T(8,128)(2,1)} %get-tuple-element.93), channel_id=1, source_target_pairs={{0,5},{1,4},{2,7},{3,6},{4,1},{5,0},{6,3},{7,2},{8,13},{9,12},{10,... | collective-permute-start | bytes 245768 | tf_op jit(solution)/shard_map/ppermute | solution.py:429
  67.2 9.2 %collective-permute-start.11 = (bf16[160,256]{1,0:T(8,128)(2,1)S(1)}, bf16[160,256]{1,0:T(8,128)(2,1)S(1)}, u32[]{:S(2)}, u32[]{:S(2)}) collective-permute-start(bf16[160,256]{1,0:T(8,128)(2,1)S(1)} %copy-done.32), channel_id=1, source_target_pairs={{0,6},{1,7},{2,4},{3,5},{4,2},{5,3},{6,0},{7,1},{8,14},{9,15},{10,... | collective-permute-start | bytes 245768 | tf_op jit(solution)/shard_map/ppermute | solution.py:429
  68.5 8.9 %collective-permute-start.12 = (bf16[160,256]{1,0:T(8,128)(2,1)S(1)}, bf16[160,256]{1,0:T(8,128)(2,1)S(1)}, u32[]{:S(2)}, u32[]{:S(2)}) collective-permute-start(bf16[160,256]{1,0:T(8,128)(2,1)S(1)} %copy-done.31), channel_id=1, source_target_pairs={{0,7},{1,6},{2,5},{3,4},{4,3},{5,2},{6,1},{7,0},{8,15},{9,14},{10,... | collective-permute-start | bytes 245768 | tf_op jit(solution)/shard_map/ppermute | solution.py:429
  69.2 9.6 %collective-permute-start.13 = (bf16[160,384]{1,0:T(8,128)(2,1)}, bf16[160,384]{1,0:T(8,128)(2,1)S(1)}, u32[]{:S(2)}, u32[]{:S(2)}) collective-permute-start(bf16[160,384]{1,0:T(8,128)(2,1)} %get-tuple-element.97), channel_id=1, source_target_pairs={{0,1},{1,0},{2,3},{3,2},{4,5},{5,4},{6,7},{7,6},{8,9},{9,8},{10,11... | collective-permute-start | bytes 368648 | tf_op jit(solution)/shard_map/ppermute | solution.py:429
  69.5 10.2 %collective-permute-start.14 = (bf16[160,384]{1,0:T(8,128)(2,1)}, bf16[160,384]{1,0:T(8,128)(2,1)S(1)}, u32[]{:S(2)}, u32[]{:S(2)}) collective-permute-start(bf16[160,384]{1,0:T(8,128)(2,1)} %get-tuple-element.98), channel_id=1, source_target_pairs={{0,2},{1,3},{2,0},{3,1},{4,6},{5,7},{6,4},{7,5},{8,10},{9,11},{10,... | collective-permute-start | bytes 368648 | tf_op jit(solution)/shard_map/ppermute | solution.py:429
  77.3 17.2 %collective-permute-start.17 = (bf16[160,384]{1,0:T(8,128)(2,1)}, bf16[160,384]{1,0:T(8,128)(2,1)S(1)}, u32[]{:S(2)}, u32[]{:S(2)}) collective-permute-start(bf16[160,384]{1,0:T(8,128)(2,1)} %get-tuple-element.101), channel_id=1, source_target_pairs={{0,5},{1,4},{2,7},{3,6},{4,1},{5,0},{6,3},{7,2},{8,13},{9,12},{10,... | collective-permute-start | bytes 368648 | tf_op jit(solution)/shard_map/ppermute | solution.py:429
  78.8 20.8 %collective-permute-start.18 = (bf16[160,384]{1,0:T(8,128)(2,1)}, bf16[160,384]{1,0:T(8,128)(2,1)S(1)}, u32[]{:S(2)}, u32[]{:S(2)}) collective-permute-start(bf16[160,384]{1,0:T(8,128)(2,1)} %get-tuple-element.102), channel_id=1, source_target_pairs={{0,6},{1,7},{2,4},{3,5},{4,2},{5,3},{6,0},{7,1},{8,14},{9,15},{10,... | collective-permute-start | bytes 368648 | tf_op jit(solution)/shard_map/ppermute | solution.py:429
  79.7 21.8 %collective-permute-start.19 = (bf16[160,384]{1,0:T(8,128)(2,1)}, bf16[160,384]{1,0:T(8,128)(2,1)S(1)}, u32[]{:S(2)}, u32[]{:S(2)}) collective-permute-start(bf16[160,384]{1,0:T(8,128)(2,1)} %get-tuple-element.103), channel_id=1, source_target_pairs={{0,7},{1,6},{2,5},{3,4},{4,3},{5,2},{6,1},{7,0},{8,15},{9,14},{10,... | collective-permute-start | bytes 368648 | tf_op jit(solution)/shard_map/ppermute | solution.py:429
  115.4 15.4 %collective-permute-start.23 = (bf16[3,8,5248]{2,1,0:T(8,128)(2,1)}, bf16[3,8,5248]{2,1,0:T(8,128)(2,1)S(1)}, u32[]{:S(2)}, u32[]{:S(2)}) collective-permute-start(bf16[3,8,5248]{2,1,0:T(8,128)(2,1)} %forward.3.refs_0_), channel_id=1, source_target_pairs={{0,8},{8,0},{16,24},{24,16},{1,9},{9,1},{17,25},{25,17},{2,10},{10... | collective-permute-start | bytes 755720 | tf_op jit(solution)/shard_map/ppermute | solution.py:429
  115.9 16.4 %collective-permute-start.24 = (bf16[3,8,5248]{2,1,0:T(8,128)(2,1)}, bf16[3,8,5248]{2,1,0:T(8,128)(2,1)S(1)}, u32[]{:S(2)}, u32[]{:S(2)}) collective-permute-start(bf16[3,8,5248]{2,1,0:T(8,128)(2,1)} %forward.3.refs_0_), channel_id=1, source_target_pairs={{0,16},{8,24},{16,0},{24,8},{1,17},{9,25},{17,1},{25,9},{2,18},{10... | collective-permute-start | bytes 755720 | tf_op jit(solution)/shard_map/ppermute | solution.py:429
  117.4 14.8 %collective-permute-start.25 = (bf16[3,8,5248]{2,1,0:T(8,128)(2,1)}, bf16[3,8,5248]{2,1,0:T(8,128)(2,1)S(1)}, u32[]{:S(2)}, u32[]{:S(2)}) collective-permute-start(bf16[3,8,5248]{2,1,0:T(8,128)(2,1)} %forward.3.refs_0_), channel_id=1, source_target_pairs={{0,24},{8,16},{16,8},{24,0},{1,25},{9,17},{17,9},{25,1},{2,26},{10... | collective-permute-start | bytes 755720 | tf_op jit(solution)/shard_map/ppermute | solution.py:429
  128.8 16.6 %collective-permute-start.20 = (bf16[2,8,5248]{2,1,0:T(8,128)(2,1)}, bf16[2,8,5248]{2,1,0:T(8,128)(2,1)S(1)}, u32[]{:S(2)}, u32[]{:S(2)}) collective-permute-start(bf16[2,8,5248]{2,1,0:T(8,128)(2,1)} %forward.2.refs_0_), channel_id=1, source_target_pairs={{0,8},{8,0},{16,24},{24,16},{1,9},{9,1},{17,25},{25,17},{2,10},{10... | collective-permute-start | bytes 503816 | tf_op jit(solution)/shard_map/ppermute | solution.py:429
  129.3 16.1 %collective-permute-start.21 = (bf16[2,8,5248]{2,1,0:T(8,128)(2,1)}, bf16[2,8,5248]{2,1,0:T(8,128)(2,1)S(1)}, u32[]{:S(2)}, u32[]{:S(2)}) collective-permute-start(bf16[2,8,5248]{2,1,0:T(8,128)(2,1)} %forward.2.refs_0_), channel_id=1, source_target_pairs={{0,16},{8,24},{16,0},{24,8},{1,17},{9,25},{17,1},{25,9},{2,18},{10... | collective-permute-start | bytes 503816 | tf_op jit(solution)/shard_map/ppermute | solution.py:429
  130.8 14.6 %collective-permute-start.22 = (bf16[2,8,5248]{2,1,0:T(8,128)(2,1)}, bf16[2,8,5248]{2,1,0:T(8,128)(2,1)S(1)}, u32[]{:S(2)}, u32[]{:S(2)}) collective-permute-start(bf16[2,8,5248]{2,1,0:T(8,128)(2,1)} %forward.2.refs_0_), channel_id=1, source_target_pairs={{0,24},{8,16},{16,8},{24,0},{1,25},{9,17},{17,9},{25,1},{2,26},{10... | collective-permute-start | bytes 503816 | tf_op jit(solution)/shard_map/ppermute | solution.py:429
  (36 other events, 506.3 us)

commit v4 on v3

--- a/solution.py
+++ b/solution.py
@@ -134,46 +134,56 @@
     )(couples)
 
 
-def fourier_call(place, here, waves, pieces, peers):
+def fourier_call(place, here, waves, pieces, peers, cuts):
     parts = len(pieces)
+    total_outs = peers * len(cuts)
     rows, lons = pieces[0].shape
     columns = waves.shape[0]
     block = columns // peers
 
+    steps = 2
+    share = columns // steps
+
     def body(place_ref, here_ref, w_ref, *refs):
-        outs, total = refs[parts : parts + peers], refs[parts + peers]
-        for d in range(parts):
-
-            @pl.when(pl.program_id(0) == d)
-            def _():
-                term = lax.dot_general(
-                    w_ref[...], refs[d][...], (((1,), (1,)), ((), ())), preferred_element_type=F32
-                )
-                if d > 0:
-                    term = total[...] + term
-                total[...] = term
-
-        @pl.when(pl.program_id(0) == parts - 1)
+        outs = refs[parts : parts + total_outs]
+        whole, total = refs[parts + total_outs :]
+        step = pl.program_id(0)
+
+        @pl.when(step == 0)
         def _():
-            for e in range(peers):
-                start = pl.multiple_of(jnp.bitwise_xor(here_ref[0], e) * block, 16)
-                outs[e][...] = total[pl.ds(start, block)].astype(BF)
+            for d in range(parts):
+                start = jnp.bitwise_xor(place_ref[0], d) * lons
+                whole[:, pl.ds(pl.multiple_of(start, LANE), lons)] = refs[d][...]
+
+        total[pl.ds(pl.multiple_of(step * share, 32), share)] = lax.dot_general(
+            w_ref[...], whole[...], (((1,), (1,)), ((), ())), preferred_element_type=F32
+        ).astype(BF)
+
+        @pl.when(step == steps - 1)
+        def _():
+            for number, (first, size) in enumerate(cuts):
+                for e in range(peers):
+                    start = jnp.bitwise_xor(here_ref[0], e) * block + first
+                    outs[number * peers + e][...] = total[pl.ds(pl.multiple_of(start, 32), size)]
 
     return pl.pallas_call(
         body,
         name="fourier",
         grid_spec=pltpu.PrefetchScalarGridSpec(
             num_scalar_prefetch=2,
-            grid=(parts,),
-            in_specs=[
-                pl.BlockSpec((columns, lons), lambda i, p, h: (0, jnp.bitwise_xor(p[0], i)))
-            ]
-            + [pl.BlockSpec((rows, lons), lambda i, *_: (0, 0))] * parts,
-            out_specs=[pl.BlockSpec((block, rows), lambda i, *_: (0, 0))] * peers,
-            scratch_shapes=[pltpu.VMEM((columns, rows), F32)],
+            grid=(steps,),
+            in_specs=[pl.BlockSpec((share, parts * lons), lambda i, *_: (i, 0))]
+            + [pl.BlockSpec((rows, lons), lambda i, *_: (0, 0))]
+            + [pl.BlockSpec(memory_space=pltpu.VMEM)] * (parts - 1),
+            out_specs=[
+                pl.BlockSpec((size, rows), lambda i, *_: (0, 0)) for _, size in cuts for _ in range(peers)
+            ],
+            scratch_shapes=[pltpu.VMEM((rows, parts * lons), BF), pltpu.VMEM((columns, rows), BF)],
         ),
-        out_shape=[jax.ShapeDtypeStruct((block, rows), BF)] * peers,
-    )(place, here, waves, *pieces)
+        out_shape=[
+            jax.ShapeDtypeStruct((size, rows), BF) for _, size in cuts for _ in range(peers)
+        ],
+    )(place, here, waves, *in_vmem(pieces))
 
 
 def by_slot(index, pairs, group):
@@ -210,8 +220,8 @@
 def forward_call(pairs, here, received, chunks, table, quadrature, first, groups):
     row_total, _, half_lat = table.shape
     wave_count = row_total - 1
-    bands = len(received[0])
-    shares = [block for blocks in received for block in blocks]
+    bands = len(received[0][1])
+    shares = [block for _, blocks in received for block in in_vmem(blocks)]
     units = chunks[-1][1]
     row_block = GROUP * 4
     fields = LANE // SUB
@@ -227,8 +237,9 @@
         table_ref, quad_ref, out, spread = refs[len(shares) : len(shares) + 4]
         recv = refs[len(shares) + 4 :]
         group = pl.program_id(0) + first
-        mine = pl.ds(pl.multiple_of(group * row_block, row_block), row_block)
         for number in range(len(chunks)):
+            start = group * row_block - received[number][0]
+            mine = pl.ds(pl.multiple_of(start, row_block), row_block)
             for e in range(bands):
                 band = jnp.bitwise_xor(here_ref[0], e)
                 recv[number][band] = shared[number * bands + e][mine]
@@ -294,7 +305,12 @@
         grid_spec=pltpu.PrefetchScalarGridSpec(
             num_scalar_prefetch=2,
             grid=(groups,),
-            in_specs=[pl.BlockSpec(block.shape, lambda g, *_: (0, 0)) for block in shares]
+            in_specs=[
+                pl.BlockSpec(memory_space=pltpu.VMEM)
+                if number % bands
+                else pl.BlockSpec(block.shape, lambda g, *_: (0, 0))
+                for number, block in enumerate(shares)
+            ]
             + [
                 pl.BlockSpec((row_total, GROUP, half_lat), lambda g, *_: (0, first + g, 0)),
                 pl.BlockSpec((1, half_lat), lambda g, *_: (0, 0)),
@@ -304,7 +320,7 @@
             + [pltpu.VMEM((bands, row_block, (hi - lo) * LANE), BF) for lo, hi in chunks],
         ),
         out_shape=jax.ShapeDtypeStruct((groups, 8, 2 * per + LANE), BF),
-    )(pairs, here, *shares, table, quadrature[None, :])
+    )(pairs, here, *shares, table, quadrature)
 
 
 def mix_matrix(operator, own):
@@ -335,7 +351,8 @@
         out, stack, x_ref = refs[-3:]
         group = pl.program_id(0) + first
         for d in range(lev):
-            stack[jnp.bitwise_xor(place_ref[0], d)] = got[d][0].astype(F32)
+            part = got[d][0 if d == 0 else pl.program_id(0)]
+            stack[jnp.bitwise_xor(place_ref[0], d)] = part.astype(F32)
         lane = lax.broadcasted_iota(jnp.int32, (1, lanes), 1)
         place = lane // GROUP
         half = wave_count // 2
@@ -402,7 +419,8 @@
         grid_spec=pltpu.PrefetchScalarGridSpec(
             num_scalar_prefetch=2,
             grid=(groups,),
-            in_specs=[pl.BlockSpec((1, eight, lanes), lambda g, *_: (g, 0, 0))] * lev
+            in_specs=[pl.BlockSpec((1, eight, lanes), lambda g, *_: (g, 0, 0))]
+            + [pl.BlockSpec(memory_space=pltpu.VMEM)] * (lev - 1)
             + [
                 pl.BlockSpec((n, n), lambda g, *_: (0, 0)),
                 pl.BlockSpec((eight, n), lambda g, p, q: (q[0], 0)),
@@ -420,7 +438,11 @@
         ),
         out_shape=jax.ShapeDtypeStruct((2, own, slots, 2, 2, 2 * half_lat), F32),
         input_output_aliases={lev + 6: 0} if more else {},
-    )(pairs, place, *gathered, project, rebuild, factors, table, *more)
+    )(pairs, place, *in_vmem(gathered), project, rebuild, factors, table, *more)
+
+
+def in_vmem(arrays):
+    return [arrays[0]] + [pltpu.with_memory_space_constraint(x, pltpu.VMEM) for x in arrays[1:]]
 
 
 def swap(blocks, axis):
@@ -445,29 +467,40 @@
         products.append(products_call(place, u, v, t, operator, lev, lo, hi - lo))
     couples, products[-1] = lax.optimization_barrier((couples, products[-1]))
     waves = wave_rows_call(couples, lons * lev, wave_count)
+    groups = slots // GROUP
+    cut = -(-groups * CUT[0] // CUT[1])
+    parts = ((0, cut), (cut, groups - cut))
+    rows = 4 * GROUP
     for (lo, hi), blocks in zip(CHUNKS, products):
         blocks = swap(blocks, "lev")
+        if lo > 0:
+            blocks, late = lax.optimization_barrier((blocks, late))
         pieces = [x.reshape((hi - lo) * LANE, lons) for x in blocks]
-        blocks = fourier_call(place, here, waves, pieces, lat)
-        if hi == CHUNKS[-1][1]:
+        ending = hi == CHUNKS[-1][1]
+        cuts = [(first * rows, count * rows) for first, count in parts]
+        cuts = cuts if ending else [(0, groups * rows)]
+        blocks = fourier_call(place, here, waves, pieces, lat, cuts)
+        if lo == 0:
             blocks, late = lax.optimization_barrier(
                 (blocks, (couples, quadrature, project, rebuild, factors))
             )
-        received.append(swap(blocks, "lat"))
-    couples, quadrature, project, rebuild, factors = late
-    pairs = lax.dynamic_slice_in_dim(couples, lax.axis_index("lat") * slots, slots)
-    to_modes, level = mix_matrix(project, own)
-    to_levels, _ = mix_matrix(rebuild, own)
-    factor_rows = jnp.broadcast_to(factors[level][:, None], (level.shape[0], LANE))
-    received, to_modes, to_levels, factor_rows = lax.optimization_barrier(
-        (received, to_modes, to_levels, factor_rows)
-    )
-    groups = slots // GROUP
-    cut = -(-groups * CUT[0] // CUT[1])
-    parts = ((0, cut), (cut, groups - cut))
+            late_couples, late_quadrature, project, rebuild, factors = late
+            pairs = lax.dynamic_slice_in_dim(
+                late_couples, lax.axis_index("lat") * slots, slots
+            )
+            to_modes, level = mix_matrix(project, own)
+            to_levels, _ = mix_matrix(rebuild, own)
+            factor_rows = jnp.broadcast_to(factors[level][:, None], (level.shape[0], LANE))
+            late = (pairs, late_quadrature[None, :], to_modes, to_levels, factor_rows)
+        shares = []
+        for number, (first, _) in enumerate(cuts):
+            shares.append((first, swap(blocks[number * lat : (number + 1) * lat], "lat")))
+        received.append(shares)
+    pairs, quadrature, to_modes, to_levels, factor_rows = late
     gathered = []
-    for first, count in parts:
-        block = forward_call(pairs, here, received, CHUNKS, flat, quadrature, first, count)
+    for number, (first, count) in enumerate(parts):
+        shares = [each[number if len(each) > 1 else 0] for each in received]
+        block = forward_call(pairs, here, shares, CHUNKS, flat, quadrature, first, count)
         gathered.append(swap([block] * lev, "lev"))
     result = None
     for (first, _), blocks in zip(parts, gathered):

time: 156 us -> 158 us (1.013)
  the two profiles are of different devices: /device:TPU:18 before, /device:TPU:0 now
where the time goes in v4:
time: 158 us
  Pallas kernels  69.5 us (44%)
  starting transfers between devices  45.2 us (29%)
  waiting for transfers between devices  37.8 us (24%)
  local copies, waits for them, and re-layouts  3.32 us (2%)
  matrix products  1.79 us (1%)
    ppermute x33, starting transfers between devices, swap(): lax.ppermute(blocks[d], axis, [(i, i ^ d) for i in range(count)])  45.2 us
    ppermute x33, waiting for transfers between devices, swap(): lax.ppermute(blocks[d], axis, [(i, i ^ d) for i in range(count)])  37.8 us
    pallas_call x2, Pallas kernels, forward_call(): pl.pallas_call(body, name='forward', grid_spec=pltpu.PrefetchScalarGridSp...  21.9 us
    pallas_call x2, Pallas kernels, inverse_call(): pl.pallas_call(body, name='inverse', grid_spec=pltpu.PrefetchScalarGridSp...  19.9 us
    pallas_call x2, Pallas kernels, fourier_call(): pl.pallas_call(body, name='fourier', grid_spec=pltpu.PrefetchScalarGridSp...  12.2 us
    pallas_call x2, Pallas kernels, products_call(): pl.pallas_call(body, name='products', grid_spec=pltpu.PrefetchScalarGridS...  7.85 us
    pallas_call x1, Pallas kernels, wave_rows_call(): pl.pallas_call(body, name='wave_rows', grid_spec=pltpu.PrefetchScalarGrid...  7.61 us
  transfers between devices with their start and end apart: 33, of which 6 were waited for; matrix products, arithmetic and copies ran while one was open for 3% of the time, Pallas kernels for 29%

profile of v4, /device:TPU:0, one launch (start us, length us, event | category | flops | bytes accessed | tf_op | source)
XLA Modules:
  0.0 157.7 jit_solution(13082887995444035037)
XLA Ops:
  0.0 3.3 %products.3 = (bf16[2,4,32,640]{3,2,1,0:T(8,128)(2,1)}, bf16[2,4,32,640]{3,2,1,0:T(8,128)(2,1)}, bf16[2,4,32,640]{3,2,1,0:T(8,128)(2,1)}, bf16[2,4,32,640]{3,2,1,0:T(8,128)(2,1)}) custom-call(s32[1]{0:T(128)} %bitcast.place_ref, bf16[8,8]{1,0:T(8,128)(2,1)} %op_ref.3, bf16[8,160,640]{2,1,0:T(8,128)(2,1)} %u_ref.3, bf16[8,160,640]{2,1,0:T(8,128)(2,1)} %v_ref.3, ...), custom_call_target="tpu_custom_call" | custom-call | tf_op jit(solution)/shard_map/products/pallas_call | solution.py:52
  3.3 3.0 %collective-permute-start.3 = (bf16[2,4,32,640]{3,2,1,0:T(8,128)(2,1)}, bf16[2,4,32,640]{3,2,1,0:T(8,128)(2,1)S(1)}, u32[]{:S(2)}, u32[]{:S(2)}) collective-permute-start(bf16[2,4,32,640]{3,2,1,0:T(8,128)(2,1)} %get-tuple-element.74), channel_id=1, source_target_pairs={{0,8},{8,0},{16,24},{24,16},{1,9},{9,1},{17,25},{25,17},{2,10},{10... | collective-permute-start | bytes 983048 | tf_op jit(solution)/shard_map/ppermute | solution.py:451
  6.3 4.6 %products.2 = (bf16[3,4,32,640]{3,2,1,0:T(8,128)(2,1)}, bf16[3,4,32,640]{3,2,1,0:T(8,128)(2,1)}, bf16[3,4,32,640]{3,2,1,0:T(8,128)(2,1)}, bf16[3,4,32,640]{3,2,1,0:T(8,128)(2,1)}) custom-call(s32[1]{0:T(128)} %bitcast.place_ref, bf16[8,8]{1,0:T(8,128)(2,1)} %op_ref.3, bf16[8,160,640]{2,1,0:T(8,128)(2,1)} %u_ref.3, bf16[8,160,640]{2,1,0:T(8,128)(2,1)} %v_ref.3, ...), custom_call_target="tpu_custom_call" | custom-call | tf_op jit(solution)/shard_map/products/pallas_call | solution.py:52
  11.0 1.9 %collective-permute-start.1 = (bf16[3,4,32,640]{3,2,1,0:T(8,128)(2,1)}, bf16[3,4,32,640]{3,2,1,0:T(8,128)(2,1)S(1)}, u32[]{:S(2)}, u32[]{:S(2)}) collective-permute-start(bf16[3,4,32,640]{3,2,1,0:T(8,128)(2,1)} %get-tuple-element.70), channel_id=1, source_target_pairs={{0,16},{8,24},{16,0},{24,8},{1,17},{9,25},{17,1},{25,9},{2,18},{10... | collective-permute-start | bytes 1474568 | tf_op jit(solution)/shard_map/ppermute | solution.py:451
  15.9 2.2 %collective-permute-start.5 = (bf16[2,4,32,640]{3,2,1,0:T(8,128)(2,1)S(1)}, bf16[2,4,32,640]{3,2,1,0:T(8,128)(2,1)S(1)}, u32[]{:S(2)}, u32[]{:S(2)}) collective-permute-start(bf16[2,4,32,640]{3,2,1,0:T(8,128)(2,1)S(1)} %copy-done.3), channel_id=1, source_target_pairs={{0,24},{8,16},{16,8},{24,0},{1,25},{9,17},{17,9},{25,1},{2,26},{10... | collective-permute-start | bytes 983048 | tf_op jit(solution)/shard_map/ppermute | solution.py:451
  18.1 7.6 %wave_rows.1.w_ref = bf16[1280,2560]{1,0:T(8,128)(2,1)} custom-call(s32[320]{0:T(512)} %couples_ref), custom_call_target="tpu_custom_call" | custom-call | tf_op jit(solution)/shard_map/wave_rows/pallas_call | solution.py:124
  25.7 22.7 %collective-permute-done.4 = bf16[2,4,32,640]{3,2,1,0:T(8,128)(2,1)S(1)} collective-permute-done((bf16[2,4,32,640]{3,2,1,0:T(8,128)(2,1)S(1)}, bf16[2,4,32,640]{3,2,1,0:T(8,128)(2,1)S(1)}, u32[]{:S(2)}, u32[]{:S(2)}) %collective-permute-start.4) | collective-permute-done | bytes 327712 | tf_op jit(solution)/shard_map/ppermute | solution.py:451
  48.5 5.2 %fourier.2 = (bf16[160,256]{1,0:T(8,128)(2,1)}, bf16[160,256]{1,0:T(8,128)(2,1)}, bf16[160,256]{1,0:T(8,128)(2,1)}, bf16[160,256]{1,0:T(8,128)(2,1)}, bf16[160,2...) custom-call(s32[1]{0:T(128)} %bitcast.place_ref, ...), custom_call_target="tpu_custom_call" | custom-call | tf_op jit(solution)/shard_map/fourier/pallas_call | solution.py:169
  53.6 1.8 %collective-permute-start.7 = (bf16[160,256]{1,0:T(8,128)(2,1)}, bf16[160,256]{1,0:T(8,128)(2,1)S(1)}, u32[]{:S(2)}, u32[]{:S(2)}) collective-permute-start(bf16[160,256]{1,0:T(8,128)(2,1)} %get-tuple-element.93), channel_id=1, source_target_pairs={{0,2},{1,3},{2,0},{3,1},{4,6},{5,7},{6,4},{7,5},{8,10},{9,11},{10,... | collective-permute-start | bytes 245768 | tf_op jit(solution)/shard_map/ppermute | solution.py:451
  56.6 2.1 %collective-permute-done.7.refs_2_ = bf16[160,256]{1,0:T(8,128)(2,1)S(1)} collective-permute-done((bf16[160,256]{1,0:T(8,128)(2,1)}, bf16[160,256]{1,0:T(8,128)(2,1)S(1)}, u32[]{:S(2)}, u32[]{:S(2)}) %collective-permute-start.7) | collective-permute-done | bytes 81952 | tf_op jit(solution)/shard_map/ppermute | solution.py:451
  58.7 2.7 %collective-permute-start.9 = (bf16[160,256]{1,0:T(8,128)(2,1)}, bf16[160,256]{1,0:T(8,128)(2,1)S(1)}, u32[]{:S(2)}, u32[]{:S(2)}) collective-permute-start(bf16[160,256]{1,0:T(8,128)(2,1)} %get-tuple-element.95), channel_id=1, source_target_pairs={{0,4},{1,5},{2,6},{3,7},{4,0},{5,1},{6,2},{7,3},{8,12},{9,13},{10,... | collective-permute-start | bytes 245768 | tf_op jit(solution)/shard_map/ppermute | solution.py:451
  61.5 2.9 %collective-permute-start.11 = (bf16[160,256]{1,0:T(8,128)(2,1)}, bf16[160,256]{1,0:T(8,128)(2,1)S(1)}, u32[]{:S(2)}, u32[]{:S(2)}) collective-permute-start(bf16[160,256]{1,0:T(8,128)(2,1)} %get-tuple-element.97), channel_id=1, source_target_pairs={{0,6},{1,7},{2,4},{3,5},{4,2},{5,3},{6,0},{7,1},{8,14},{9,15},{10,... | collective-permute-start | bytes 245768 | tf_op jit(solution)/shard_map/ppermute | solution.py:451
  69.8 7.0 %fourier.3 = (bf16[96,384]{1,0:T(8,128)(2,1)}, bf16[96,384]{1,0:T(8,128)(2,1)}, bf16[96,384]{1,0:T(8,128)(2,1)}, bf16[96,384]{1,0:T(8,128)(2,1)}, bf16[96,384]{1...) custom-call(s32[1]{0:T(128)} %bitcast.place_ref, ...), custom_call_target="tpu_custom_call" | custom-call | tf_op jit(solution)/shard_map/fourier/pallas_call | solution.py:169
  78.8 2.4 %collective-permute-start.26 = (bf16[96,384]{1,0:T(8,128)(2,1)}, bf16[96,384]{1,0:T(8,128)(2,1)S(1)}, u32[]{:S(2)}, u32[]{:S(2)}) collective-permute-start(bf16[96,384]{1,0:T(8,128)(2,1)} %get-tuple-element.119), channel_id=1, source_target_pairs={{0,4},{1,5},{2,6},{3,7},{4,0},{5,1},{6,2},{7,3},{8,12},{9,13},{10,... | collective-permute-start | bytes 221192 | tf_op jit(solution)/shard_map/ppermute | solution.py:451
  81.4 3.5 %collective-permute-start.28 = (bf16[96,384]{1,0:T(8,128)(2,1)}, bf16[96,384]{1,0:T(8,128)(2,1)S(1)}, u32[]{:S(2)}, u32[]{:S(2)}) collective-permute-start(bf16[96,384]{1,0:T(8,128)(2,1)} %get-tuple-element.121), channel_id=1, source_target_pairs={{0,6},{1,7},{2,4},{3,5},{4,2},{5,3},{6,0},{7,1},{8,14},{9,15},{10,... | collective-permute-start | bytes 221192 | tf_op jit(solution)/shard_map/ppermute | solution.py:451
  85.0 8.0 %collective-permute-done.27.refs_13_ = bf16[96,384]{1,0:T(8,128)(2,1)S(1)} collective-permute-done((bf16[96,384]{1,0:T(8,128)(2,1)}, bf16[96,384]{1,0:T(8,128)(2,1)S(1)}, u32[]{:S(2)}, u32[]{:S(2)}) %collective-permute-start.27) | collective-permute-done | bytes 73760 | tf_op jit(solution)/shard_map/ppermute | solution.py:451
  93.0 12.5 %forward.3.refs_0_ = bf16[3,8,5248]{2,1,0:T(8,128)(2,1)} custom-call(s32[40]{0:T(128)} %dynamic_slice.3.pairs_ref, s32[1]{0:T(128)} %bitcast.1.here_ref, bf16[160,256]{1,0:T(8,128)(2,1)} %get-tuple-element.91.refs_0_, bf16[160,256]{1,0:T(8,128)(2,1)S(1)} %collective-permute-done.6.refs_1_, bf16[160,256]{1,0:T(8,128)(2,1)S(1)} %collective-permute-done.7.refs_2_, ...), custom_call_target="tpu_custom_call" | custom-call | tf_op jit(solution)/shard_map/forward/pallas_call | solution.py:302
  107.0 3.8 %collective-permute-start.14 = (bf16[64,384]{1,0:T(8,128)(2,1)S(1)}, bf16[64,384]{1,0:T(8,128)(2,1)S(1)}, u32[]{:S(2)}, u32[]{:S(2)}) collective-permute-start(bf16[64,384]{1,0:T(8,128)(2,1)S(1)} %copy-done.10), channel_id=1, source_target_pairs={{0,2},{1,3},{2,0},{3,1},{4,6},{5,7},{6,4},{7,5},{8,10},{9,11},{10,... | collective-permute-start | bytes 147464 | tf_op jit(solution)/shard_map/ppermute | solution.py:451
  110.9 2.5 %collective-permute-start.16 = (bf16[64,384]{1,0:T(8,128)(2,1)S(1)}, bf16[64,384]{1,0:T(8,128)(2,1)S(1)}, u32[]{:S(2)}, u32[]{:S(2)}) collective-permute-start(bf16[64,384]{1,0:T(8,128)(2,1)S(1)} %copy-done.8), channel_id=1, source_target_pairs={{0,4},{1,5},{2,6},{3,7},{4,0},{5,1},{6,2},{7,3},{8,12},{9,13},{10,... | collective-permute-start | bytes 147464 | tf_op jit(solution)/shard_map/ppermute | solution.py:451
  116.0 2.3 %collective-permute-start.18 = (bf16[64,384]{1,0:T(8,128)(2,1)S(1)}, bf16[64,384]{1,0:T(8,128)(2,1)S(1)}, u32[]{:S(2)}, u32[]{:S(2)}) collective-permute-start(bf16[64,384]{1,0:T(8,128)(2,1)S(1)} %copy-done.6), channel_id=1, source_target_pairs={{0,6},{1,7},{2,4},{3,5},{4,2},{5,3},{6,0},{7,1},{8,14},{9,15},{10,... | collective-permute-start | bytes 147464 | tf_op jit(solution)/shard_map/ppermute | solution.py:451
  121.9 2.9 %collective-permute-done.19.refs_15_ = bf16[64,384]{1,0:T(8,128)(2,1)S(1)} collective-permute-done((bf16[64,384]{1,0:T(8,128)(2,1)S(1)}, bf16[64,384]{1,0:T(8,128)(2,1)S(1)}, u32[]{:S(2)}, u32[]{:S(2)}) %collective-permute-start.19) | collective-permute-done | bytes 49184 | tf_op jit(solution)/shard_map/ppermute | solution.py:451
  124.9 9.5 %forward.2.refs_0_ = bf16[2,8,5248]{2,1,0:T(8,128)(2,1)} custom-call(s32[40]{0:T(128)} %dynamic_slice.3.pairs_ref, s32[1]{0:T(128)} %bitcast.1.here_ref, bf16[160,256]{1,0:T(8,128)(2,1)} %get-tuple-element.91.refs_0_, bf16[160,256]{1,0:T(8,128)(2,1)S(1)} %collective-permute-done.6.refs_1_, bf16[160,256]{1,0:T(8,128)(2,1)S(1)} %collective-permute-done.7.refs_2_, ...), custom_call_target="tpu_custom_call" | custom-call | tf_op jit(solution)/shard_map/forward/pallas_call | solution.py:302
  137.8 11.7 %inverse.2.refs_8_ = f32[2,2,40,2,2,1280]{5,4,3,2,1,0:T(2,128)} custom-call(s32[40]{0:T(128)} %dynamic_slice.3.pairs_ref, s32[1]{0:T(128)} %bitcast.place_ref, bf16[3,8,5248]{2,1,0:T(8,128)(2,1)} %forward.3.refs_0_, bf16[3,8,5248]{2,1,0:T(8,128)(2,1)S(1)} %collective-permute-done.30.refs_1_, bf16[3,8,5248]{2,1,0:T(8,128)(2,1)S(1)} %collective-permute-done.31.refs_2_, ...), custom_call_target="tpu_custom_call" | custom-call | tf_op jit(solution)/shard_map/inverse/pallas_call | solution.py:416
  149.5 8.2 %inverse.3 = f32[2,2,40,2,2,1280]{5,4,3,2,1,0:T(2,128)} custom-call(s32[40]{0:T(128)} %dynamic_slice.3.pairs_ref, s32[1]{0:T(128)} %bitcast.place_ref, bf16[2,8,5248]{2,1,0:T(8,128)(2,1)} %forward.2.refs_0_, bf16[2,8,5248]{2,1,0:T(8,128)(2,1)S(1)} %collective-permute-done.20.refs_1_, ...), custom_call_target="tpu_custom_call", output_to_operand_aliasing={{}: (10, {})} | custom-call | tf_op jit(solution)/shard_map/inverse/pallas_call | solution.py:416
  (86 shorter events, 23.3 us)
Async XLA Ops:
  3.3 12.6 %collective-permute-start.3 = (bf16[2,4,32,640]{3,2,1,0:T(8,128)(2,1)}, bf16[2,4,32,640]{3,2,1,0:T(8,128)(2,1)S(1)}, u32[]{:S(2)}, u32[]{:S(2)}) collective-permute-start(bf16[2,4,32,640]{3,2,1,0:T(8,128)(2,1)} %get-tuple-element.74), channel_id=1, source_target_pairs={{0,8},{8,0},{16,24},{24,16},{1,9},{9,1},{17,25},{25,17},{2,10},{10... | collective-permute-start | bytes 983048 | tf_op jit(solution)/shard_map/ppermute | solution.py:451
  10.9 50.6 %collective-permute-start = (bf16[3,4,32,640]{3,2,1,0:T(8,128)(2,1)}, bf16[3,4,32,640]{3,2,1,0:T(8,128)(2,1)S(1)}, u32[]{:S(2)}, u32[]{:S(2)}) collective-permute-start(bf16[3,4,32,640]{3,2,1,0:T(8,128)(2,1)} %get-tuple-element.69), channel_id=1, source_target_pairs={{0,8},{8,0},{16,24},{24,16},{1,9},{9,1},{17,25},{25,17},{2,10},{10... | collective-permute-start | bytes 1474568 | tf_op jit(solution)/shard_map/ppermute | solution.py:451
  11.0 50.5 %collective-permute-start.1 = (bf16[3,4,32,640]{3,2,1,0:T(8,128)(2,1)}, bf16[3,4,32,640]{3,2,1,0:T(8,128)(2,1)S(1)}, u32[]{:S(2)}, u32[]{:S(2)}) collective-permute-start(bf16[3,4,32,640]{3,2,1,0:T(8,128)(2,1)} %get-tuple-element.70), channel_id=1, source_target_pairs={{0,16},{8,24},{16,0},{24,8},{1,17},{9,25},{17,1},{25,9},{2,18},{10... | collective-permute-start | bytes 1474568 | tf_op jit(solution)/shard_map/ppermute | solution.py:451
  13.0 51.4 %collective-permute-start.2 = (bf16[3,4,32,640]{3,2,1,0:T(8,128)(2,1)}, bf16[3,4,32,640]{3,2,1,0:T(8,128)(2,1)S(1)}, u32[]{:S(2)}, u32[]{:S(2)}) collective-permute-start(bf16[3,4,32,640]{3,2,1,0:T(8,128)(2,1)} %get-tuple-element.71), channel_id=1, source_target_pairs={{0,24},{8,16},{16,8},{24,0},{1,25},{9,17},{17,9},{25,1},{2,26},{10... | collective-permute-start | bytes 1474568 | tf_op jit(solution)/shard_map/ppermute | solution.py:451
  14.4 34.1 %collective-permute-start.4 = (bf16[2,4,32,640]{3,2,1,0:T(8,128)(2,1)S(1)}, bf16[2,4,32,640]{3,2,1,0:T(8,128)(2,1)S(1)}, u32[]{:S(2)}, u32[]{:S(2)}) collective-permute-start(bf16[2,4,32,640]{3,2,1,0:T(8,128)(2,1)S(1)} %copy-done.4), channel_id=1, source_target_pairs={{0,16},{8,24},{16,0},{24,8},{1,17},{9,25},{17,1},{25,9},{2,18},{10... | collective-permute-start | bytes 983048 | tf_op jit(solution)/shard_map/ppermute | solution.py:451
  15.9 32.6 %collective-permute-start.5 = (bf16[2,4,32,640]{3,2,1,0:T(8,128)(2,1)S(1)}, bf16[2,4,32,640]{3,2,1,0:T(8,128)(2,1)S(1)}, u32[]{:S(2)}, u32[]{:S(2)}) collective-permute-start(bf16[2,4,32,640]{3,2,1,0:T(8,128)(2,1)S(1)} %copy-done.3), channel_id=1, source_target_pairs={{0,24},{8,16},{16,8},{24,0},{1,25},{9,17},{17,9},{25,1},{2,26},{10... | collective-permute-start | bytes 983048 | tf_op jit(solution)/shard_map/ppermute | solution.py:451
  56.3 20.5 %collective-permute-start.8 = (bf16[160,256]{1,0:T(8,128)(2,1)}, bf16[160,256]{1,0:T(8,128)(2,1)S(1)}, u32[]{:S(2)}, u32[]{:S(2)}) collective-permute-start(bf16[160,256]{1,0:T(8,128)(2,1)} %get-tuple-element.94), channel_id=1, source_target_pairs={{0,3},{1,2},{2,1},{3,0},{4,7},{5,6},{6,5},{7,4},{8,11},{9,10},{10,... | collective-permute-start | bytes 245768 | tf_op jit(solution)/shard_map/ppermute | solution.py:451
  58.7 18.2 %collective-permute-start.9 = (bf16[160,256]{1,0:T(8,128)(2,1)}, bf16[160,256]{1,0:T(8,128)(2,1)S(1)}, u32[]{:S(2)}, u32[]{:S(2)}) collective-permute-start(bf16[160,256]{1,0:T(8,128)(2,1)} %get-tuple-element.95), channel_id=1, source_target_pairs={{0,4},{1,5},{2,6},{3,7},{4,0},{5,1},{6,2},{7,3},{8,12},{9,13},{10,... | collective-permute-start | bytes 245768 | tf_op jit(solution)/shard_map/ppermute | solution.py:451
  61.5 15.5 %collective-permute-start.10 = (bf16[160,256]{1,0:T(8,128)(2,1)}, bf16[160,256]{1,0:T(8,128)(2,1)S(1)}, u32[]{:S(2)}, u32[]{:S(2)}) collective-permute-start(bf16[160,256]{1,0:T(8,128)(2,1)} %get-tuple-element.96), channel_id=1, source_target_pairs={{0,5},{1,4},{2,7},{3,6},{4,1},{5,0},{6,3},{7,2},{8,13},{9,12},{10,... | collective-permute-start | bytes 245768 | tf_op jit(solution)/shard_map/ppermute | solution.py:451
  61.5 17.3 %collective-permute-start.11 = (bf16[160,256]{1,0:T(8,128)(2,1)}, bf16[160,256]{1,0:T(8,128)(2,1)S(1)}, u32[]{:S(2)}, u32[]{:S(2)}) collective-permute-start(bf16[160,256]{1,0:T(8,128)(2,1)} %get-tuple-element.97), channel_id=1, source_target_pairs={{0,6},{1,7},{2,4},{3,5},{4,2},{5,3},{6,0},{7,1},{8,14},{9,15},{10,... | collective-permute-start | bytes 245768 | tf_op jit(solution)/shard_map/ppermute | solution.py:451
  64.3 16.8 %collective-permute-start.12 = (bf16[160,256]{1,0:T(8,128)(2,1)}, bf16[160,256]{1,0:T(8,128)(2,1)S(1)}, u32[]{:S(2)}, u32[]{:S(2)}) collective-permute-start(bf16[160,256]{1,0:T(8,128)(2,1)} %get-tuple-element.98), channel_id=1, source_target_pairs={{0,7},{1,6},{2,5},{3,4},{4,3},{5,2},{6,1},{7,0},{8,15},{9,14},{10,... | collective-permute-start | bytes 245768 | tf_op jit(solution)/shard_map/ppermute | solution.py:451
  77.0 7.9 %collective-permute-start.24 = (bf16[96,384]{1,0:T(8,128)(2,1)}, bf16[96,384]{1,0:T(8,128)(2,1)S(1)}, u32[]{:S(2)}, u32[]{:S(2)}) collective-permute-start(bf16[96,384]{1,0:T(8,128)(2,1)} %get-tuple-element.117), channel_id=1, source_target_pairs={{0,2},{1,3},{2,0},{3,1},{4,6},{5,7},{6,4},{7,5},{8,10},{9,11},{10,... | collective-permute-start | bytes 221192 | tf_op jit(solution)/shard_map/ppermute | solution.py:451
  77.0 8.0 %collective-permute-start.25 = (bf16[96,384]{1,0:T(8,128)(2,1)}, bf16[96,384]{1,0:T(8,128)(2,1)S(1)}, u32[]{:S(2)}, u32[]{:S(2)}) collective-permute-start(bf16[96,384]{1,0:T(8,128)(2,1)} %get-tuple-element.118), channel_id=1, source_target_pairs={{0,3},{1,2},{2,1},{3,0},{4,7},{5,6},{6,5},{7,4},{8,11},{9,10},{10,... | collective-permute-start | bytes 221192 | tf_op jit(solution)/shard_map/ppermute | solution.py:451
  81.1 11.8 %collective-permute-start.27 = (bf16[96,384]{1,0:T(8,128)(2,1)}, bf16[96,384]{1,0:T(8,128)(2,1)S(1)}, u32[]{:S(2)}, u32[]{:S(2)}) collective-permute-start(bf16[96,384]{1,0:T(8,128)(2,1)} %get-tuple-element.120), channel_id=1, source_target_pairs={{0,5},{1,4},{2,7},{3,6},{4,1},{5,0},{6,3},{7,2},{8,13},{9,12},{10,... | collective-permute-start | bytes 221192 | tf_op jit(solution)/shard_map/ppermute | solution.py:451
  81.4 11.6 %collective-permute-start.28 = (bf16[96,384]{1,0:T(8,128)(2,1)}, bf16[96,384]{1,0:T(8,128)(2,1)S(1)}, u32[]{:S(2)}, u32[]{:S(2)}) collective-permute-start(bf16[96,384]{1,0:T(8,128)(2,1)} %get-tuple-element.121), channel_id=1, source_target_pairs={{0,6},{1,7},{2,4},{3,5},{4,2},{5,3},{6,0},{7,1},{8,14},{9,15},{10,... | collective-permute-start | bytes 221192 | tf_op jit(solution)/shard_map/ppermute | solution.py:451
  84.9 8.1 %collective-permute-start.29 = (bf16[96,384]{1,0:T(8,128)(2,1)}, bf16[96,384]{1,0:T(8,128)(2,1)S(1)}, u32[]{:S(2)}, u32[]{:S(2)}) collective-permute-start(bf16[96,384]{1,0:T(8,128)(2,1)} %get-tuple-element.122), channel_id=1, source_target_pairs={{0,7},{1,6},{2,5},{3,4},{4,3},{5,2},{6,1},{7,0},{8,15},{9,14},{10,... | collective-permute-start | bytes 221192 | tf_op jit(solution)/shard_map/ppermute | solution.py:451
  105.5 30.8 %collective-permute-start.30 = (bf16[3,8,5248]{2,1,0:T(8,128)(2,1)}, bf16[3,8,5248]{2,1,0:T(8,128)(2,1)S(1)}, u32[]{:S(2)}, u32[]{:S(2)}) collective-permute-start(bf16[3,8,5248]{2,1,0:T(8,128)(2,1)} %forward.3.refs_0_), channel_id=1, source_target_pairs={{0,8},{8,0},{16,24},{24,16},{1,9},{9,1},{17,25},{25,17},{2,10},{10... | collective-permute-start | bytes 755720 | tf_op jit(solution)/shard_map/ppermute | solution.py:451
  107.0 6.4 %collective-permute-start.13 = (bf16[64,384]{1,0:T(8,128)(2,1)S(1)}, bf16[64,384]{1,0:T(8,128)(2,1)S(1)}, u32[]{:S(2)}, u32[]{:S(2)}) collective-permute-start(bf16[64,384]{1,0:T(8,128)(2,1)S(1)} %copy-done.11), channel_id=1, source_target_pairs={{0,1},{1,0},{2,3},{3,2},{4,5},{5,4},{6,7},{7,6},{8,9},{9,8},{10,11... | collective-permute-start | bytes 147464 | tf_op jit(solution)/shard_map/ppermute | solution.py:451
  107.0 6.4 %collective-permute-start.14 = (bf16[64,384]{1,0:T(8,128)(2,1)S(1)}, bf16[64,384]{1,0:T(8,128)(2,1)S(1)}, u32[]{:S(2)}, u32[]{:S(2)}) collective-permute-start(bf16[64,384]{1,0:T(8,128)(2,1)S(1)} %copy-done.10), channel_id=1, source_target_pairs={{0,2},{1,3},{2,0},{3,1},{4,6},{5,7},{6,4},{7,5},{8,10},{9,11},{10,... | collective-permute-start | bytes 147464 | tf_op jit(solution)/shard_map/ppermute | solution.py:451
  113.4 24.4 %collective-permute-start.31 = (bf16[3,8,5248]{2,1,0:T(8,128)(2,1)}, bf16[3,8,5248]{2,1,0:T(8,128)(2,1)S(1)}, u32[]{:S(2)}, u32[]{:S(2)}) collective-permute-start(bf16[3,8,5248]{2,1,0:T(8,128)(2,1)} %forward.3.refs_0_), channel_id=1, source_target_pairs={{0,16},{8,24},{16,0},{24,8},{1,17},{9,25},{17,1},{25,9},{2,18},{10... | collective-permute-start | bytes 755720 | tf_op jit(solution)/shard_map/ppermute | solution.py:451
  115.0 22.8 %collective-permute-start.32 = (bf16[3,8,5248]{2,1,0:T(8,128)(2,1)}, bf16[3,8,5248]{2,1,0:T(8,128)(2,1)S(1)}, u32[]{:S(2)}, u32[]{:S(2)}) collective-permute-start(bf16[3,8,5248]{2,1,0:T(8,128)(2,1)} %forward.3.refs_0_), channel_id=1, source_target_pairs={{0,24},{8,16},{16,8},{24,0},{1,25},{9,17},{17,9},{25,1},{2,26},{10... | collective-permute-start | bytes 755720 | tf_op jit(solution)/shard_map/ppermute | solution.py:451
  134.3 15.2 %collective-permute-start.20 = (bf16[2,8,5248]{2,1,0:T(8,128)(2,1)}, bf16[2,8,5248]{2,1,0:T(8,128)(2,1)S(1)}, u32[]{:S(2)}, u32[]{:S(2)}) collective-permute-start(bf16[2,8,5248]{2,1,0:T(8,128)(2,1)} %forward.2.refs_0_), channel_id=1, source_target_pairs={{0,8},{8,0},{16,24},{24,16},{1,9},{9,1},{17,25},{25,17},{2,10},{10... | collective-permute-start | bytes 503816 | tf_op jit(solution)/shard_map/ppermute | solution.py:451
  134.9 14.6 %collective-permute-start.21 = (bf16[2,8,5248]{2,1,0:T(8,128)(2,1)}, bf16[2,8,5248]{2,1,0:T(8,128)(2,1)S(1)}, u32[]{:S(2)}, u32[]{:S(2)}) collective-permute-start(bf16[2,8,5248]{2,1,0:T(8,128)(2,1)} %forward.2.refs_0_), channel_id=1, source_target_pairs={{0,16},{8,24},{16,0},{24,8},{1,17},{9,25},{17,1},{25,9},{2,18},{10... | collective-permute-start | bytes 503816 | tf_op jit(solution)/shard_map/ppermute | solution.py:451
  136.4 13.1 %collective-permute-start.22 = (bf16[2,8,5248]{2,1,0:T(8,128)(2,1)}, bf16[2,8,5248]{2,1,0:T(8,128)(2,1)S(1)}, u32[]{:S(2)}, u32[]{:S(2)}) collective-permute-start(bf16[2,8,5248]{2,1,0:T(8,128)(2,1)} %forward.2.refs_0_), channel_id=1, source_target_pairs={{0,24},{8,16},{16,8},{24,0},{1,25},{9,17},{17,9},{25,1},{2,26},{10... | collective-permute-start | bytes 503816 | tf_op jit(solution)/shard_map/ppermute | solution.py:451
  (22 other events, 312.8 us)

commit v5 on v4

--- a/solution.py
+++ b/solution.py
@@ -134,9 +134,9 @@
     )(couples)
 
 
-def fourier_call(place, here, waves, pieces, peers, cuts):
+def fourier_call(place, here, waves, pieces, peers, wanted):
     parts = len(pieces)
-    total_outs = peers * len(cuts)
+    total_outs = len(wanted)
     rows, lons = pieces[0].shape
     columns = waves.shape[0]
     block = columns // peers
@@ -161,10 +161,9 @@
 
         @pl.when(step == steps - 1)
         def _():
-            for number, (first, size) in enumerate(cuts):
-                for e in range(peers):
-                    start = jnp.bitwise_xor(here_ref[0], e) * block + first
-                    outs[number * peers + e][...] = total[pl.ds(pl.multiple_of(start, 32), size)]
+            for out, (e, first, size) in zip(outs, wanted):
+                start = jnp.bitwise_xor(here_ref[0], e) * block + first
+                out[...] = total[pl.ds(pl.multiple_of(start, 32), size)]
 
     return pl.pallas_call(
         body,
@@ -175,14 +174,10 @@
             in_specs=[pl.BlockSpec((share, parts * lons), lambda i, *_: (i, 0))]
             + [pl.BlockSpec((rows, lons), lambda i, *_: (0, 0))]
             + [pl.BlockSpec(memory_space=pltpu.VMEM)] * (parts - 1),
-            out_specs=[
-                pl.BlockSpec((size, rows), lambda i, *_: (0, 0)) for _, size in cuts for _ in range(peers)
-            ],
+            out_specs=[pl.BlockSpec((size, rows), lambda i, *_: (0, 0)) for _, _, size in wanted],
             scratch_shapes=[pltpu.VMEM((rows, parts * lons), BF), pltpu.VMEM((columns, rows), BF)],
         ),
-        out_shape=[
-            jax.ShapeDtypeStruct((size, rows), BF) for _, size in cuts for _ in range(peers)
-        ],
+        out_shape=[jax.ShapeDtypeStruct((size, rows), BF) for _, _, size in wanted],
     )(place, here, waves, *in_vmem(pieces))
 
 
@@ -220,8 +215,9 @@
 def forward_call(pairs, here, received, chunks, table, quadrature, first, groups):
     row_total, _, half_lat = table.shape
     wave_count = row_total - 1
-    bands = len(received[0][1])
-    shares = [block for _, blocks in received for block in in_vmem(blocks)]
+    bands = len(received[0])
+    begins = [[begin for begin, _ in parts] for parts in received]
+    shares = [block for parts in received for block in in_vmem([block for _, block in parts])]
     units = chunks[-1][1]
     row_block = GROUP * 4
     fields = LANE // SUB
@@ -238,9 +234,9 @@
         recv = refs[len(shares) + 4 :]
         group = pl.program_id(0) + first
         for number in range(len(chunks)):
-            start = group * row_block - received[number][0]
-            mine = pl.ds(pl.multiple_of(start, row_block), row_block)
             for e in range(bands):
+                start = group * row_block - begins[number][e]
+                mine = pl.ds(pl.multiple_of(start, row_block), row_block)
                 band = jnp.bitwise_xor(here_ref[0], e)
                 recv[number][band] = shared[number * bands + e][mine]
         lane = lax.broadcasted_iota(jnp.int32, (row_block, LANE), 1)
@@ -332,7 +328,7 @@
     hot = (level[:, None] == jnp.arange(levels)[None, :]).astype(BF)
     spread = jnp.dot(jnp.dot(hot, operator, preferred_element_type=F32).astype(BF), hot.T,
                      preferred_element_type=F32)
-    return jnp.where(rest[:, None] == rest[None, :], spread, 0.0).astype(BF), level
+    return jnp.where(rest[:, None] == rest[None, :], spread, 0.0).astype(BF)
 
 
 def inverse_call(pairs, place, gathered, project, rebuild, factors, table, first, before):
@@ -348,11 +344,11 @@
     def body(pairs_ref, place_ref, *refs):
         got = refs[:lev]
         p_ref, r_ref, f_ref, table_ref = refs[lev : lev + 4]
-        out, stack, x_ref = refs[-3:]
+        out, stack, damping, x_ref = refs[-4:]
         group = pl.program_id(0) + first
         for d in range(lev):
             part = got[d][0 if d == 0 else pl.program_id(0)]
-            stack[jnp.bitwise_xor(place_ref[0], d)] = part.astype(F32)
+            stack[jnp.bitwise_xor(place_ref[0], d)] = part
         lane = lax.broadcasted_iota(jnp.int32, (1, lanes), 1)
         place = lane // GROUP
         half = wave_count // 2
@@ -360,18 +356,32 @@
             place < half, 2 * place, jnp.where(place < 2 * half, 2 * (place - half) + 1, wave_count)
         )
         low = by_slot(lane % GROUP, pairs_ref, group)
-        degree = jnp.where(r >= wave_count - low, r - 1, low + r).astype(F32)
+        second = r >= wave_count - low
+        codes = 2 * (lane % GROUP) + second.astype(jnp.int32)
+        degree = jnp.where(second, r - 1, low + r).astype(F32)
         factor = degree * (degree + 1.0) / float(wave_count * wave_count)
-        damping = 1.0 / (1.0 + factor * f_ref[:, 0:1])
-        values = stack[...].reshape(n, lanes).astype(BF)
+        levels = lev * own
+        level = lax.broadcasted_iota(jnp.int32, (levels, 1), 0)
+        coefficient = jnp.full((levels, 1), f_ref[0], F32)
+        for q in range(1, levels):
+            coefficient = jnp.where(level == q, f_ref[q], coefficient)
+        damping[...] = 1.0 / (1.0 + factor * coefficient)
+        values = stack[...].reshape(n, lanes)
         modes = jnp.dot(p_ref[...], values, preferred_element_type=F32)
-        damped = (modes * damping).astype(BF)
+        own_level = lax.broadcasted_iota(jnp.int32, (eight, 1), 0) // 2 % own
+        damped = []
+        for owner in range(lev):
+            rate = damping[owner * own : owner * own + 1]
+            for q in range(1, own):
+                rate = jnp.where(own_level == q, damping[owner * own + q : owner * own + q + 1], rate)
+            damped.append(modes[owner * eight : (owner + 1) * eight] * rate)
+        damped = jnp.concatenate(damped, axis=0).astype(BF)
         x_ref[...] = jnp.dot(r_ref[...], damped, preferred_element_type=F32).astype(BF)
         whole = table_ref[0:wave_count].reshape(wave_count // 2, 2, GROUP, half_lat)
         sums = []
         for par in range(2):
             value = x_ref[:, par * per : (par + 1) * per].astype(F32)
-            code = part_code(pairs_ref, group, wave_count, 0, par, per)
+            code = codes[:, par * per : (par + 1) * per]
             spread = jnp.concatenate(
                 [jnp.where(code == b, value, 0.0) for b in range(2 * GROUP)], axis=0
             ).astype(BF)
@@ -424,7 +434,7 @@
             + [
                 pl.BlockSpec((n, n), lambda g, *_: (0, 0)),
                 pl.BlockSpec((eight, n), lambda g, p, q: (q[0], 0)),
-                pl.BlockSpec((n, LANE), lambda g, *_: (0, 0)),
+                pl.BlockSpec(memory_space=pltpu.SMEM),
                 pl.BlockSpec((row_total, GROUP, half_lat), lambda g, *_: (0, first + g, 0)),
             ]
             + [pl.BlockSpec(memory_space=pl.ANY)] * len(more),
@@ -432,7 +442,8 @@
                 (2, own, GROUP, 2, 2, 2 * half_lat), lambda g, *_: (0, 0, first + g, 0, 0, 0)
             ),
             scratch_shapes=[
-                pltpu.VMEM((lev, eight, lanes), F32),
+                pltpu.VMEM((lev, eight, lanes), BF),
+                pltpu.VMEM((lev * own, lanes), F32),
                 pltpu.VMEM((eight, lanes), BF),
             ],
         ),
@@ -445,11 +456,14 @@
     return [arrays[0]] + [pltpu.with_memory_space_constraint(x, pltpu.VMEM) for x in arrays[1:]]
 
 
+def send(block, axis, bits):
+    if bits == 0:
+        return block
+    return lax.ppermute(block, axis, [(i, i ^ bits) for i in range(lax.axis_size(axis))])
+
+
 def swap(blocks, axis):
-    count = len(blocks)
-    return [blocks[0]] + [
-        lax.ppermute(blocks[d], axis, [(i, i ^ d) for i in range(count)]) for d in range(1, count)
-    ]
+    return [send(block, axis, d) for d, block in enumerate(blocks)]
 
 
 def tiled_local(u, v, t, operator, quadrature, table, couples, project, rebuild, factors):
@@ -477,26 +491,33 @@
             blocks, late = lax.optimization_barrier((blocks, late))
         pieces = [x.reshape((hi - lo) * LANE, lons) for x in blocks]
         ending = hi == CHUNKS[-1][1]
-        cuts = [(first * rows, count * rows) for first, count in parts]
-        cuts = cuts if ending else [(0, groups * rows)]
-        blocks = fourier_call(place, here, waves, pieces, lat, cuts)
+        near = lat // 2 if ending else lat
+        wanted = [(e, 0, groups * rows) for e in range(near)]
+        for first, count in parts if ending else ():
+            wanted += [(e, first * rows, count * rows) for e in range(near, lat)]
+        blocks = fourier_call(place, here, waves, pieces, lat, wanted)
         if lo == 0:
             blocks, late = lax.optimization_barrier(
-                (blocks, (couples, quadrature, project, rebuild, factors))
+                (blocks, (couples, quadrature, project, rebuild))
             )
-            late_couples, late_quadrature, project, rebuild, factors = late
+            late_couples, late_quadrature, project, rebuild = late
             pairs = lax.dynamic_slice_in_dim(
                 late_couples, lax.axis_index("lat") * slots, slots
             )
-            to_modes, level = mix_matrix(project, own)
-            to_levels, _ = mix_matrix(rebuild, own)
-            factor_rows = jnp.broadcast_to(factors[level][:, None], (level.shape[0], LANE))
-            late = (pairs, late_quadrature[None, :], to_modes, to_levels, factor_rows)
+            to_modes = mix_matrix(project, own)
+            to_levels = mix_matrix(rebuild, own)
+            late = (pairs, late_quadrature[None, :], to_modes, to_levels)
+        whole = [(0, send(blocks[e], "lat", e)) for e in range(near)]
         shares = []
-        for number, (first, _) in enumerate(cuts):
-            shares.append((first, swap(blocks[number * lat : (number + 1) * lat], "lat")))
+        for number in range(len(parts) if ending else 1):
+            at = slice(near + number * (lat - near), near + (number + 1) * (lat - near))
+            rest = [
+                (first, send(block, "lat", e))
+                for block, (e, first, _) in zip(blocks[at], wanted[at])
+            ]
+            shares.append(whole + rest)
         received.append(shares)
-    pairs, quadrature, to_modes, to_levels, factor_rows = late
+    pairs, quadrature, to_modes, to_levels = late
     gathered = []
     for number, (first, count) in enumerate(parts):
         shares = [each[number if len(each) > 1 else 0] for each in received]
@@ -505,7 +526,7 @@
     result = None
     for (first, _), blocks in zip(parts, gathered):
         result = inverse_call(
-            pairs, place, blocks, to_modes, to_levels, factor_rows, flat, first, result
+            pairs, place, blocks, to_modes, to_levels, factors, flat, first, result
         )
     return result
 

time: 158 us -> 134 us (0.85)
  waiting for transfers between devices: 37.8 us -> 23.6 us
  starting transfers between devices: 45.2 us -> 37.3 us
    ppermute x33 -> x30, waiting for transfers between devices: 37.8 us -> 23.6 us  [send(): lax.ppermute(block, axis, [(i, i ^ bits) for i in range(lax.axis_size(axi...]
    ppermute x33 -> x30, starting transfers between devices: 45.2 us -> 37.3 us  [send(): lax.ppermute(block, axis, [(i, i ^ bits) for i in range(lax.axis_size(axi...]
  transfers between devices with their start and end apart: 33 -> 30, of which waited for: 6 -> 9; matrix products, arithmetic and copies ran while one was open for 3% -> 3% of each run, Pallas kernels for 29% -> 34%
where the time goes in v5:
time: 134 us
  Pallas kernels  69.3 us (52%)
  starting transfers between devices  37.3 us (28%)
  waiting for transfers between devices  23.6 us (18%)
  local copies, waits for them, and re-layouts  1.9 us (1%)
  matrix products  1.79 us (1%)
    ppermute x30, starting transfers between devices, send(): lax.ppermute(block, axis, [(i, i ^ bits) for i in range(lax.axis_size(axi...  37.3 us
    ppermute x30, waiting for transfers between devices, send(): lax.ppermute(block, axis, [(i, i ^ bits) for i in range(lax.axis_size(axi...  23.6 us
    pallas_call x2, Pallas kernels, forward_call(): pl.pallas_call(body, name='forward', grid_spec=pltpu.PrefetchScalarGridSp...  22 us
    pallas_call x2, Pallas kernels, inverse_call(): pl.pallas_call(body, name='inverse', grid_spec=pltpu.PrefetchScalarGridSp...  19.6 us
    pallas_call x2, Pallas kernels, fourier_call(): pl.pallas_call(body, name='fourier', grid_spec=pltpu.PrefetchScalarGridSp...  12.2 us
    pallas_call x2, Pallas kernels, products_call(): pl.pallas_call(body, name='products', grid_spec=pltpu.PrefetchScalarGridS...  7.89 us
    pallas_call x1, Pallas kernels, wave_rows_call(): pl.pallas_call(body, name='wave_rows', grid_spec=pltpu.PrefetchScalarGrid...  7.59 us
  transfers between devices with their start and end apart: 30, of which 9 were waited for; matrix products, arithmetic and copies ran while one was open for 3% of the time, Pallas kernels for 34%

profile of v5, /device:TPU:0, one launch (start us, length us, event | category | flops | bytes accessed | tf_op | source)
XLA Modules:
  0.0 134.0 jit_solution(6822232851246141421)
XLA Ops:
  0.0 3.3 %products.3 = (bf16[2,4,32,640]{3,2,1,0:T(8,128)(2,1)}, bf16[2,4,32,640]{3,2,1,0:T(8,128)(2,1)}, bf16[2,4,32,640]{3,2,1,0:T(8,128)(2,1)}, bf16[2,4,32,640]{3,2,1,0:T(8,128)(2,1)}) custom-call(s32[1]{0:T(128)} %bitcast.place_ref, bf16[8,8]{1,0:T(8,128)(2,1)} %op_ref.3, bf16[8,160,640]{2,1,0:T(8,128)(2,1)} %u_ref.3, bf16[8,160,640]{2,1,0:T(8,128)(2,1)} %v_ref.3, ...), custom_call_target="tpu_custom_call" | custom-call | tf_op jit(solution)/shard_map/products/pallas_call | solution.py:52
  3.3 3.0 %collective-permute-start.3 = (bf16[2,4,32,640]{3,2,1,0:T(8,128)(2,1)}, bf16[2,4,32,640]{3,2,1,0:T(8,128)(2,1)S(1)}, u32[]{:S(2)}, u32[]{:S(2)}) collective-permute-start(bf16[2,4,32,640]{3,2,1,0:T(8,128)(2,1)} %get-tuple-element.68), channel_id=1, source_target_pairs={{0,8},{8,0},{16,24},{24,16},{1,9},{9,1},{17,25},{25,17},{2,10},{10... | collective-permute-start | bytes 983048 | tf_op jit(solution)/shard_map/ppermute | solution.py:462
  7.8 4.6 %products.2 = (bf16[3,4,32,640]{3,2,1,0:T(8,128)(2,1)}, bf16[3,4,32,640]{3,2,1,0:T(8,128)(2,1)}, bf16[3,4,32,640]{3,2,1,0:T(8,128)(2,1)}, bf16[3,4,32,640]{3,2,1,0:T(8,128)(2,1)}) custom-call(s32[1]{0:T(128)} %bitcast.place_ref, bf16[8,8]{1,0:T(8,128)(2,1)} %op_ref.3, bf16[8,160,640]{2,1,0:T(8,128)(2,1)} %u_ref.3, bf16[8,160,640]{2,1,0:T(8,128)(2,1)} %v_ref.3, ...), custom_call_target="tpu_custom_call" | custom-call | tf_op jit(solution)/shard_map/products/pallas_call | solution.py:52
  12.4 1.9 %collective-permute-start = (bf16[3,4,32,640]{3,2,1,0:T(8,128)(2,1)}, bf16[3,4,32,640]{3,2,1,0:T(8,128)(2,1)S(1)}, u32[]{:S(2)}, u32[]{:S(2)}) collective-permute-start(bf16[3,4,32,640]{3,2,1,0:T(8,128)(2,1)} %get-tuple-element.63), channel_id=1, source_target_pairs={{0,8},{8,0},{16,24},{24,16},{1,9},{9,1},{17,25},{25,17},{2,10},{10... | collective-permute-start | bytes 1474568 | tf_op jit(solution)/shard_map/ppermute | solution.py:462
  15.9 2.2 %collective-permute-start.2 = (bf16[3,4,32,640]{3,2,1,0:T(8,128)(2,1)}, bf16[3,4,32,640]{3,2,1,0:T(8,128)(2,1)S(1)}, u32[]{:S(2)}, u32[]{:S(2)}) collective-permute-start(bf16[3,4,32,640]{3,2,1,0:T(8,128)(2,1)} %get-tuple-element.65), channel_id=1, source_target_pairs={{0,24},{8,16},{16,8},{24,0},{1,25},{9,17},{17,9},{25,1},{2,26},{10... | collective-permute-start | bytes 1474568 | tf_op jit(solution)/shard_map/ppermute | solution.py:462
  18.0 7.6 %wave_rows.1.w_ref = bf16[1280,2560]{1,0:T(8,128)(2,1)} custom-call(s32[320]{0:T(512)} %couples_ref), custom_call_target="tpu_custom_call" | custom-call | tf_op jit(solution)/shard_map/wave_rows/pallas_call | solution.py:124
  25.7 5.1 %fourier.2 = (bf16[160,256]{1,0:T(8,128)(2,1)}, bf16[160,256]{1,0:T(8,128)(2,1)}, bf16[160,256]{1,0:T(8,128)(2,1)}, bf16[160,256]{1,0:T(8,128)(2,1)}, bf16[160,2...) custom-call(s32[1]{0:T(128)} %bitcast.place_ref, ...), custom_call_target="tpu_custom_call" | custom-call | tf_op jit(solution)/shard_map/fourier/pallas_call | solution.py:168
  33.6 2.2 %collective-permute-done.7.refs_2_ = bf16[160,256]{1,0:T(8,128)(2,1)S(1)} collective-permute-done((bf16[160,256]{1,0:T(8,128)(2,1)}, bf16[160,256]{1,0:T(8,128)(2,1)S(1)}, u32[]{:S(2)}, u32[]{:S(2)}) %collective-permute-start.7) | collective-permute-done | bytes 81952 | tf_op jit(solution)/shard_map/ppermute | solution.py:462
  35.9 2.6 %collective-permute-start.9 = (bf16[160,256]{1,0:T(8,128)(2,1)}, bf16[160,256]{1,0:T(8,128)(2,1)S(1)}, u32[]{:S(2)}, u32[]{:S(2)}) collective-permute-start(bf16[160,256]{1,0:T(8,128)(2,1)} %get-tuple-element.88), channel_id=1, source_target_pairs={{0,4},{1,5},{2,6},{3,7},{4,0},{5,1},{6,2},{7,3},{8,12},{9,13},{10,... | collective-permute-start | bytes 245768 | tf_op jit(solution)/shard_map/ppermute | solution.py:462
  38.5 5.3 %collective-permute-done.1 = bf16[3,4,32,640]{3,2,1,0:T(8,128)(2,1)S(1)} collective-permute-done((bf16[3,4,32,640]{3,2,1,0:T(8,128)(2,1)}, bf16[3,4,32,640]{3,2,1,0:T(8,128)(2,1)S(1)}, u32[]{:S(2)}, u32[]{:S(2)}) %collective-permute-start.1) | collective-permute-done | bytes 491552 | tf_op jit(solution)/shard_map/ppermute | solution.py:462
  43.8 3.6 %collective-permute-start.11 = (bf16[160,256]{1,0:T(8,128)(2,1)}, bf16[160,256]{1,0:T(8,128)(2,1)S(1)}, u32[]{:S(2)}, u32[]{:S(2)}) collective-permute-start(bf16[160,256]{1,0:T(8,128)(2,1)} %get-tuple-element.90), channel_id=1, source_target_pairs={{0,6},{1,7},{2,4},{3,5},{4,2},{5,3},{6,0},{7,1},{8,14},{9,15},{10,... | collective-permute-start | bytes 245768 | tf_op jit(solution)/shard_map/ppermute | solution.py:462
  50.1 7.0 %fourier.3 = (bf16[160,384]{1,0:T(8,128)(2,1)}, bf16[160,384]{1,0:T(8,128)(2,1)}, bf16[160,384]{1,0:T(8,128)(2,1)}, bf16[160,384]{1,0:T(8,128)(2,1)}, bf16[96,38...) custom-call(s32[1]{0:T(128)} %bitcast.place_ref, ...), custom_call_target="tpu_custom_call" | custom-call | tf_op jit(solution)/shard_map/fourier/pallas_call | solution.py:168
  57.3 2.6 %collective-permute-start.24 = (bf16[96,384]{1,0:T(8,128)(2,1)}, bf16[96,384]{1,0:T(8,128)(2,1)S(1)}, u32[]{:S(2)}, u32[]{:S(2)}) collective-permute-start(bf16[96,384]{1,0:T(8,128)(2,1)} %get-tuple-element.108), channel_id=1, source_target_pairs={{0,5},{1,4},{2,7},{3,6},{4,1},{5,0},{6,3},{7,2},{8,13},{9,12},{10,... | collective-permute-start | bytes 221192 | tf_op jit(solution)/shard_map/ppermute | solution.py:462
  61.7 3.5 %collective-permute-done.23.refs_12_ = bf16[96,384]{1,0:T(8,128)(2,1)S(1)} collective-permute-done((bf16[96,384]{1,0:T(8,128)(2,1)}, bf16[96,384]{1,0:T(8,128)(2,1)S(1)}, u32[]{:S(2)}, u32[]{:S(2)}) %collective-permute-start.23) | collective-permute-done | bytes 73760 | tf_op jit(solution)/shard_map/ppermute | solution.py:462
  65.3 1.7 %collective-permute-done.24.refs_13_ = bf16[96,384]{1,0:T(8,128)(2,1)S(1)} collective-permute-done((bf16[96,384]{1,0:T(8,128)(2,1)}, bf16[96,384]{1,0:T(8,128)(2,1)S(1)}, u32[]{:S(2)}, u32[]{:S(2)}) %collective-permute-start.24) | collective-permute-done | bytes 73760 | tf_op jit(solution)/shard_map/ppermute | solution.py:462
  68.2 5.1 %collective-permute-done.25.refs_14_ = bf16[96,384]{1,0:T(8,128)(2,1)S(1)} collective-permute-done((bf16[96,384]{1,0:T(8,128)(2,1)}, bf16[96,384]{1,0:T(8,128)(2,1)S(1)}, u32[]{:S(2)}, u32[]{:S(2)}) %collective-permute-start.25) | collective-permute-done | bytes 73760 | tf_op jit(solution)/shard_map/ppermute | solution.py:462
  73.7 12.5 %forward.3.refs_0_ = bf16[3,8,5248]{2,1,0:T(8,128)(2,1)} custom-call(s32[40]{0:T(128)} %dynamic_slice.3.pairs_ref, s32[1]{0:T(128)} %bitcast.1.here_ref, bf16[160,256]{1,0:T(8,128)(2,1)} %get-tuple-element.84.refs_0_, bf16[160,256]{1,0:T(8,128)(2,1)S(1)} %collective-permute-done.6.refs_1_, bf16[160,256]{1,0:T(8,128)(2,1)S(1)} %collective-permute-done.7.refs_2_, ...), custom_call_target="tpu_custom_call" | custom-call | tf_op jit(solution)/shard_map/forward/pallas_call | solution.py:298
  87.9 1.9 %collective-permute-start.17 = (bf16[64,384]{1,0:T(8,128)(2,1)S(1)}, bf16[64,384]{1,0:T(8,128)(2,1)S(1)}, u32[]{:S(2)}, u32[]{:S(2)}) collective-permute-start(bf16[64,384]{1,0:T(8,128)(2,1)S(1)} %copy-done.4), channel_id=1, source_target_pairs={{0,5},{1,4},{2,7},{3,6},{4,1},{5,0},{6,3},{7,2},{8,13},{9,12},{10,... | collective-permute-start | bytes 147464 | tf_op jit(solution)/shard_map/ppermute | solution.py:462
  93.2 1.8 %collective-permute-start.18 = (bf16[64,384]{1,0:T(8,128)(2,1)S(1)}, bf16[64,384]{1,0:T(8,128)(2,1)S(1)}, u32[]{:S(2)}, u32[]{:S(2)}) collective-permute-start(bf16[64,384]{1,0:T(8,128)(2,1)S(1)} %copy-done.3), channel_id=1, source_target_pairs={{0,6},{1,7},{2,4},{3,5},{4,2},{5,3},{6,0},{7,1},{8,14},{9,15},{10,... | collective-permute-start | bytes 147464 | tf_op jit(solution)/shard_map/ppermute | solution.py:462
  96.2 2.9 %collective-permute-done.18.refs_14_ = bf16[64,384]{1,0:T(8,128)(2,1)S(1)} collective-permute-done((bf16[64,384]{1,0:T(8,128)(2,1)S(1)}, bf16[64,384]{1,0:T(8,128)(2,1)S(1)}, u32[]{:S(2)}, u32[]{:S(2)}) %collective-permute-start.18) | collective-permute-done | bytes 49184 | tf_op jit(solution)/shard_map/ppermute | solution.py:462
  100.6 9.5 %forward.2.refs_0_ = bf16[2,8,5248]{2,1,0:T(8,128)(2,1)} custom-call(s32[40]{0:T(128)} %dynamic_slice.3.pairs_ref, s32[1]{0:T(128)} %bitcast.1.here_ref, bf16[160,256]{1,0:T(8,128)(2,1)} %get-tuple-element.84.refs_0_, bf16[160,256]{1,0:T(8,128)(2,1)S(1)} %collective-permute-done.6.refs_1_, bf16[160,256]{1,0:T(8,128)(2,1)S(1)} %collective-permute-done.7.refs_2_, ...), custom_call_target="tpu_custom_call" | custom-call | tf_op jit(solution)/shard_map/forward/pallas_call | solution.py:298
  110.1 2.8 %collective-permute-start.20 = (bf16[2,8,5248]{2,1,0:T(8,128)(2,1)}, bf16[2,8,5248]{2,1,0:T(8,128)(2,1)S(1)}, u32[]{:S(2)}, u32[]{:S(2)}) collective-permute-start(bf16[2,8,5248]{2,1,0:T(8,128)(2,1)} %forward.2.refs_0_), channel_id=1, source_target_pairs={{0,8},{8,0},{16,24},{24,16},{1,9},{9,1},{17,25},{25,17},{2,10},{10... | collective-permute-start | bytes 503816 | tf_op jit(solution)/shard_map/ppermute | solution.py:462
  114.4 11.4 %inverse.2.refs_8_ = f32[2,2,40,2,2,1280]{5,4,3,2,1,0:T(2,128)} custom-call(s32[40]{0:T(128)} %dynamic_slice.3.pairs_ref, s32[1]{0:T(128)} %bitcast.place_ref, bf16[3,8,5248]{2,1,0:T(8,128)(2,1)} %forward.3.refs_0_, bf16[3,8,5248]{2,1,0:T(8,128)(2,1)S(1)} %collective-permute-done.27.refs_1_, bf16[3,8,5248]{2,1,0:T(8,128)(2,1)S(1)} %collective-permute-done.28.refs_2_, ...), custom_call_target="tpu_custom_call" | custom-call | tf_op jit(solution)/shard_map/inverse/pallas_call | solution.py:426
  125.8 8.2 %inverse.3 = f32[2,2,40,2,2,1280]{5,4,3,2,1,0:T(2,128)} custom-call(s32[40]{0:T(128)} %dynamic_slice.3.pairs_ref, s32[1]{0:T(128)} %bitcast.place_ref, bf16[2,8,5248]{2,1,0:T(8,128)(2,1)} %forward.2.refs_0_, bf16[2,8,5248]{2,1,0:T(8,128)(2,1)S(1)} %collective-permute-done.20.refs_1_, ...), custom_call_target="tpu_custom_call", output_to_operand_aliasing={{}: (10, {})} | custom-call | tf_op jit(solution)/shard_map/inverse/pallas_call | solution.py:426
  (64 shorter events, 21.5 us)
Async XLA Ops:
  3.3 12.5 %collective-permute-start.3 = (bf16[2,4,32,640]{3,2,1,0:T(8,128)(2,1)}, bf16[2,4,32,640]{3,2,1,0:T(8,128)(2,1)S(1)}, u32[]{:S(2)}, u32[]{:S(2)}) collective-permute-start(bf16[2,4,32,640]{3,2,1,0:T(8,128)(2,1)} %get-tuple-element.68), channel_id=1, source_target_pairs={{0,8},{8,0},{16,24},{24,16},{1,9},{9,1},{17,25},{25,17},{2,10},{10... | collective-permute-start | bytes 983048 | tf_op jit(solution)/shard_map/ppermute | solution.py:462
  6.3 19.3 %collective-permute-start.4 = (bf16[2,4,32,640]{3,2,1,0:T(8,128)(2,1)}, bf16[2,4,32,640]{3,2,1,0:T(8,128)(2,1)S(1)}, u32[]{:S(2)}, u32[]{:S(2)}) collective-permute-start(bf16[2,4,32,640]{3,2,1,0:T(8,128)(2,1)} %get-tuple-element.69), channel_id=1, source_target_pairs={{0,16},{8,24},{16,0},{24,8},{1,17},{9,25},{17,1},{25,9},{2,18},{10... | collective-permute-start | bytes 983048 | tf_op jit(solution)/shard_map/ppermute | solution.py:462
  7.8 17.8 %collective-permute-start.5 = (bf16[2,4,32,640]{3,2,1,0:T(8,128)(2,1)}, bf16[2,4,32,640]{3,2,1,0:T(8,128)(2,1)S(1)}, u32[]{:S(2)}, u32[]{:S(2)}) collective-permute-start(bf16[2,4,32,640]{3,2,1,0:T(8,128)(2,1)} %get-tuple-element.70), channel_id=1, source_target_pairs={{0,24},{8,16},{16,8},{24,0},{1,25},{9,17},{17,9},{25,1},{2,26},{10... | collective-permute-start | bytes 983048 | tf_op jit(solution)/shard_map/ppermute | solution.py:462
  12.4 26.1 %collective-permute-start = (bf16[3,4,32,640]{3,2,1,0:T(8,128)(2,1)}, bf16[3,4,32,640]{3,2,1,0:T(8,128)(2,1)S(1)}, u32[]{:S(2)}, u32[]{:S(2)}) collective-permute-start(bf16[3,4,32,640]{3,2,1,0:T(8,128)(2,1)} %get-tuple-element.63), channel_id=1, source_target_pairs={{0,8},{8,0},{16,24},{24,16},{1,9},{9,1},{17,25},{25,17},{2,10},{10... | collective-permute-start | bytes 1474568 | tf_op jit(solution)/shard_map/ppermute | solution.py:462
  14.3 29.4 %collective-permute-start.1 = (bf16[3,4,32,640]{3,2,1,0:T(8,128)(2,1)}, bf16[3,4,32,640]{3,2,1,0:T(8,128)(2,1)S(1)}, u32[]{:S(2)}, u32[]{:S(2)}) collective-permute-start(bf16[3,4,32,640]{3,2,1,0:T(8,128)(2,1)} %get-tuple-element.64), channel_id=1, source_target_pairs={{0,16},{8,24},{16,0},{24,8},{1,17},{9,25},{17,1},{25,9},{2,18},{10... | collective-permute-start | bytes 1474568 | tf_op jit(solution)/shard_map/ppermute | solution.py:462
  15.9 31.5 %collective-permute-start.2 = (bf16[3,4,32,640]{3,2,1,0:T(8,128)(2,1)}, bf16[3,4,32,640]{3,2,1,0:T(8,128)(2,1)S(1)}, u32[]{:S(2)}, u32[]{:S(2)}) collective-permute-start(bf16[3,4,32,640]{3,2,1,0:T(8,128)(2,1)} %get-tuple-element.65), channel_id=1, source_target_pairs={{0,24},{8,16},{16,8},{24,0},{1,25},{9,17},{17,9},{25,1},{2,26},{10... | collective-permute-start | bytes 1474568 | tf_op jit(solution)/shard_map/ppermute | solution.py:462
  33.4 23.8 %collective-permute-start.8 = (bf16[160,256]{1,0:T(8,128)(2,1)}, bf16[160,256]{1,0:T(8,128)(2,1)S(1)}, u32[]{:S(2)}, u32[]{:S(2)}) collective-permute-start(bf16[160,256]{1,0:T(8,128)(2,1)} %get-tuple-element.87), channel_id=1, source_target_pairs={{0,3},{1,2},{2,1},{3,0},{4,7},{5,6},{6,5},{7,4},{8,11},{9,10},{10,... | collective-permute-start | bytes 245768 | tf_op jit(solution)/shard_map/ppermute | solution.py:462
  35.9 21.4 %collective-permute-start.9 = (bf16[160,256]{1,0:T(8,128)(2,1)}, bf16[160,256]{1,0:T(8,128)(2,1)S(1)}, u32[]{:S(2)}, u32[]{:S(2)}) collective-permute-start(bf16[160,256]{1,0:T(8,128)(2,1)} %get-tuple-element.88), channel_id=1, source_target_pairs={{0,4},{1,5},{2,6},{3,7},{4,0},{5,1},{6,2},{7,3},{8,12},{9,13},{10,... | collective-permute-start | bytes 245768 | tf_op jit(solution)/shard_map/ppermute | solution.py:462
  38.5 21.4 %collective-permute-start.10 = (bf16[160,256]{1,0:T(8,128)(2,1)}, bf16[160,256]{1,0:T(8,128)(2,1)S(1)}, u32[]{:S(2)}, u32[]{:S(2)}) collective-permute-start(bf16[160,256]{1,0:T(8,128)(2,1)} %get-tuple-element.89), channel_id=1, source_target_pairs={{0,5},{1,4},{2,7},{3,6},{4,1},{5,0},{6,3},{7,2},{8,13},{9,12},{10,... | collective-permute-start | bytes 245768 | tf_op jit(solution)/shard_map/ppermute | solution.py:462
  43.8 16.5 %collective-permute-start.11 = (bf16[160,256]{1,0:T(8,128)(2,1)}, bf16[160,256]{1,0:T(8,128)(2,1)S(1)}, u32[]{:S(2)}, u32[]{:S(2)}) collective-permute-start(bf16[160,256]{1,0:T(8,128)(2,1)} %get-tuple-element.90), channel_id=1, source_target_pairs={{0,6},{1,7},{2,4},{3,5},{4,2},{5,3},{6,0},{7,1},{8,14},{9,15},{10,... | collective-permute-start | bytes 245768 | tf_op jit(solution)/shard_map/ppermute | solution.py:462
  47.4 14.2 %collective-permute-start.12 = (bf16[160,256]{1,0:T(8,128)(2,1)}, bf16[160,256]{1,0:T(8,128)(2,1)S(1)}, u32[]{:S(2)}, u32[]{:S(2)}) collective-permute-start(bf16[160,256]{1,0:T(8,128)(2,1)} %get-tuple-element.91), channel_id=1, source_target_pairs={{0,7},{1,6},{2,5},{3,4},{4,3},{5,2},{6,1},{7,0},{8,15},{9,14},{10,... | collective-permute-start | bytes 245768 | tf_op jit(solution)/shard_map/ppermute | solution.py:462
  57.2 8.0 %collective-permute-start.23 = (bf16[96,384]{1,0:T(8,128)(2,1)}, bf16[96,384]{1,0:T(8,128)(2,1)S(1)}, u32[]{:S(2)}, u32[]{:S(2)}) collective-permute-start(bf16[96,384]{1,0:T(8,128)(2,1)} %get-tuple-element.107), channel_id=1, source_target_pairs={{0,4},{1,5},{2,6},{3,7},{4,0},{5,1},{6,2},{7,3},{8,12},{9,13},{10,... | collective-permute-start | bytes 221192 | tf_op jit(solution)/shard_map/ppermute | solution.py:462
  57.3 9.8 %collective-permute-start.24 = (bf16[96,384]{1,0:T(8,128)(2,1)}, bf16[96,384]{1,0:T(8,128)(2,1)S(1)}, u32[]{:S(2)}, u32[]{:S(2)}) collective-permute-start(bf16[96,384]{1,0:T(8,128)(2,1)} %get-tuple-element.108), channel_id=1, source_target_pairs={{0,5},{1,4},{2,7},{3,6},{4,1},{5,0},{6,3},{7,2},{8,13},{9,12},{10,... | collective-permute-start | bytes 221192 | tf_op jit(solution)/shard_map/ppermute | solution.py:462
  59.8 13.8 %collective-permute-start.13 = (bf16[160,384]{1,0:T(8,128)(2,1)}, bf16[160,384]{1,0:T(8,128)(2,1)S(1)}, u32[]{:S(2)}, u32[]{:S(2)}) collective-permute-start(bf16[160,384]{1,0:T(8,128)(2,1)} %get-tuple-element.97), channel_id=1, source_target_pairs={{0,1},{1,0},{2,3},{3,2},{4,5},{5,4},{6,7},{7,6},{8,9},{9,8},{10,11... | collective-permute-start | bytes 368648 | tf_op jit(solution)/shard_map/ppermute | solution.py:462
  60.3 13.3 %collective-permute-start.14 = (bf16[160,384]{1,0:T(8,128)(2,1)}, bf16[160,384]{1,0:T(8,128)(2,1)S(1)}, u32[]{:S(2)}, u32[]{:S(2)}) collective-permute-start(bf16[160,384]{1,0:T(8,128)(2,1)} %get-tuple-element.98), channel_id=1, source_target_pairs={{0,2},{1,3},{2,0},{3,1},{4,6},{5,7},{6,4},{7,5},{8,10},{9,11},{10,... | collective-permute-start | bytes 368648 | tf_op jit(solution)/shard_map/ppermute | solution.py:462
  61.5 12.1 %collective-permute-start.15 = (bf16[160,384]{1,0:T(8,128)(2,1)}, bf16[160,384]{1,0:T(8,128)(2,1)S(1)}, u32[]{:S(2)}, u32[]{:S(2)}) collective-permute-start(bf16[160,384]{1,0:T(8,128)(2,1)} %get-tuple-element.99), channel_id=1, source_target_pairs={{0,3},{1,2},{2,1},{3,0},{4,7},{5,6},{6,5},{7,4},{8,11},{9,10},{10,... | collective-permute-start | bytes 368648 | tf_op jit(solution)/shard_map/ppermute | solution.py:462
  65.2 8.1 %collective-permute-start.25 = (bf16[96,384]{1,0:T(8,128)(2,1)}, bf16[96,384]{1,0:T(8,128)(2,1)S(1)}, u32[]{:S(2)}, u32[]{:S(2)}) collective-permute-start(bf16[96,384]{1,0:T(8,128)(2,1)} %get-tuple-element.109), channel_id=1, source_target_pairs={{0,6},{1,7},{2,4},{3,5},{4,2},{5,3},{6,0},{7,1},{8,14},{9,15},{10,... | collective-permute-start | bytes 221192 | tf_op jit(solution)/shard_map/ppermute | solution.py:462
  86.2 28.1 %collective-permute-start.27 = (bf16[3,8,5248]{2,1,0:T(8,128)(2,1)}, bf16[3,8,5248]{2,1,0:T(8,128)(2,1)S(1)}, u32[]{:S(2)}, u32[]{:S(2)}) collective-permute-start(bf16[3,8,5248]{2,1,0:T(8,128)(2,1)} %forward.3.refs_0_), channel_id=1, source_target_pairs={{0,8},{8,0},{16,24},{24,16},{1,9},{9,1},{17,25},{25,17},{2,10},{10... | collective-permute-start | bytes 755720 | tf_op jit(solution)/shard_map/ppermute | solution.py:462
  87.9 7.1 %collective-permute-start.17 = (bf16[64,384]{1,0:T(8,128)(2,1)S(1)}, bf16[64,384]{1,0:T(8,128)(2,1)S(1)}, u32[]{:S(2)}, u32[]{:S(2)}) collective-permute-start(bf16[64,384]{1,0:T(8,128)(2,1)S(1)} %copy-done.4), channel_id=1, source_target_pairs={{0,5},{1,4},{2,7},{3,6},{4,1},{5,0},{6,3},{7,2},{8,13},{9,12},{10,... | collective-permute-start | bytes 147464 | tf_op jit(solution)/shard_map/ppermute | solution.py:462
  89.8 24.5 %collective-permute-start.28 = (bf16[3,8,5248]{2,1,0:T(8,128)(2,1)}, bf16[3,8,5248]{2,1,0:T(8,128)(2,1)S(1)}, u32[]{:S(2)}, u32[]{:S(2)}) collective-permute-start(bf16[3,8,5248]{2,1,0:T(8,128)(2,1)} %forward.3.refs_0_), channel_id=1, source_target_pairs={{0,16},{8,24},{16,0},{24,8},{1,17},{9,25},{17,1},{25,9},{2,18},{10... | collective-permute-start | bytes 755720 | tf_op jit(solution)/shard_map/ppermute | solution.py:462
  90.7 23.7 %collective-permute-start.29 = (bf16[3,8,5248]{2,1,0:T(8,128)(2,1)}, bf16[3,8,5248]{2,1,0:T(8,128)(2,1)S(1)}, u32[]{:S(2)}, u32[]{:S(2)}) collective-permute-start(bf16[3,8,5248]{2,1,0:T(8,128)(2,1)} %forward.3.refs_0_), channel_id=1, source_target_pairs={{0,24},{8,16},{16,8},{24,0},{1,25},{9,17},{17,9},{25,1},{2,26},{10... | collective-permute-start | bytes 755720 | tf_op jit(solution)/shard_map/ppermute | solution.py:462
  110.1 15.8 %collective-permute-start.20 = (bf16[2,8,5248]{2,1,0:T(8,128)(2,1)}, bf16[2,8,5248]{2,1,0:T(8,128)(2,1)S(1)}, u32[]{:S(2)}, u32[]{:S(2)}) collective-permute-start(bf16[2,8,5248]{2,1,0:T(8,128)(2,1)} %forward.2.refs_0_), channel_id=1, source_target_pairs={{0,8},{8,0},{16,24},{24,16},{1,9},{9,1},{17,25},{25,17},{2,10},{10... | collective-permute-start | bytes 503816 | tf_op jit(solution)/shard_map/ppermute | solution.py:462
  112.8 13.0 %collective-permute-start.21 = (bf16[2,8,5248]{2,1,0:T(8,128)(2,1)}, bf16[2,8,5248]{2,1,0:T(8,128)(2,1)S(1)}, u32[]{:S(2)}, u32[]{:S(2)}) collective-permute-start(bf16[2,8,5248]{2,1,0:T(8,128)(2,1)} %forward.2.refs_0_), channel_id=1, source_target_pairs={{0,16},{8,24},{16,0},{24,8},{1,17},{9,25},{17,1},{25,9},{2,18},{10... | collective-permute-start | bytes 503816 | tf_op jit(solution)/shard_map/ppermute | solution.py:462
  114.4 11.5 %collective-permute-start.22 = (bf16[2,8,5248]{2,1,0:T(8,128)(2,1)}, bf16[2,8,5248]{2,1,0:T(8,128)(2,1)S(1)}, u32[]{:S(2)}, u32[]{:S(2)}) collective-permute-start(bf16[2,8,5248]{2,1,0:T(8,128)(2,1)} %forward.2.refs_0_), channel_id=1, source_target_pairs={{0,24},{8,16},{16,8},{24,0},{1,25},{9,17},{17,9},{25,1},{2,26},{10... | collective-permute-start | bytes 503816 | tf_op jit(solution)/shard_map/ppermute | solution.py:462
  (13 other events, 177.2 us)

commit v6 on v5

--- a/solution.py
+++ b/solution.py
@@ -486,7 +486,10 @@
     parts = ((0, cut), (cut, groups - cut))
     rows = 4 * GROUP
     for (lo, hi), blocks in zip(CHUNKS, products):
-        blocks = swap(blocks, "lev")
+        came = []
+        for d, block in enumerate(blocks):
+            came.append(send(block, "lev", d))
+        blocks = came
         if lo > 0:
             blocks, late = lax.optimization_barrier((blocks, late))
         pieces = [x.reshape((hi - lo) * LANE, lons) for x in blocks]

time: 134 us -> 134 us (level)
  no operation moved by 1% of the time
where the time goes in v6:
time: 134 us
  Pallas kernels  69.3 us (52%)
  starting transfers between devices  37.3 us (28%)
  waiting for transfers between devices  23.6 us (18%)
  local copies, waits for them, and re-layouts  1.9 us (1%)
  matrix products  1.79 us (1%)
    ppermute x30, starting transfers between devices, send(): lax.ppermute(block, axis, [(i, i ^ bits) for i in range(lax.axis_size(axi...  37.3 us
    ppermute x30, waiting for transfers between devices, send(): lax.ppermute(block, axis, [(i, i ^ bits) for i in range(lax.axis_size(axi...  23.6 us
    pallas_call x2, Pallas kernels, forward_call(): pl.pallas_call(body, name='forward', grid_spec=pltpu.PrefetchScalarGridSp...  22 us
    pallas_call x2, Pallas kernels, inverse_call(): pl.pallas_call(body, name='inverse', grid_spec=pltpu.PrefetchScalarGridSp...  19.6 us
    pallas_call x2, Pallas kernels, fourier_call(): pl.pallas_call(body, name='fourier', grid_spec=pltpu.PrefetchScalarGridSp...  12.2 us
    pallas_call x2, Pallas kernels, products_call(): pl.pallas_call(body, name='products', grid_spec=pltpu.PrefetchScalarGridS...  7.89 us
    pallas_call x1, Pallas kernels, wave_rows_call(): pl.pallas_call(body, name='wave_rows', grid_spec=pltpu.PrefetchScalarGrid...  7.59 us
  transfers between devices with their start and end apart: 30, of which 9 were waited for; matrix products, arithmetic and copies ran while one was open for 3% of the time, Pallas kernels for 34%

profile of v6, /device:TPU:0, one launch (start us, length us, event | category | flops | bytes accessed | tf_op | source)
XLA Modules:
  0.0 134.0 jit_solution(6822232851246141421)
XLA Ops:
  0.0 3.3 %products.3 = (bf16[2,4,32,640]{3,2,1,0:T(8,128)(2,1)}, bf16[2,4,32,640]{3,2,1,0:T(8,128)(2,1)}, bf16[2,4,32,640]{3,2,1,0:T(8,128)(2,1)}, bf16[2,4,32,640]{3,2,1,0:T(8,128)(2,1)}) custom-call(s32[1]{0:T(128)} %bitcast.place_ref, bf16[8,8]{1,0:T(8,128)(2,1)} %op_ref.3, bf16[8,160,640]{2,1,0:T(8,128)(2,1)} %u_ref.3, bf16[8,160,640]{2,1,0:T(8,128)(2,1)} %v_ref.3, ...), custom_call_target="tpu_custom_call" | custom-call | tf_op jit(solution)/shard_map/products/pallas_call | solution.py:52
  3.3 3.0 %collective-permute-start.3 = (bf16[2,4,32,640]{3,2,1,0:T(8,128)(2,1)}, bf16[2,4,32,640]{3,2,1,0:T(8,128)(2,1)S(1)}, u32[]{:S(2)}, u32[]{:S(2)}) collective-permute-start(bf16[2,4,32,640]{3,2,1,0:T(8,128)(2,1)} %get-tuple-element.68), channel_id=1, source_target_pairs={{0,8},{8,0},{16,24},{24,16},{1,9},{9,1},{17,25},{25,17},{2,10},{10... | collective-permute-start | bytes 983048 | tf_op jit(solution)/shard_map/ppermute | solution.py:462
  7.8 4.6 %products.2 = (bf16[3,4,32,640]{3,2,1,0:T(8,128)(2,1)}, bf16[3,4,32,640]{3,2,1,0:T(8,128)(2,1)}, bf16[3,4,32,640]{3,2,1,0:T(8,128)(2,1)}, bf16[3,4,32,640]{3,2,1,0:T(8,128)(2,1)}) custom-call(s32[1]{0:T(128)} %bitcast.place_ref, bf16[8,8]{1,0:T(8,128)(2,1)} %op_ref.3, bf16[8,160,640]{2,1,0:T(8,128)(2,1)} %u_ref.3, bf16[8,160,640]{2,1,0:T(8,128)(2,1)} %v_ref.3, ...), custom_call_target="tpu_custom_call" | custom-call | tf_op jit(solution)/shard_map/products/pallas_call | solution.py:52
  12.4 1.9 %collective-permute-start = (bf16[3,4,32,640]{3,2,1,0:T(8,128)(2,1)}, bf16[3,4,32,640]{3,2,1,0:T(8,128)(2,1)S(1)}, u32[]{:S(2)}, u32[]{:S(2)}) collective-permute-start(bf16[3,4,32,640]{3,2,1,0:T(8,128)(2,1)} %get-tuple-element.63), channel_id=1, source_target_pairs={{0,8},{8,0},{16,24},{24,16},{1,9},{9,1},{17,25},{25,17},{2,10},{10... | collective-permute-start | bytes 1474568 | tf_op jit(solution)/shard_map/ppermute | solution.py:462
  15.9 2.2 %collective-permute-start.2 = (bf16[3,4,32,640]{3,2,1,0:T(8,128)(2,1)}, bf16[3,4,32,640]{3,2,1,0:T(8,128)(2,1)S(1)}, u32[]{:S(2)}, u32[]{:S(2)}) collective-permute-start(bf16[3,4,32,640]{3,2,1,0:T(8,128)(2,1)} %get-tuple-element.65), channel_id=1, source_target_pairs={{0,24},{8,16},{16,8},{24,0},{1,25},{9,17},{17,9},{25,1},{2,26},{10... | collective-permute-start | bytes 1474568 | tf_op jit(solution)/shard_map/ppermute | solution.py:462
  18.0 7.6 %wave_rows.1.w_ref = bf16[1280,2560]{1,0:T(8,128)(2,1)} custom-call(s32[320]{0:T(512)} %couples_ref), custom_call_target="tpu_custom_call" | custom-call | tf_op jit(solution)/shard_map/wave_rows/pallas_call | solution.py:124
  25.7 5.1 %fourier.2 = (bf16[160,256]{1,0:T(8,128)(2,1)}, bf16[160,256]{1,0:T(8,128)(2,1)}, bf16[160,256]{1,0:T(8,128)(2,1)}, bf16[160,256]{1,0:T(8,128)(2,1)}, bf16[160,2...) custom-call(s32[1]{0:T(128)} %bitcast.place_ref, ...), custom_call_target="tpu_custom_call" | custom-call | tf_op jit(solution)/shard_map/fourier/pallas_call | solution.py:168
  33.6 2.2 %collective-permute-done.7.refs_2_ = bf16[160,256]{1,0:T(8,128)(2,1)S(1)} collective-permute-done((bf16[160,256]{1,0:T(8,128)(2,1)}, bf16[160,256]{1,0:T(8,128)(2,1)S(1)}, u32[]{:S(2)}, u32[]{:S(2)}) %collective-permute-start.7) | collective-permute-done | bytes 81952 | tf_op jit(solution)/shard_map/ppermute | solution.py:462
  35.9 2.6 %collective-permute-start.9 = (bf16[160,256]{1,0:T(8,128)(2,1)}, bf16[160,256]{1,0:T(8,128)(2,1)S(1)}, u32[]{:S(2)}, u32[]{:S(2)}) collective-permute-start(bf16[160,256]{1,0:T(8,128)(2,1)} %get-tuple-element.88), channel_id=1, source_target_pairs={{0,4},{1,5},{2,6},{3,7},{4,0},{5,1},{6,2},{7,3},{8,12},{9,13},{10,... | collective-permute-start | bytes 245768 | tf_op jit(solution)/shard_map/ppermute | solution.py:462
  38.5 5.3 %collective-permute-done.1 = bf16[3,4,32,640]{3,2,1,0:T(8,128)(2,1)S(1)} collective-permute-done((bf16[3,4,32,640]{3,2,1,0:T(8,128)(2,1)}, bf16[3,4,32,640]{3,2,1,0:T(8,128)(2,1)S(1)}, u32[]{:S(2)}, u32[]{:S(2)}) %collective-permute-start.1) | collective-permute-done | bytes 491552 | tf_op jit(solution)/shard_map/ppermute | solution.py:462
  43.8 3.6 %collective-permute-start.11 = (bf16[160,256]{1,0:T(8,128)(2,1)}, bf16[160,256]{1,0:T(8,128)(2,1)S(1)}, u32[]{:S(2)}, u32[]{:S(2)}) collective-permute-start(bf16[160,256]{1,0:T(8,128)(2,1)} %get-tuple-element.90), channel_id=1, source_target_pairs={{0,6},{1,7},{2,4},{3,5},{4,2},{5,3},{6,0},{7,1},{8,14},{9,15},{10,... | collective-permute-start | bytes 245768 | tf_op jit(solution)/shard_map/ppermute | solution.py:462
  50.1 7.0 %fourier.3 = (bf16[160,384]{1,0:T(8,128)(2,1)}, bf16[160,384]{1,0:T(8,128)(2,1)}, bf16[160,384]{1,0:T(8,128)(2,1)}, bf16[160,384]{1,0:T(8,128)(2,1)}, bf16[96,38...) custom-call(s32[1]{0:T(128)} %bitcast.place_ref, ...), custom_call_target="tpu_custom_call" | custom-call | tf_op jit(solution)/shard_map/fourier/pallas_call | solution.py:168
  57.3 2.6 %collective-permute-start.24 = (bf16[96,384]{1,0:T(8,128)(2,1)}, bf16[96,384]{1,0:T(8,128)(2,1)S(1)}, u32[]{:S(2)}, u32[]{:S(2)}) collective-permute-start(bf16[96,384]{1,0:T(8,128)(2,1)} %get-tuple-element.108), channel_id=1, source_target_pairs={{0,5},{1,4},{2,7},{3,6},{4,1},{5,0},{6,3},{7,2},{8,13},{9,12},{10,... | collective-permute-start | bytes 221192 | tf_op jit(solution)/shard_map/ppermute | solution.py:462
  61.7 3.5 %collective-permute-done.23.refs_12_ = bf16[96,384]{1,0:T(8,128)(2,1)S(1)} collective-permute-done((bf16[96,384]{1,0:T(8,128)(2,1)}, bf16[96,384]{1,0:T(8,128)(2,1)S(1)}, u32[]{:S(2)}, u32[]{:S(2)}) %collective-permute-start.23) | collective-permute-done | bytes 73760 | tf_op jit(solution)/shard_map/ppermute | solution.py:462
  65.3 1.7 %collective-permute-done.24.refs_13_ = bf16[96,384]{1,0:T(8,128)(2,1)S(1)} collective-permute-done((bf16[96,384]{1,0:T(8,128)(2,1)}, bf16[96,384]{1,0:T(8,128)(2,1)S(1)}, u32[]{:S(2)}, u32[]{:S(2)}) %collective-permute-start.24) | collective-permute-done | bytes 73760 | tf_op jit(solution)/shard_map/ppermute | solution.py:462
  68.2 5.1 %collective-permute-done.25.refs_14_ = bf16[96,384]{1,0:T(8,128)(2,1)S(1)} collective-permute-done((bf16[96,384]{1,0:T(8,128)(2,1)}, bf16[96,384]{1,0:T(8,128)(2,1)S(1)}, u32[]{:S(2)}, u32[]{:S(2)}) %collective-permute-start.25) | collective-permute-done | bytes 73760 | tf_op jit(solution)/shard_map/ppermute | solution.py:462
  73.7 12.5 %forward.3.refs_0_ = bf16[3,8,5248]{2,1,0:T(8,128)(2,1)} custom-call(s32[40]{0:T(128)} %dynamic_slice.3.pairs_ref, s32[1]{0:T(128)} %bitcast.1.here_ref, bf16[160,256]{1,0:T(8,128)(2,1)} %get-tuple-element.84.refs_0_, bf16[160,256]{1,0:T(8,128)(2,1)S(1)} %collective-permute-done.6.refs_1_, bf16[160,256]{1,0:T(8,128)(2,1)S(1)} %collective-permute-done.7.refs_2_, ...), custom_call_target="tpu_custom_call" | custom-call | tf_op jit(solution)/shard_map/forward/pallas_call | solution.py:298
  87.9 1.9 %collective-permute-start.17 = (bf16[64,384]{1,0:T(8,128)(2,1)S(1)}, bf16[64,384]{1,0:T(8,128)(2,1)S(1)}, u32[]{:S(2)}, u32[]{:S(2)}) collective-permute-start(bf16[64,384]{1,0:T(8,128)(2,1)S(1)} %copy-done.4), channel_id=1, source_target_pairs={{0,5},{1,4},{2,7},{3,6},{4,1},{5,0},{6,3},{7,2},{8,13},{9,12},{10,... | collective-permute-start | bytes 147464 | tf_op jit(solution)/shard_map/ppermute | solution.py:462
  93.2 1.8 %collective-permute-start.18 = (bf16[64,384]{1,0:T(8,128)(2,1)S(1)}, bf16[64,384]{1,0:T(8,128)(2,1)S(1)}, u32[]{:S(2)}, u32[]{:S(2)}) collective-permute-start(bf16[64,384]{1,0:T(8,128)(2,1)S(1)} %copy-done.3), channel_id=1, source_target_pairs={{0,6},{1,7},{2,4},{3,5},{4,2},{5,3},{6,0},{7,1},{8,14},{9,15},{10,... | collective-permute-start | bytes 147464 | tf_op jit(solution)/shard_map/ppermute | solution.py:462
  96.2 2.9 %collective-permute-done.18.refs_14_ = bf16[64,384]{1,0:T(8,128)(2,1)S(1)} collective-permute-done((bf16[64,384]{1,0:T(8,128)(2,1)S(1)}, bf16[64,384]{1,0:T(8,128)(2,1)S(1)}, u32[]{:S(2)}, u32[]{:S(2)}) %collective-permute-start.18) | collective-permute-done | bytes 49184 | tf_op jit(solution)/shard_map/ppermute | solution.py:462
  100.6 9.5 %forward.2.refs_0_ = bf16[2,8,5248]{2,1,0:T(8,128)(2,1)} custom-call(s32[40]{0:T(128)} %dynamic_slice.3.pairs_ref, s32[1]{0:T(128)} %bitcast.1.here_ref, bf16[160,256]{1,0:T(8,128)(2,1)} %get-tuple-element.84.refs_0_, bf16[160,256]{1,0:T(8,128)(2,1)S(1)} %collective-permute-done.6.refs_1_, bf16[160,256]{1,0:T(8,128)(2,1)S(1)} %collective-permute-done.7.refs_2_, ...), custom_call_target="tpu_custom_call" | custom-call | tf_op jit(solution)/shard_map/forward/pallas_call | solution.py:298
  110.1 2.8 %collective-permute-start.20 = (bf16[2,8,5248]{2,1,0:T(8,128)(2,1)}, bf16[2,8,5248]{2,1,0:T(8,128)(2,1)S(1)}, u32[]{:S(2)}, u32[]{:S(2)}) collective-permute-start(bf16[2,8,5248]{2,1,0:T(8,128)(2,1)} %forward.2.refs_0_), channel_id=1, source_target_pairs={{0,8},{8,0},{16,24},{24,16},{1,9},{9,1},{17,25},{25,17},{2,10},{10... | collective-permute-start | bytes 503816 | tf_op jit(solution)/shard_map/ppermute | solution.py:462
  114.4 11.4 %inverse.2.refs_8_ = f32[2,2,40,2,2,1280]{5,4,3,2,1,0:T(2,128)} custom-call(s32[40]{0:T(128)} %dynamic_slice.3.pairs_ref, s32[1]{0:T(128)} %bitcast.place_ref, bf16[3,8,5248]{2,1,0:T(8,128)(2,1)} %forward.3.refs_0_, bf16[3,8,5248]{2,1,0:T(8,128)(2,1)S(1)} %collective-permute-done.27.refs_1_, bf16[3,8,5248]{2,1,0:T(8,128)(2,1)S(1)} %collective-permute-done.28.refs_2_, ...), custom_call_target="tpu_custom_call" | custom-call | tf_op jit(solution)/shard_map/inverse/pallas_call | solution.py:426
  125.8 8.2 %inverse.3 = f32[2,2,40,2,2,1280]{5,4,3,2,1,0:T(2,128)} custom-call(s32[40]{0:T(128)} %dynamic_slice.3.pairs_ref, s32[1]{0:T(128)} %bitcast.place_ref, bf16[2,8,5248]{2,1,0:T(8,128)(2,1)} %forward.2.refs_0_, bf16[2,8,5248]{2,1,0:T(8,128)(2,1)S(1)} %collective-permute-done.20.refs_1_, ...), custom_call_target="tpu_custom_call", output_to_operand_aliasing={{}: (10, {})} | custom-call | tf_op jit(solution)/shard_map/inverse/pallas_call | solution.py:426
  (64 shorter events, 21.5 us)
Async XLA Ops:
  3.3 12.5 %collective-permute-start.3 = (bf16[2,4,32,640]{3,2,1,0:T(8,128)(2,1)}, bf16[2,4,32,640]{3,2,1,0:T(8,128)(2,1)S(1)}, u32[]{:S(2)}, u32[]{:S(2)}) collective-permute-start(bf16[2,4,32,640]{3,2,1,0:T(8,128)(2,1)} %get-tuple-element.68), channel_id=1, source_target_pairs={{0,8},{8,0},{16,24},{24,16},{1,9},{9,1},{17,25},{25,17},{2,10},{10... | collective-permute-start | bytes 983048 | tf_op jit(solution)/shard_map/ppermute | solution.py:462
  6.3 19.3 %collective-permute-start.4 = (bf16[2,4,32,640]{3,2,1,0:T(8,128)(2,1)}, bf16[2,4,32,640]{3,2,1,0:T(8,128)(2,1)S(1)}, u32[]{:S(2)}, u32[]{:S(2)}) collective-permute-start(bf16[2,4,32,640]{3,2,1,0:T(8,128)(2,1)} %get-tuple-element.69), channel_id=1, source_target_pairs={{0,16},{8,24},{16,0},{24,8},{1,17},{9,25},{17,1},{25,9},{2,18},{10... | collective-permute-start | bytes 983048 | tf_op jit(solution)/shard_map/ppermute | solution.py:462
  7.8 17.8 %collective-permute-start.5 = (bf16[2,4,32,640]{3,2,1,0:T(8,128)(2,1)}, bf16[2,4,32,640]{3,2,1,0:T(8,128)(2,1)S(1)}, u32[]{:S(2)}, u32[]{:S(2)}) collective-permute-start(bf16[2,4,32,640]{3,2,1,0:T(8,128)(2,1)} %get-tuple-element.70), channel_id=1, source_target_pairs={{0,24},{8,16},{16,8},{24,0},{1,25},{9,17},{17,9},{25,1},{2,26},{10... | collective-permute-start | bytes 983048 | tf_op jit(solution)/shard_map/ppermute | solution.py:462
  12.4 26.1 %collective-permute-start = (bf16[3,4,32,640]{3,2,1,0:T(8,128)(2,1)}, bf16[3,4,32,640]{3,2,1,0:T(8,128)(2,1)S(1)}, u32[]{:S(2)}, u32[]{:S(2)}) collective-permute-start(bf16[3,4,32,640]{3,2,1,0:T(8,128)(2,1)} %get-tuple-element.63), channel_id=1, source_target_pairs={{0,8},{8,0},{16,24},{24,16},{1,9},{9,1},{17,25},{25,17},{2,10},{10... | collective-permute-start | bytes 1474568 | tf_op jit(solution)/shard_map/ppermute | solution.py:462
  14.3 29.4 %collective-permute-start.1 = (bf16[3,4,32,640]{3,2,1,0:T(8,128)(2,1)}, bf16[3,4,32,640]{3,2,1,0:T(8,128)(2,1)S(1)}, u32[]{:S(2)}, u32[]{:S(2)}) collective-permute-start(bf16[3,4,32,640]{3,2,1,0:T(8,128)(2,1)} %get-tuple-element.64), channel_id=1, source_target_pairs={{0,16},{8,24},{16,0},{24,8},{1,17},{9,25},{17,1},{25,9},{2,18},{10... | collective-permute-start | bytes 1474568 | tf_op jit(solution)/shard_map/ppermute | solution.py:462
  15.9 31.5 %collective-permute-start.2 = (bf16[3,4,32,640]{3,2,1,0:T(8,128)(2,1)}, bf16[3,4,32,640]{3,2,1,0:T(8,128)(2,1)S(1)}, u32[]{:S(2)}, u32[]{:S(2)}) collective-permute-start(bf16[3,4,32,640]{3,2,1,0:T(8,128)(2,1)} %get-tuple-element.65), channel_id=1, source_target_pairs={{0,24},{8,16},{16,8},{24,0},{1,25},{9,17},{17,9},{25,1},{2,26},{10... | collective-permute-start | bytes 1474568 | tf_op jit(solution)/shard_map/ppermute | solution.py:462
  33.4 23.8 %collective-permute-start.8 = (bf16[160,256]{1,0:T(8,128)(2,1)}, bf16[160,256]{1,0:T(8,128)(2,1)S(1)}, u32[]{:S(2)}, u32[]{:S(2)}) collective-permute-start(bf16[160,256]{1,0:T(8,128)(2,1)} %get-tuple-element.87), channel_id=1, source_target_pairs={{0,3},{1,2},{2,1},{3,0},{4,7},{5,6},{6,5},{7,4},{8,11},{9,10},{10,... | collective-permute-start | bytes 245768 | tf_op jit(solution)/shard_map/ppermute | solution.py:462
  35.9 21.4 %collective-permute-start.9 = (bf16[160,256]{1,0:T(8,128)(2,1)}, bf16[160,256]{1,0:T(8,128)(2,1)S(1)}, u32[]{:S(2)}, u32[]{:S(2)}) collective-permute-start(bf16[160,256]{1,0:T(8,128)(2,1)} %get-tuple-element.88), channel_id=1, source_target_pairs={{0,4},{1,5},{2,6},{3,7},{4,0},{5,1},{6,2},{7,3},{8,12},{9,13},{10,... | collective-permute-start | bytes 245768 | tf_op jit(solution)/shard_map/ppermute | solution.py:462
  38.5 21.4 %collective-permute-start.10 = (bf16[160,256]{1,0:T(8,128)(2,1)}, bf16[160,256]{1,0:T(8,128)(2,1)S(1)}, u32[]{:S(2)}, u32[]{:S(2)}) collective-permute-start(bf16[160,256]{1,0:T(8,128)(2,1)} %get-tuple-element.89), channel_id=1, source_target_pairs={{0,5},{1,4},{2,7},{3,6},{4,1},{5,0},{6,3},{7,2},{8,13},{9,12},{10,... | collective-permute-start | bytes 245768 | tf_op jit(solution)/shard_map/ppermute | solution.py:462
  43.8 16.5 %collective-permute-start.11 = (bf16[160,256]{1,0:T(8,128)(2,1)}, bf16[160,256]{1,0:T(8,128)(2,1)S(1)}, u32[]{:S(2)}, u32[]{:S(2)}) collective-permute-start(bf16[160,256]{1,0:T(8,128)(2,1)} %get-tuple-element.90), channel_id=1, source_target_pairs={{0,6},{1,7},{2,4},{3,5},{4,2},{5,3},{6,0},{7,1},{8,14},{9,15},{10,... | collective-permute-start | bytes 245768 | tf_op jit(solution)/shard_map/ppermute | solution.py:462
  47.4 14.2 %collective-permute-start.12 = (bf16[160,256]{1,0:T(8,128)(2,1)}, bf16[160,256]{1,0:T(8,128)(2,1)S(1)}, u32[]{:S(2)}, u32[]{:S(2)}) collective-permute-start(bf16[160,256]{1,0:T(8,128)(2,1)} %get-tuple-element.91), channel_id=1, source_target_pairs={{0,7},{1,6},{2,5},{3,4},{4,3},{5,2},{6,1},{7,0},{8,15},{9,14},{10,... | collective-permute-start | bytes 245768 | tf_op jit(solution)/shard_map/ppermute | solution.py:462
  57.2 8.0 %collective-permute-start.23 = (bf16[96,384]{1,0:T(8,128)(2,1)}, bf16[96,384]{1,0:T(8,128)(2,1)S(1)}, u32[]{:S(2)}, u32[]{:S(2)}) collective-permute-start(bf16[96,384]{1,0:T(8,128)(2,1)} %get-tuple-element.107), channel_id=1, source_target_pairs={{0,4},{1,5},{2,6},{3,7},{4,0},{5,1},{6,2},{7,3},{8,12},{9,13},{10,... | collective-permute-start | bytes 221192 | tf_op jit(solution)/shard_map/ppermute | solution.py:462
  57.3 9.8 %collective-permute-start.24 = (bf16[96,384]{1,0:T(8,128)(2,1)}, bf16[96,384]{1,0:T(8,128)(2,1)S(1)}, u32[]{:S(2)}, u32[]{:S(2)}) collective-permute-start(bf16[96,384]{1,0:T(8,128)(2,1)} %get-tuple-element.108), channel_id=1, source_target_pairs={{0,5},{1,4},{2,7},{3,6},{4,1},{5,0},{6,3},{7,2},{8,13},{9,12},{10,... | collective-permute-start | bytes 221192 | tf_op jit(solution)/shard_map/ppermute | solution.py:462
  59.8 13.8 %collective-permute-start.13 = (bf16[160,384]{1,0:T(8,128)(2,1)}, bf16[160,384]{1,0:T(8,128)(2,1)S(1)}, u32[]{:S(2)}, u32[]{:S(2)}) collective-permute-start(bf16[160,384]{1,0:T(8,128)(2,1)} %get-tuple-element.97), channel_id=1, source_target_pairs={{0,1},{1,0},{2,3},{3,2},{4,5},{5,4},{6,7},{7,6},{8,9},{9,8},{10,11... | collective-permute-start | bytes 368648 | tf_op jit(solution)/shard_map/ppermute | solution.py:462
  60.3 13.3 %collective-permute-start.14 = (bf16[160,384]{1,0:T(8,128)(2,1)}, bf16[160,384]{1,0:T(8,128)(2,1)S(1)}, u32[]{:S(2)}, u32[]{:S(2)}) collective-permute-start(bf16[160,384]{1,0:T(8,128)(2,1)} %get-tuple-element.98), channel_id=1, source_target_pairs={{0,2},{1,3},{2,0},{3,1},{4,6},{5,7},{6,4},{7,5},{8,10},{9,11},{10,... | collective-permute-start | bytes 368648 | tf_op jit(solution)/shard_map/ppermute | solution.py:462
  61.5 12.1 %collective-permute-start.15 = (bf16[160,384]{1,0:T(8,128)(2,1)}, bf16[160,384]{1,0:T(8,128)(2,1)S(1)}, u32[]{:S(2)}, u32[]{:S(2)}) collective-permute-start(bf16[160,384]{1,0:T(8,128)(2,1)} %get-tuple-element.99), channel_id=1, source_target_pairs={{0,3},{1,2},{2,1},{3,0},{4,7},{5,6},{6,5},{7,4},{8,11},{9,10},{10,... | collective-permute-start | bytes 368648 | tf_op jit(solution)/shard_map/ppermute | solution.py:462
  65.2 8.1 %collective-permute-start.25 = (bf16[96,384]{1,0:T(8,128)(2,1)}, bf16[96,384]{1,0:T(8,128)(2,1)S(1)}, u32[]{:S(2)}, u32[]{:S(2)}) collective-permute-start(bf16[96,384]{1,0:T(8,128)(2,1)} %get-tuple-element.109), channel_id=1, source_target_pairs={{0,6},{1,7},{2,4},{3,5},{4,2},{5,3},{6,0},{7,1},{8,14},{9,15},{10,... | collective-permute-start | bytes 221192 | tf_op jit(solution)/shard_map/ppermute | solution.py:462
  86.2 28.1 %collective-permute-start.27 = (bf16[3,8,5248]{2,1,0:T(8,128)(2,1)}, bf16[3,8,5248]{2,1,0:T(8,128)(2,1)S(1)}, u32[]{:S(2)}, u32[]{:S(2)}) collective-permute-start(bf16[3,8,5248]{2,1,0:T(8,128)(2,1)} %forward.3.refs_0_), channel_id=1, source_target_pairs={{0,8},{8,0},{16,24},{24,16},{1,9},{9,1},{17,25},{25,17},{2,10},{10... | collective-permute-start | bytes 755720 | tf_op jit(solution)/shard_map/ppermute | solution.py:462
  87.9 7.1 %collective-permute-start.17 = (bf16[64,384]{1,0:T(8,128)(2,1)S(1)}, bf16[64,384]{1,0:T(8,128)(2,1)S(1)}, u32[]{:S(2)}, u32[]{:S(2)}) collective-permute-start(bf16[64,384]{1,0:T(8,128)(2,1)S(1)} %copy-done.4), channel_id=1, source_target_pairs={{0,5},{1,4},{2,7},{3,6},{4,1},{5,0},{6,3},{7,2},{8,13},{9,12},{10,... | collective-permute-start | bytes 147464 | tf_op jit(solution)/shard_map/ppermute | solution.py:462
  89.8 24.5 %collective-permute-start.28 = (bf16[3,8,5248]{2,1,0:T(8,128)(2,1)}, bf16[3,8,5248]{2,1,0:T(8,128)(2,1)S(1)}, u32[]{:S(2)}, u32[]{:S(2)}) collective-permute-start(bf16[3,8,5248]{2,1,0:T(8,128)(2,1)} %forward.3.refs_0_), channel_id=1, source_target_pairs={{0,16},{8,24},{16,0},{24,8},{1,17},{9,25},{17,1},{25,9},{2,18},{10... | collective-permute-start | bytes 755720 | tf_op jit(solution)/shard_map/ppermute | solution.py:462
  90.7 23.7 %collective-permute-start.29 = (bf16[3,8,5248]{2,1,0:T(8,128)(2,1)}, bf16[3,8,5248]{2,1,0:T(8,128)(2,1)S(1)}, u32[]{:S(2)}, u32[]{:S(2)}) collective-permute-start(bf16[3,8,5248]{2,1,0:T(8,128)(2,1)} %forward.3.refs_0_), channel_id=1, source_target_pairs={{0,24},{8,16},{16,8},{24,0},{1,25},{9,17},{17,9},{25,1},{2,26},{10... | collective-permute-start | bytes 755720 | tf_op jit(solution)/shard_map/ppermute | solution.py:462
  110.1 15.8 %collective-permute-start.20 = (bf16[2,8,5248]{2,1,0:T(8,128)(2,1)}, bf16[2,8,5248]{2,1,0:T(8,128)(2,1)S(1)}, u32[]{:S(2)}, u32[]{:S(2)}) collective-permute-start(bf16[2,8,5248]{2,1,0:T(8,128)(2,1)} %forward.2.refs_0_), channel_id=1, source_target_pairs={{0,8},{8,0},{16,24},{24,16},{1,9},{9,1},{17,25},{25,17},{2,10},{10... | collective-permute-start | bytes 503816 | tf_op jit(solution)/shard_map/ppermute | solution.py:462
  112.8 13.0 %collective-permute-start.21 = (bf16[2,8,5248]{2,1,0:T(8,128)(2,1)}, bf16[2,8,5248]{2,1,0:T(8,128)(2,1)S(1)}, u32[]{:S(2)}, u32[]{:S(2)}) collective-permute-start(bf16[2,8,5248]{2,1,0:T(8,128)(2,1)} %forward.2.refs_0_), channel_id=1, source_target_pairs={{0,16},{8,24},{16,0},{24,8},{1,17},{9,25},{17,1},{25,9},{2,18},{10... | collective-permute-start | bytes 503816 | tf_op jit(solution)/shard_map/ppermute | solution.py:462
  114.4 11.5 %collective-permute-start.22 = (bf16[2,8,5248]{2,1,0:T(8,128)(2,1)}, bf16[2,8,5248]{2,1,0:T(8,128)(2,1)S(1)}, u32[]{:S(2)}, u32[]{:S(2)}) collective-permute-start(bf16[2,8,5248]{2,1,0:T(8,128)(2,1)} %forward.2.refs_0_), channel_id=1, source_target_pairs={{0,24},{8,16},{16,8},{24,0},{1,25},{9,17},{17,9},{25,1},{2,26},{10... | collective-permute-start | bytes 503816 | tf_op jit(solution)/shard_map/ppermute | solution.py:462
  (13 other events, 177.2 us)
